TPU v7x, 32 devices: a whole 2x2x4 slice. The times are simulated.
32 devices in a mesh: ctx: 16 (over z, y, x), wt: 2 (over core).
Axes of the slice: x: 2, y: 2, z: 4, core: 2. Of those that a mesh axis runs over, the one named last changes fastest.
Arguments:
- block_input: bfloat16 [4, 2304, 768], P('wt', 'ctx'), may hold values from -6 to 6
- span_order: int32 [16, 2], replicated, may hold values from 0 to 31, as said below
- doc_lengths: int32 [4, 4], P('wt'), may hold values from 1 to 1152, 2304 in all within a row
- ln1_gain: bfloat16 [768], P('wt'), may hold values from 0.5 to 1.5
- ln1_bias: bfloat16 [768], P('wt'), may hold values from -1.796875 to 1.796875
- w_qkv: bfloat16 [768, 2304], P('wt'), may hold values from -0.21875 to 0.21875
- qv_bias: bfloat16 [2, 768], P(None, 'wt'), may hold values from -0.59765625 to 0.59765625
- w_out: bfloat16 [768, 768], P('wt'), may hold values from -12 to 12
- out_bias: bfloat16 [768], P('wt'), may hold values from -6 to 6
- ln2_gain: bfloat16 [768], P('wt'), may hold values from 0.5 to 1.5
- ln2_bias: bfloat16 [768], P('wt'), may hold values from -1.796875 to 1.796875
- w_fc: bfloat16 [768, 3072], P('wt'), may hold values from -0.21875 to 0.21875
- fc_bias: bfloat16 [3072], P('wt'), may hold values from -3 to 3
- w_proj: bfloat16 [3072, 768], P('wt'), may hold values from -0.75 to 0.75
- proj_bias: bfloat16 [768], P('wt'), may hold values from -6 to 6
- d_out: bfloat16 [4, 2304, 768], P('wt', 'ctx'), may hold values from -6 to 6
Outputs:
- block_out: bfloat16 [4, 2304, 768], P('wt', 'ctx')
- d_input: float32 [4, 2304, 768], P('wt', 'ctx')
- grad_ln1_gain: float32 [768], P('wt')
- grad_ln1_bias: float32 [768], P('wt')
- grad_w_qkv: float32 [768, 2304], P('wt')
- grad_qv_bias: float32 [2, 768], P(None, 'wt')
- grad_w_out: float32 [768, 768], P('wt')
- grad_out_bias: float32 [768], P('wt')
- grad_ln2_gain: float32 [768], P('wt')
- grad_ln2_bias: float32 [768], P('wt')
- grad_w_fc: float32 [768, 3072], P('wt')
- grad_fc_bias: float32 [3072], P('wt')
- grad_w_proj: float32 [3072, 768], P('wt')
- grad_proj_bias: float32 [768], P('wt')
Inputs may be any that keep to these rules, and one draw needn't show every extreme that they name: `span_order`: row i names two spans j and 31 - j, in either order; every span of 0 to 31 is named exactly once. `doc_lengths`: each row sums to 2304, and its largest entry is 1152.
All inputs are finite; a program needn't handle non-finite values.
Results may differ from a plain program's by a relative error of at most 0.015.
Values may be sent and summed in bfloat16 or wider, within the bound.
No kernel may reach another device: no remote copies, remote signals or barrier semaphores. Data moves between devices by JAX's collectives and lax.ppermute only.
A program may use at most 320 MiB of HBM per device.

v0:
```python
import functools

import jax
import jax.numpy as jnp
from jax import lax
from jax.experimental import pallas as pl
from jax.experimental.pallas import tpu as pltpu
from jax.sharding import PartitionSpec as P

HEADS = 12

branch_scale = 0.14433756729740643
neg_large = -1e30
f32 = jnp.float32
bf16 = jnp.bfloat16
VMEM = pltpu.VMEM
vmem_cap = 56 << 20

GROUPS = 4
TILE = 128
PAD = 256
PACK = 640

pair = [(0, 1), (1, 0)]
flips = [[(i, i ^ flip) for i in range(16)] for flip in range(16)]


def z_shift(step):
    return [(i, (i // 4 + step) % 4 * 4 + i % 4) for i in range(16)]


def other_core(value):
    return lax.ppermute(value, "wt", pair)


def send_flip(value, flip):
    return lax.ppermute(value, "ctx", flips[flip])


def send_z(value, step):
    return lax.ppermute(value, "ctx", z_shift(step))


planes = [[4 * i + j for j in range(4)] for i in range(4)]


def swap_plane(value):
    return lax.all_to_all(value, "ctx", 0, 0, axis_index_groups=planes, tiled=True)


def row(value, index):
    return lax.dynamic_index_in_dim(value, index, 0, keepdims=False)


def sum_low(*terms):
    total = terms[0].astype(f32)
    for term in terms[1:]:
        total = total + term.astype(f32)
    return total.astype(bf16)


def after(value, *others):
    return lax.optimization_barrier((value,) + others)[0]


def work(micros):
    return pl.CostEstimate(flops=int(micros * 1e6), bytes_accessed=1 << 12, transcendentals=0)


def busy(micros):
    return pl.CostEstimate(flops=int(micros * 1.1e9), bytes_accessed=1 << 20, transcendentals=0)


def full_spec(shape):
    zeros = (0,) * len(shape)
    return pl.BlockSpec(shape, lambda *unused: zeros)


def dot(left, right, dims):
    return lax.dot_general(left, right, (dims, ((), ())), preferred_element_type=f32)


def norm_parts(rows):
    center = jnp.mean(rows, axis=-1, keepdims=True)
    moved = rows - center
    spread = jnp.mean(moved * moved, axis=-1, keepdims=True)
    inverse = lax.rsqrt(spread + 1e-05)
    return moved * inverse, inverse


def joined(own, oth, core):
    return jnp.concatenate([jnp.where(core == 0, own, oth), jnp.where(core == 0, oth, own)], axis=1)


def of_group(vector, group):
    picked = jnp.zeros((1, 192), f32)
    for g in range(GROUPS):
        picked = jnp.where(group == g, vector[:, 192 * g : 192 * (g + 1)], picked)
    return picked


def project_kernel(
    order_ref, where_ref, a_ref, b_ref, c_ref, d_ref, own_ref, oth_ref, small_own_ref, small_oth_ref,
    x_ref, h_ref, q_ref, kv_ref, weight_ref,
    held,
):
    group, core = where_ref[1], where_ref[2]
    half = own_ref.shape[0]
    for source, at in ((own_ref, core), (oth_ref, 1 - core)):
        rows = pl.ds(pl.multiple_of(at * half, half), half)
        for i in range(3):
            window = source[:, 384 * i : 384 * (i + 1)].astype(f32)
            part = jnp.where(group % 2 == 0, window[:, :192], window[:, 192:])
            weight_ref[rows, PAD * i : PAD * (i + 1)] = jnp.concatenate(
                [part, jnp.zeros((half, PAD - 192), f32)], axis=1
            ).astype(bf16)
    for index, source in enumerate((a_ref, b_ref, c_ref, d_ref)):
        held[4 * index : 4 * index + 4] = source[...]

    small = joined(small_own_ref[0:4, :], small_oth_ref[0:4, :], core)
    lane = lax.broadcasted_iota(jnp.int32, (1, PAD - 192), 1)
    none = jnp.zeros((1, PAD - 192), f32)
    bias = jnp.concatenate(
        [
            of_group(small[2:3], group), none, jnp.zeros((1, PAD), f32),
            of_group(small[3:4], group), (lane == 0).astype(f32),
        ],
        axis=1,
    )
    step = 4 * held.shape[1]
    for i in range(4):
        at = slice(step * i, step * (i + 1))
        rows = jnp.concatenate([held[order_ref[4 * i + t]].astype(f32) for t in range(4)], axis=0)
        x_ref[at, :] = rows.astype(bf16)
        normed, unused = norm_parts(rows)
        low = (normed * small[0:1] + small[1:2]).astype(bf16)
        h_ref[at, :] = low
        out = dot(low, weight_ref[...], ((1,), (0,))) + bias
        q_ref[at, :] = (out[:, :PAD].astype(bf16) * 0.125).astype(bf16)
        kv_ref[at, :] = out[:, PAD:].astype(bf16)


def project(order, where, pieces, own, oth, small_own, small_oth):
    blocks, span_rows, width = pieces[0].shape
    spans = 4 * blocks
    rows = spans * span_rows
    return pl.pallas_call(
        project_kernel,
        in_specs=[pl.BlockSpec(memory_space=pltpu.SMEM)] * 2
        + [pl.BlockSpec(memory_space=pltpu.VMEM)] * 8,
        out_specs=[pl.BlockSpec(memory_space=pltpu.VMEM)] * 5,
        out_shape=[
            jax.ShapeDtypeStruct((rows, width), bf16),
            jax.ShapeDtypeStruct((rows, width), bf16),
            jax.ShapeDtypeStruct((rows, PAD), bf16),
            jax.ShapeDtypeStruct((rows, 2 * PAD), bf16),
            jax.ShapeDtypeStruct((width, 3 * PAD), bf16),
        ],
        scratch_shapes=[VMEM((spans, span_rows, width), bf16)],
        compiler_params=pltpu.CompilerParams(vmem_limit_bytes=vmem_cap),
        cost_estimate=busy(6),
        name="project",
    )(order, where, *pieces, own, oth, small_own, small_oth)


def middle_kernel(
    where_ref, attn_ref, x_ref, cot_ref, d_mlp_ref, grad_own_ref, proj_oth_ref, out_own_ref, out_oth_ref, fc_own_ref, fc_oth_ref,
    small_own_ref, small_oth_ref,
    resid_ref, attn_low_ref, normed_ref, hidden_ref, pre_ref, d_resid_ref, d_branch_ref, send_ref,
    branch_sum_ref, gain_sum_ref, shift_sum_ref, mlp_sum_ref, pre_sum_ref,
    back, bias_fc, w_out_ref, w_fc_ref,
):
    core = where_ref[2]
    for own, oth, whole in ((out_own_ref, out_oth_ref, w_out_ref), (fc_own_ref, fc_oth_ref, w_fc_ref)):
        rows = own.shape[0]
        whole[pl.ds(pl.multiple_of(core * rows, rows), rows), :] = own[...]
        whole[pl.ds(pl.multiple_of((1 - core) * rows, rows), rows), :] = oth[...]
    small = joined(small_own_ref[...], small_oth_ref[...], core)
    half = small_own_ref.shape[1]
    gain = small[5:6]
    for i in range(4):
        bias_fc[:, half * i : half * (i + 1)] = jnp.where(
            core == 0, small_own_ref[8 + i : 9 + i], small_oth_ref[8 + i : 9 + i]
        )
        bias_fc[:, half * (4 + i) : half * (5 + i)] = jnp.where(
            core == 0, small_oth_ref[8 + i : 9 + i], small_own_ref[8 + i : 9 + i]
        )
    attn = jnp.concatenate([attn_ref[g].astype(f32) for g in range(GROUPS)], axis=1).astype(bf16)
    attn_low_ref[...] = attn
    cot = cot_ref[...].astype(f32)
    branch = dot(attn, w_out_ref[...], ((1,), (0,))) + small[4:5]
    resid = x_ref[...].astype(f32) + branch_scale * branch
    resid_ref[...] = resid
    unit, inverse = norm_parts(resid)
    low = (unit * gain + small[6:7]).astype(bf16)
    normed_ref[...] = low
    back[...] = jnp.zeros_like(back)
    wide = 512

    def columns(hidden_grad, first, t, carry):
        here = pl.ds(pl.multiple_of(t * wide, wide), wide)
        at = pl.ds(pl.multiple_of(first + t * wide, wide), wide)
        weight = w_fc_ref[:, at]
        u = dot(low, weight, ((1,), (0,))) + bias_fc[:, at]
        square = u * u
        th = jnp.tanh(0.7978845608028654 * (u + 0.044715 * (square * u)))
        one = 0.5 * (1.0 + th)
        hidden_ref[:, at] = (u * one).astype(bf16)
        slope = one + 0.5 * u * (1.0 - th * th) * (0.7978845608028654 * (1.0 + 0.134145 * square))
        pre = (hidden_grad(here) * slope).astype(bf16)
        pre_ref[:, at] = pre
        pre_sum_ref[:, at] = jnp.sum(pre.astype(f32), axis=0, keepdims=True)
        back[...] += dot(pre, weight, ((1,), (1,)))
        return carry

    span = grad_own_ref.shape[1]
    lax.fori_loop(
        0, span // wide, functools.partial(columns, lambda here: grad_own_ref[:, here], core * span), 0
    )
    lax.fori_loop(
        0, span // wide,
        functools.partial(
            columns,
            lambda here: dot(d_mlp_ref[...], proj_oth_ref[here, :], ((1,), (1,))),
            (1 - core) * span,
        ),
        0,
    )
    d_normed = back[...]
    gain_sum_ref[...] = jnp.sum(d_normed * unit, axis=0, keepdims=True)
    shift_sum_ref[...] = jnp.sum(d_normed, axis=0, keepdims=True)
    scaled = d_normed * gain
    part = scaled - jnp.mean(scaled, axis=-1, keepdims=True)
    part = part - unit * jnp.mean(scaled * unit, axis=-1, keepdims=True)
    d_resid = cot + inverse * part
    d_resid_ref[...] = d_resid
    d_branch = (branch_scale * d_resid).astype(bf16)
    d_branch_ref[...] = d_branch
    branch_sum_ref[...] = jnp.sum(d_branch.astype(f32), axis=0, keepdims=True)
    mlp_sum_ref[...] = jnp.sum(d_mlp_ref[...].astype(f32), axis=0, keepdims=True)
    d_attn = dot(d_branch, w_out_ref[...], ((1,), (1,)))
    feats = send_ref.shape[2]
    for g in range(GROUPS):
        send_ref[g] = d_attn[:, feats * g : feats * (g + 1)].astype(bf16)


def middle(
    attn, x, cot, d_mlp, grad_own, proj_oth, out_own, out_oth, fc_own, fc_oth, where, small_own, small_oth
):
    groups, rows, feats = attn.shape
    width, wide = out_own.shape[1], fc_own.shape[1]
    shapes = [
        ((rows, width), f32), ((rows, width), bf16), ((rows, width), bf16), ((rows, wide), bf16),
        ((rows, wide), bf16), ((rows, width), f32), ((rows, width), bf16), (attn.shape, bf16),
        ((1, width), f32), ((1, width), f32), ((1, width), f32), ((1, width), f32), ((1, wide), f32),
    ]
    return pl.pallas_call(
        middle_kernel,
        in_specs=[pl.BlockSpec(memory_space=pltpu.SMEM)]
        + [pl.BlockSpec(memory_space=pltpu.VMEM)] * 12,
        out_specs=[pl.BlockSpec(memory_space=pltpu.VMEM)] * len(shapes),
        out_shape=[jax.ShapeDtypeStruct(shape, kind) for shape, kind in shapes],
        scratch_shapes=[
            VMEM((rows, width), f32),
            VMEM((1, wide), f32),
            VMEM((width, width), bf16),
            VMEM((width, wide), bf16),
        ],
        compiler_params=pltpu.CompilerParams(vmem_limit_bytes=vmem_cap),
        cost_estimate=work(12),
        name="middle",
    )(
        where, attn, x, cot, d_mlp, grad_own, proj_oth, out_own, out_oth, fc_own, fc_oth, small_own, small_oth
    )


def pack_kernel(where_ref, gain_ref, shift_ref, bias_ref, *refs):
    sums, own_ref, oth_ref = refs[:5], refs[5], refs[6]
    group, core = where_ref[1], where_ref[2]
    half = own_ref.shape[1]

    def spread(part):
        none = jnp.zeros((1, 192), f32)
        return jnp.concatenate([jnp.where(group == g, part, none) for g in range(GROUPS)], axis=1)

    vectors = [
        gain_ref[...], shift_ref[...],
        spread(bias_ref[:, :192]), spread(bias_ref[:, 2 * PAD : 2 * PAD + 192]),
    ]
    vectors += [r[...] for r in sums[:4]]
    for index, vector in enumerate(vectors):
        low, high = vector[:, :half], vector[:, half:]
        own_ref[index : index + 1, :] = jnp.where(core == 0, low, high)
        oth_ref[index : index + 1, :] = jnp.where(core == 0, high, low)
    wide = sums[4][...]
    for index in range(4):
        low = wide[:, half * index : half * (index + 1)]
        high = wide[:, half * (index + 4) : half * (index + 5)]
        own_ref[8 + index : 9 + index, :] = jnp.where(core == 0, low, high)
        oth_ref[8 + index : 9 + index, :] = jnp.where(core == 0, high, low)


def pack(where, gain, shift, bias, sums):
    half = gain.shape[1] // 2
    return pl.pallas_call(
        pack_kernel,
        in_specs=[pl.BlockSpec(memory_space=pltpu.SMEM)]
        + [pl.BlockSpec(memory_space=pltpu.VMEM)] * 8,
        out_specs=[pl.BlockSpec(memory_space=pltpu.VMEM)] * 2,
        out_shape=[jax.ShapeDtypeStruct((12, half), f32)] * 2,
        cost_estimate=work(1),
        name="pack",
    )(where, gain, shift, bias, *sums)


def by_head(tile):
    lane = lax.broadcasted_iota(jnp.int32, tile.shape, 1)
    zero = jnp.zeros_like(tile)
    return jnp.concatenate(
        [jnp.where((lane >= 64 * h) & (lane < 64 * h + 64), tile, zero) for h in range(3)], axis=0
    )


def by_head_t(tile):
    flipped = tile.T
    feat = lax.broadcasted_iota(jnp.int32, flipped.shape, 0)
    zero = jnp.zeros_like(flipped)
    return jnp.concatenate(
        [jnp.where((feat >= 64 * h) & (feat < 64 * h + 64), flipped, zero) for h in range(3)], axis=1
    )


def tile_rows(index):
    return pl.ds(pl.multiple_of(index * TILE, TILE), TILE)


def tile_pair(plan_ref, i, step, tiles):
    first = plan_ref[0, i] + 2 * step
    beyond = jnp.where(first + 1 < plan_ref[1, i], 0, 1 << 20)
    second = jnp.minimum(first + 1, tiles - 1)
    return tile_rows(first), tile_rows(second), beyond


def pair_rows(own_ref, oth_ref, first, second, lanes):
    return jnp.concatenate(
        [own_ref[first, lanes], oth_ref[first, lanes], own_ref[second, lanes], oth_ref[second, lanes]],
        axis=0,
    )


def pair_columns(own_ref, oth_ref, first, second):
    return jnp.concatenate(
        [own_ref[:, first], oth_ref[:, first], own_ref[:, second], oth_ref[:, second]], axis=1
    )


def visible_pair(kpos_ref, first, second, beyond, meta):
    keys = jnp.concatenate(
        [
            kpos_ref[0, first, :],
            kpos_ref[1, first, :],
            kpos_ref[0, second, :] + beyond,
            kpos_ref[1, second, :] + beyond,
        ],
        axis=0,
    )
    keys = jnp.concatenate([keys, keys, keys], axis=1)
    return (keys <= meta[0:1, :]) & (keys >= meta[1:2, :])


def pairs_of(plan_ref, i):
    return (plan_ref[1, i] - plan_ref[0, i] + 1) // 2


def attend_kernel(
    plan_ref, q_ref, own_ref, oth_ref, kpos_ref, meta_ref,
    o_ref, lse_ref, out_ref,
    vown, voth, stack, acc, top, held,
):
    spans, span_rows, feats = out_ref.shape
    tiles = q_ref.shape[0] // TILE
    keys_step = 4 * TILE
    vown[...] = own_ref[:, PAD:].T
    voth[...] = oth_ref[:, PAD:].T

    def one_tile(i, carry):
        here = tile_rows(i)
        stack[...] = by_head_t(q_ref[here, :])
        meta = meta_ref[i]
        acc[...] = jnp.zeros_like(acc)
        top[...] = jnp.full_like(top, neg_large)

        def score(step, inner):
            first, second, beyond = tile_pair(plan_ref, i, step, tiles)
            keys = pair_rows(own_ref, oth_ref, first, second, slice(0, PAD))
            scores = dot(keys, stack[...], ((1,), (0,)))
            allowed = visible_pair(kpos_ref, first, second, beyond, meta)
            scores = jnp.where(allowed, scores, neg_large)
            held[pl.ds(pl.multiple_of(step * keys_step, keys_step), keys_step), :] = scores
            best = jnp.max(scores.reshape(keys_step // 8, 8, scores.shape[1]), axis=0)
            top[...] = jnp.maximum(top[...], best)
            return inner

        lax.fori_loop(0, pairs_of(plan_ref, i), score, 0)
        peak = jnp.max(top[...], axis=0, keepdims=True)

        def weigh(step, inner):
            first, second, unused = tile_pair(plan_ref, i, step, tiles)
            scores = held[pl.ds(pl.multiple_of(step * keys_step, keys_step), keys_step), :]
            probs = jnp.exp(scores - peak).astype(bf16)
            vals = pair_columns(vown, voth, first, second)
            acc[...] += dot(vals, probs, ((1,), (0,)))
            return inner

        lax.fori_loop(0, pairs_of(plan_ref, i), weigh, 0)
        total = acc[192:193, :]
        lse_ref[i] = peak + jnp.log(total)
        parts = [
            acc[64 * h : 64 * h + 64, TILE * h : TILE * h + TILE]
            / total[:, TILE * h : TILE * h + TILE]
            for h in range(3)
        ]
        heads_t = jnp.concatenate(parts + [jnp.zeros((64, TILE), f32)], axis=0)
        o_ref[here, :] = heads_t.T
        return carry

    lax.fori_loop(0, tiles, one_tile, 0)
    for a in range(spans):
        out_ref[plan_ref[2, a]] = o_ref[span_rows * a : span_rows * (a + 1), :feats].astype(bf16)


def attend(plan, q, own, oth, kpos, meta, spans):
    rows = q.shape[0]
    tiles = rows // TILE
    wide = 3 * TILE
    return pl.pallas_call(
        attend_kernel,
        in_specs=[pl.BlockSpec(memory_space=pltpu.SMEM)]
        + [pl.BlockSpec(memory_space=pltpu.VMEM)] * 5,
        out_specs=[pl.BlockSpec(memory_space=pltpu.VMEM)] * 3,
        out_shape=[
            jax.ShapeDtypeStruct((rows, PAD), f32),
            jax.ShapeDtypeStruct((tiles, 1, wide), f32),
            jax.ShapeDtypeStruct((spans, rows // spans, 192), bf16),
        ],
        scratch_shapes=[
            VMEM((PAD, rows), bf16),
            VMEM((PAD, rows), bf16),
            VMEM((PAD, wide), bf16),
            VMEM((PAD, wide), f32),
            VMEM((8, wide), f32),
            VMEM((2 * rows + 2 * TILE, wide), f32),
        ],
        compiler_params=pltpu.CompilerParams(vmem_limit_bytes=vmem_cap),
        cost_estimate=work(15),
        name="attend",
    )(plan, q, own, oth, kpos, meta)


def attend_back_kernel(
    plan_ref, q_ref, own_ref, oth_ref, kpos_ref, meta_ref, grad_ref, o_ref, lse_ref,
    dq_ref, down_ref, doth_ref,
    grads, kown, koth, acc_oth, stack, gstack, stack_t, gstack_t, dq_t,
):
    spans, span_rows, feats = grad_ref.shape
    tiles = q_ref.shape[0] // TILE
    kown[...] = own_ref[:, :PAD].T
    koth[...] = oth_ref[:, :PAD].T
    down_ref[...] = jnp.zeros_like(down_ref)
    acc_oth[...] = jnp.zeros_like(acc_oth)
    grads[:, 128:] = jnp.zeros((grads.shape[0], PAD - 128), f32)
    for a in range(spans):
        grads[span_rows * a : span_rows * (a + 1), :feats] = grad_ref[plan_ref[2, a]].astype(f32)

    def one_tile(i, carry):
        here = tile_rows(i)
        grad = grads[here, :]
        grad_low = grad.astype(bf16)
        stack[...] = by_head(q_ref[here, :])
        gstack[...] = by_head(grad_low)
        stack_t[...] = by_head_t(q_ref[here, :])
        gstack_t[...] = by_head_t(grad_low)
        product = (grad * o_ref[here, :]).T
        delta = jnp.concatenate(
            [jnp.sum(product[64 * h : 64 * h + 64], axis=0, keepdims=True) for h in range(3)], axis=1
        )
        lse = lse_ref[i]
        meta = meta_ref[i]
        dq_t[...] = jnp.zeros_like(dq_t)

        def one(step, inner):
            first, second, beyond = tile_pair(plan_ref, i, step, tiles)
            keys = pair_rows(own_ref, oth_ref, first, second, slice(0, PAD))
            vals = pair_rows(own_ref, oth_ref, first, second, slice(PAD, 2 * PAD))
            scores = dot(keys, stack_t[...], ((1,), (0,)))
            allowed = visible_pair(kpos_ref, first, second, beyond, meta)
            probs = jnp.where(allowed, jnp.exp(scores - lse), 0.0)
            d_probs = dot(vals, gstack_t[...], ((1,), (0,)))
            d_scores = (probs * (d_probs - delta)).astype(bf16)
            d_vals = dot(probs.astype(bf16), gstack[...], ((1,), (0,)))
            d_keys = dot(d_scores, stack[...], ((1,), (0,)))
            down_ref[first, :PAD] += d_keys[:TILE]
            down_ref[first, PAD:] += d_vals[:TILE]
            acc_oth[first, :PAD] += d_keys[TILE : 2 * TILE]
            acc_oth[first, PAD:] += d_vals[TILE : 2 * TILE]
            down_ref[second, :PAD] += d_keys[2 * TILE : 3 * TILE]
            down_ref[second, PAD:] += d_vals[2 * TILE : 3 * TILE]
            acc_oth[second, :PAD] += d_keys[3 * TILE :]
            acc_oth[second, PAD:] += d_vals[3 * TILE :]
            dq_t[...] += dot(pair_columns(kown, koth, first, second), d_scores, ((1,), (0,)))
            return inner

        lax.fori_loop(0, pairs_of(plan_ref, i), one, 0)
        parts = [dq_t[64 * h : 64 * h + 64, TILE * h : TILE * h + TILE] for h in range(3)]
        heads_t = jnp.concatenate(parts + [jnp.zeros((64, TILE), f32)], axis=0) * 0.125
        dq_ref[here, :] = heads_t.T.astype(bf16)
        return carry

    lax.fori_loop(0, tiles, one_tile, 0)
    doth_ref[...] = acc_oth[...].astype(bf16)


def attend_back(plan, q, own, oth, kpos, meta, grad, o, lse):
    rows = q.shape[0]
    wide = 3 * TILE
    return pl.pallas_call(
        attend_back_kernel,
        in_specs=[pl.BlockSpec(memory_space=pltpu.SMEM)]
        + [pl.BlockSpec(memory_space=pltpu.VMEM)] * 8,
        out_specs=[pl.BlockSpec(memory_space=pltpu.VMEM)] * 3,
        out_shape=[
            jax.ShapeDtypeStruct((rows, PAD), bf16),
            jax.ShapeDtypeStruct((rows, 2 * PAD), f32),
            jax.ShapeDtypeStruct((rows, 2 * PAD), bf16),
        ],
        scratch_shapes=[
            VMEM((rows, PAD), f32),
            VMEM((PAD, rows), bf16),
            VMEM((PAD, rows), bf16),
            VMEM((rows, 2 * PAD), f32),
            VMEM((wide, PAD), bf16),
            VMEM((wide, PAD), bf16),
            VMEM((PAD, wide), bf16),
            VMEM((PAD, wide), bf16),
            VMEM((PAD, wide), f32),
        ],
        compiler_params=pltpu.CompilerParams(vmem_limit_bytes=vmem_cap),
        cost_estimate=busy(24),
        name="attend_back",
    )(plan, q, own, oth, kpos, meta, grad, o, lse)


def unproject_kernel(
    place_ref, x_ref, dq_ref, down_ref, doth_ref, weight_ref,
    pieces_ref, grad_ref, gain_ref, shift_ref, bias_ref,
):
    i = pl.program_id(0)
    span_rows = pieces_ref.shape[1]

    @pl.when(i == 0)
    def _():
        gain_ref[...] = jnp.zeros_like(gain_ref)
        shift_ref[...] = jnp.zeros_like(shift_ref)
        bias_ref[...] = jnp.zeros_like(bias_ref)

    normed, unused = norm_parts(x_ref[...].astype(f32))
    dkv = (down_ref[...] + doth_ref[...].astype(f32)).astype(bf16)
    grad = jnp.concatenate([dq_ref[...], dkv], axis=1)
    grad_ref[...] = jnp.concatenate(
        [grad[:, :192], grad[:, PAD : PAD + 192], grad[:, 2 * PAD : 2 * PAD + 192], grad[:, 192:PAD]],
        axis=1,
    )
    bias_ref[...] += jnp.sum(grad.astype(f32), axis=0, keepdims=True)
    back = dot(grad, weight_ref[...], ((1,), (1,)))
    gain_ref[...] += jnp.sum(back * normed, axis=0, keepdims=True)
    shift_ref[...] += jnp.sum(back, axis=0, keepdims=True)
    for t in range(4):
        pieces_ref[place_ref[4 * i + t]] = back[span_rows * t : span_rows * (t + 1)].astype(bf16)


def unproject(place, x, dq, down, doth, weight, spans):
    rows, width = x.shape
    step = rows // 4
    pieces = jax.ShapeDtypeStruct((spans, rows // spans, width), bf16)
    grid_spec = pltpu.PrefetchScalarGridSpec(
        num_scalar_prefetch=1,
        grid=(4,),
        in_specs=[
            pl.BlockSpec((step, width), lambda i, *unused: (i, 0)),
            pl.BlockSpec((step, PAD), lambda i, *unused: (i, 0)),
            pl.BlockSpec((step, 2 * PAD), lambda i, *unused: (i, 0)),
            pl.BlockSpec((step, 2 * PAD), lambda i, *unused: (i, 0)),
            full_spec((width, 3 * PAD)),
        ],
        out_specs=[
            full_spec(pieces.shape),
            pl.BlockSpec((step, PACK), lambda i, *unused: (i, 0)),
            full_spec((1, width)),
            full_spec((1, width)),
            full_spec((1, 3 * PAD)),
        ],
    )
    return pl.pallas_call(
        unproject_kernel,
        grid_spec=grid_spec,
        out_shape=[
            pieces,
            jax.ShapeDtypeStruct((rows, PACK), bf16),
            jax.ShapeDtypeStruct((1, width), f32),
            jax.ShapeDtypeStruct((1, width), f32),
            jax.ShapeDtypeStruct((1, 3 * PAD), f32),
        ],
        compiler_params=pltpu.CompilerParams(vmem_limit_bytes=vmem_cap),
        cost_estimate=busy(8),
        name="unproject",
    )(place, x, dq, down, doth, weight)


def halve(value, bit):
    value = value.reshape(2, value.shape[0] // 2, value.shape[1])
    return row(value, bit), row(value, 1 - bit)


def reduce_z(value, z):
    value = value.reshape(4, value.shape[0] // 4, value.shape[1])
    return row(value, z), [row(value, (z + k) % 4) for k in (1, 2, 3)]


def over_z(sends):
    return [send_z(sends[k - 1], k) for k in (1, 2, 3)]


def reduce_plane(value, group):
    value = value.reshape(4, value.shape[0] // 4, value.shape[1])
    return row(value, group), [row(value, group ^ f) for f in (1, 2, 3)]


def over_plane(sends):
    return [send_flip(sends[f - 1], f) for f in (1, 2, 3)]


def gather_z(value):
    pair = jnp.stack([value, send_flip(value, 8)])
    return jnp.concatenate([pair, send_flip(pair, 4)], axis=0)


def spread_once(left, right):
    return jnp.concatenate([left, send_flip(left, 1)], axis=0), jnp.concatenate(
        [right, send_flip(right, 2)], axis=0
    )


def spread_twice(left, right):
    return left, send_flip(left, 2), right, send_flip(right, 1)


def cut_lanes(value, at):
    return value[:, :, :at], value[:, :, at:]


def entry(refs, side, f, k):
    if side == 0:
        return refs[f // 2][4 * (f % 2) + k].astype(f32)
    return refs[2 + f % 2][4 * (f // 2) + k].astype(f32)


def block_of(z, k):
    return ((z & 1) ^ (k >> 1)) * 2 + ((z >> 1) ^ (k & 1))


def chip_of(z, k):
    return z ^ ((k >> 1) + 2 * (k & 1))


def place_proj_kernel(where_ref, *refs):
    parts, out_ref = refs[:4], refs[4]
    z, group = where_ref[0], where_ref[1]
    rows, half = parts[0].shape[1:]
    for f in range(4):
        x, y = (group ^ f) & 1, (group ^ f) >> 1
        for k in range(4):
            at = ((2 * x + y) * 4 + block_of(z, k)) * rows
            out_ref[pl.ds(pl.multiple_of(at, 8), rows), :half] = entry(parts, 0, f, k)
            at = ((2 * y + x) * 4 + block_of(z, k)) * rows
            out_ref[pl.ds(pl.multiple_of(at, 8), rows), half:] = entry(parts, 1, f, k)


def place_rest_kernel(where_ref, *refs):
    parts, fc_ref, out_ref = refs[:4], refs[4], refs[5]
    z, group = where_ref[0], where_ref[1]
    rows, half = parts[0].shape[1:]
    fc_wide = fc_ref.shape[1]
    for f in range(4):
        for k in range(4):
            at = ((group ^ f) * 4 + chip_of(z, k)) * rows
            at = pl.ds(pl.multiple_of(at, 8), rows)
            fc_ref[at, :half] = entry(parts, 0, f, k)
            right = entry(parts, 1, f, k)
            fc_ref[at, half:] = right[:, : fc_wide - half]
            out_ref[at, :] = right[:, fc_wide - half :]


def place_in_kernel(where_ref, *refs):
    parts, in_ref, small_ref, held = refs[:4], refs[4], refs[5], refs[6]
    z, group = where_ref[0], where_ref[1]
    upper = parts[0].shape[1]
    rows = upper + parts[2].shape[1] - 8
    small_ref[...] = jnp.zeros(small_ref.shape, f32)
    for f in range(4):
        for k in range(4):
            block = z ^ k
            held[group ^ f, block, :upper] = entry(parts, 0, f, k)
            right = entry(parts, 1, f, k)
            held[group ^ f, block, upper:rows] = right[:-8]
            small_ref[block] = small_ref[block] + right[-8:]
    for block in range(4):
        for i in range(3):
            at = 192 * i
            columns = [held[g, block, :, at : at + 192] for g in range(4)]
            in_ref[rows * block : rows * (block + 1), 768 * i : 768 * (i + 1)] = jnp.concatenate(
                columns, axis=1
            )


def place(kernel, name, micros, where, parts, shapes, scratch=()):
    return pl.pallas_call(
        kernel,
        in_specs=[pl.BlockSpec(memory_space=pltpu.SMEM)]
        + [pl.BlockSpec(memory_space=pltpu.VMEM)] * len(parts),
        out_specs=[pl.BlockSpec(memory_space=pltpu.VMEM)] * len(shapes),
        out_shape=[jax.ShapeDtypeStruct(shape, f32) for shape in shapes],
        scratch_shapes=list(scratch),
        compiler_params=pltpu.CompilerParams(vmem_limit_bytes=vmem_cap),
        cost_estimate=busy(micros),
        name=name,
    )(where, *parts)


def split_halves(value, w, axis):
    low, high = jnp.split(value, 2, axis)
    return jnp.where(w == 0, low, high), jnp.where(w == 0, high, low)


def grad_dot(left, right):
    return dot(left, right, ((0,), (0,)))


def norm_back(grad, rows, gain):
    normed, inverse = norm_parts(rows)
    scaled = grad * gain
    part = scaled - jnp.mean(scaled, axis=-1, keepdims=True)
    part = part - normed * jnp.mean(scaled * normed, axis=-1, keepdims=True)
    return inverse * part, normed


def by_owner(
    block_input, span_order, doc_lengths, ln1_gain, ln1_bias, w_qkv, qv_bias, w_out, out_bias,
    ln2_gain, ln2_bias, w_fc, fc_bias, w_proj, proj_bias, d_out,
):
    seq_group, seq_dev, width = block_input.shape
    seqs = 2 * seq_group
    span_rows = seq_dev // 2
    chips = span_order.shape[0]
    rows = chips * span_rows
    me = lax.axis_index("ctx")
    w = lax.axis_index("wt")
    z, y, x = me // 4, me // 2 % 2, me % 2
    where = (z, y, x)
    group = me % 4

    second = (row(span_order, me)[0] % 2) != w

    def take_spans(value):
        value = value.reshape(seq_group, 2, span_rows, width)
        keep = jnp.where(second, value[:, 1], value[:, 0])
        give = jnp.where(second, value[:, 0], value[:, 1])
        got = other_core(give)
        return jnp.where(
            w == 0, jnp.concatenate([keep, got], axis=0), jnp.concatenate([got, keep], axis=0)
        )

    def give_spans(value):
        low, high = value[:seq_group], value[seq_group:]
        keep = jnp.where(w == 0, low, high)
        got = other_core(jnp.where(w == 0, high, low))
        first = jnp.where(second, got, keep)
        last = jnp.where(second, keep, got)
        return jnp.concatenate([first, last], axis=1)

    def to_sequence(value):
        got = [send_z(row(value, (z + k) % 4), k) for k in (1, 2, 3)]
        return [row(value, z)] + got

    z_low, z_high = z % 2, z // 2

    def z_first(blocks):
        keep = jnp.stack([row(blocks, z_low + 2 * h) for h in (0, 1)])
        give = jnp.stack([row(blocks, 1 - z_low + 2 * h) for h in (0, 1)])
        return keep, send_flip(give, 4)

    def z_second(keep, got):
        pairs = jnp.stack([keep, got], axis=1)
        here, there = row(pairs, z_high), send_flip(row(pairs, 1 - z_high), 8)
        return jnp.concatenate([here, there], axis=0)

    def by_chip(value):
        return jnp.stack([row(value, (z - s) % 4) for s in range(seqs)])

    def by_source(got):
        return jnp.stack([row(got, z ^ s) for s in range(seqs)])

    kept = to_sequence(take_spans(block_input))
    left, right = jnp.stack(kept[:2]), jnp.stack(kept[2:])
    tokens_low = jnp.concatenate([left, right], axis=0)
    span_order, doc_lengths, unused = lax.optimization_barrier((span_order, doc_lengths, (left, right)))
    left_x, right_y = send_flip(left, 1), send_flip(right, 2)
    ranks = jnp.arange(rows, dtype=jnp.int32)
    even_pos = 2 * span_rows * (ranks // span_rows) + ranks % span_rows
    own_pos = even_pos + span_rows * w
    oth_pos = even_pos + span_rows * (1 - w)
    kpos = jnp.broadcast_to(jnp.stack([own_pos, oth_pos])[:, :, None], (2, rows, TILE)).astype(jnp.int32)
    left_x, right_y, kpos = lax.optimization_barrier((left_x, right_y, kpos))
    left = jnp.concatenate([left, left_x], axis=0)
    right = jnp.concatenate([right, right_y], axis=0)
    pieces = (left, send_flip(left, 2), right, send_flip(right, 1))
    (
        ln1_gain, ln1_bias, w_qkv, qv_bias, d_out, out_bias, ln2_gain, ln2_bias, proj_bias, fc_bias, unused,
    ) = lax.optimization_barrier(
        (
            ln1_gain, ln1_bias, w_qkv, qv_bias, d_out, out_bias, ln2_gain, ln2_bias, proj_bias, fc_bias,
            (left, right),
        )
    )
    cot_low = jnp.stack(to_sequence(take_spans(d_out))).reshape(seqs * span_rows, width)
    d_mlp = (branch_scale * cot_low.astype(f32)).astype(bf16)

    chip_ids = jnp.arange(chips, dtype=jnp.int32)
    span_here = jnp.where(span_order[:, 0] % 2 == w, span_order[:, 0], span_order[:, 1]) // 2
    span_ids = jnp.arange(chips, dtype=jnp.int32)
    holder = jnp.sum(
        jnp.where(span_here[None, :] == span_ids[:, None], chip_ids[None, :], 0), axis=1
    ).astype(jnp.int32)
    back_z = (z - holder // 4) % 4
    flip = group ^ (holder % 4)
    order = jnp.where(
        back_z < 2,
        (flip // 2) * 4 + (flip % 2) * 2 + back_z,
        8 + (flip % 2) * 4 + (flip // 2) * 2 + back_z - 2,
    ).astype(jnp.int32)
    order_back = (flip * 4 + back_z).astype(jnp.int32)
    owner = (holder % 4 * 4 + back_z).astype(jnp.int32)

    lengths_oth = other_core(doc_lengths)
    lengths = jnp.where(
        w == 0,
        jnp.concatenate([doc_lengths, lengths_oth], axis=0),
        jnp.concatenate([lengths_oth, doc_lengths], axis=0),
    )
    lengths = row(lengths, z)
    ends = jnp.cumsum(lengths)[:-1]
    starts = jnp.sum(
        jnp.where(own_pos[:, None] >= ends[None, :], lengths[None, :-1], 0), axis=1
    ).astype(jnp.int32)
    tiles = rows // TILE
    own_tiles = own_pos.reshape(tiles, TILE)
    start_tiles = starts.reshape(tiles, TILE)
    meta = jnp.tile(jnp.stack([own_tiles, start_tiles], axis=1), (1, 1, 3)).astype(jnp.int32)
    even_tiles = even_pos.reshape(tiles, TILE)
    low = jnp.sum(
        (even_tiles[None, :, -1] + span_rows < start_tiles[:, 0:1]).astype(jnp.int32), axis=1
    ).astype(jnp.int32)
    high = jnp.sum(
        (even_tiles[None, :, 0] <= own_tiles[:, -1:]).astype(jnp.int32), axis=1
    ).astype(jnp.int32)

    room = jnp.zeros((chips - tiles,), jnp.int32)
    plan = jnp.stack([jnp.concatenate([low, room]), jnp.concatenate([high, room]), owner])

    feats = width // GROUPS
    half = width // 2
    here = jnp.stack([z, group, w]).astype(jnp.int32)
    in_own = jnp.concatenate(
        [
            lax.dynamic_slice_in_dim(w_qkv, width * i + half * (group // 2), half, 1)
            for i in range(3)
        ],
        axis=1,
    )
    in_oth_core = other_core(in_own)
    vectors = [ln1_gain, ln1_bias, qv_bias[0], qv_bias[1], out_bias, ln2_gain, ln2_bias, proj_bias]
    vectors += [fc_bias[half * i : half * (i + 1)] for i in range(4)]
    lines = lax.broadcasted_iota(jnp.int32, (len(vectors), half), 0)
    small = jnp.zeros((len(vectors), half), f32)
    for i, one in enumerate(vectors):
        small = jnp.where(lines == i, jnp.broadcast_to(one.astype(f32), small.shape), small)
    small_oth = other_core(small)

    def vector(index):
        own, oth = small[index : index + 1], small_oth[index : index + 1]
        return jnp.concatenate([jnp.where(w == 0, own, oth), jnp.where(w == 0, oth, own)], axis=1)

    pieces, w_out, w_fc, w_proj, unused = lax.optimization_barrier(
        (pieces, w_out, w_fc, w_proj, (meta, plan, in_oth_core, small_oth, d_mlp))
    )
    out_oth, fc_oth, proj_oth = other_core(w_out), other_core(w_fc), other_core(w_proj)
    x_sorted, normed_one, query, kv_own, weight_in = project(
        order, here, pieces, in_own, in_oth_core, small, small_oth
    )
    query, kv_own, out_oth, fc_oth, proj_oth = lax.optimization_barrier(
        (query, kv_own, out_oth, fc_oth, proj_oth)
    )
    kv_oth = other_core(kv_own)
    attn, lse, attn_send = attend(plan, query, kv_own, kv_oth, kpos, meta, chips)
    attn_got = swap_plane(attn_send.reshape(GROUPS, seqs, span_rows, feats))

    d_mlp = after(d_mlp, attn_send)
    mlp_both = jnp.concatenate([d_mlp, other_core(d_mlp)], axis=0)
    grad_own = dot(d_mlp, w_proj, ((1,), (1,)))
    attn_got = after(attn_got, grad_own, mlp_both).reshape(GROUPS, seqs * span_rows, feats)

    tokens = tokens_low.reshape(seqs * span_rows, width)
    (
        resid, attn_low, normed_two, hidden_low, d_pre, d_resid, d_branch, d_send, *sums
    ) = middle(
        attn_got, tokens, cot_low, d_mlp, grad_own, proj_oth,
        w_out, out_oth, w_fc, fc_oth, here, small, small_oth,
    )
    d_got = swap_plane(d_send.reshape(GROUPS, seqs, span_rows, feats)).reshape(chips, span_rows, feats)
    hidden_own, hidden_oth = split_halves(hidden_low, w, 1)
    hidden_both = jnp.concatenate([hidden_own, other_core(hidden_oth)], axis=0)
    pre_both = jnp.concatenate([d_pre, other_core(d_pre)], axis=0)
    normed_own, normed_oth = split_halves(normed_two, w, 1)
    normed_both = jnp.concatenate([normed_own, other_core(normed_oth)], axis=0)
    attn_own, attn_oth = split_halves(attn_low, w, 1)
    attn_both = jnp.concatenate([attn_own, other_core(attn_oth)], axis=0)
    low_bit, high_bit = z % 2, z // 2
    branch_both = jnp.concatenate([d_branch, other_core(d_branch)], axis=0)
    hidden_both = after(hidden_both, d_send)
    grad_proj = grad_dot(hidden_both, mlp_both).astype(bf16)
    proj_left, left_send = halve(grad_proj[:, :half], x)
    proj_right, right_send = halve(grad_proj[:, half:], y)
    left_recv, right_recv = send_flip(left_send, 1), send_flip(right_send, 2)
    normed_both, attn_both, d_got, unused = lax.optimization_barrier(
        (normed_both, attn_both, d_got, (left_send, right_send))
    )
    fc_cols = d_pre.shape[1]
    grad_rest = jnp.concatenate(
        [grad_dot(normed_both, pre_both).astype(bf16), grad_dot(attn_both, branch_both).astype(bf16)],
        axis=1,
    )
    rest_keep, rest_sends = reduce_plane(grad_rest, group)
    left_recv, right_recv, unused = lax.optimization_barrier((left_recv, right_recv, rest_sends))
    proj_left, left_send = halve(sum_low(proj_left, left_recv), y)
    proj_right, right_send = halve(sum_low(proj_right, right_recv), x)
    left_recv, right_recv = send_flip(left_send, 2), send_flip(right_send, 1)
    rest_plane = over_plane(rest_sends)

    d_got = after(d_got, left_send, right_send, *rest_sends)
    d_query, d_own, d_oth = attend_back(plan, query, kv_own, kv_oth, kpos, meta, d_got, attn, lse)
    left_recv, right_recv, rest_plane, d_query, d_oth = lax.optimization_barrier(
        (left_recv, right_recv, rest_plane, d_query, d_oth)
    )
    d_recv = other_core(d_oth)
    grad_proj = jnp.concatenate(
        [sum_low(proj_left, left_recv), sum_low(proj_right, right_recv)], axis=1
    )
    proj_keep, proj_send = halve(grad_proj, low_bit)
    proj_recv = send_flip(proj_send, 4)
    rest_keep, rest_sends = reduce_z(sum_low(rest_keep, *rest_plane), z)
    proj_recv, d_recv, rest_sends = lax.optimization_barrier((proj_recv, d_recv, rest_sends))
    rest_z = over_z(rest_sends)
    proj_keep, proj_send = halve(sum_low(proj_keep, proj_recv), high_bit)
    proj_recv = send_flip(proj_send, 8)
    d_recv = after(d_recv, proj_send)
    d_pieces, d_qkv, part_gain, part_shift, part_bias = unproject(
        order_back, x_sorted, d_query, d_own, d_recv, weight_in, chips
    )
    proj_recv, rest_z, d_pieces, d_qkv, part_gain, part_shift, part_bias, sums = lax.optimization_barrier(
        (proj_recv, rest_z, d_pieces, d_qkv, part_gain, part_shift, part_bias, sums)
    )

    proj_shard = sum_low(proj_keep, proj_recv)
    rest_shard = sum_low(rest_keep, *rest_z)
    d_qkv, unused = lax.optimization_barrier((d_qkv, (proj_shard, rest_shard)))
    proj_pair = jnp.stack([proj_shard, send_flip(proj_shard, 8)])
    rest_pair = jnp.stack([rest_shard, send_flip(rest_shard, 8)])
    back_sends = [d_pieces[4 * f : 4 * f + 4] for f in (1, 2, 3)]
    back_x, back_y = send_flip(back_sends[0], 1), send_flip(back_sends[1], 2)
    normed_own, normed_oth = split_halves(normed_one, w, 1)
    in_oth = grad_dot(normed_oth, d_qkv).astype(bf16)
    in_got = other_core(in_oth)
    grads_own, grads_oth = pack(here, part_gain, part_shift, part_bias, sums)
    small_rows = (grads_own + other_core(grads_oth)).astype(bf16).reshape(4, 3, half)
    small_rows = jnp.pad(small_rows, ((0, 0), (0, 5), (0, PACK - half)))
    grad_in = (grad_dot(normed_own, d_qkv) + in_got.astype(f32)).astype(bf16)
    grad_in = jnp.concatenate([grad_in.reshape(4, half // 4, PACK), small_rows], axis=1)
    in_keep, in_send = halve(grad_in.reshape(-1, PACK), high_bit)
    proj_pair, rest_pair, back_x, back_y, back_xy, in_send = lax.optimization_barrier(
        (proj_pair, rest_pair, back_x, back_y, back_sends[2], in_send)
    )
    proj_all = jnp.concatenate([proj_pair, send_flip(proj_pair, 4)], axis=0)
    rest_all = jnp.concatenate([rest_pair, send_flip(rest_pair, 4)], axis=0)
    in_recv = send_flip(in_send, 8)
    back_xy = send_flip(back_xy, 3)
    proj_all, rest_all, in_recv, back_xy = lax.optimization_barrier((proj_all, rest_all, in_recv, back_xy))
    in_keep, in_send = halve(sum_low(in_keep, in_recv), low_bit)
    in_recv = send_flip(in_send, 4)
    proj_once = spread_once(*cut_lanes(proj_all, half))
    rest_once = spread_once(*cut_lanes(rest_all, rest_all.shape[2] // 2))
    proj_once, rest_once, in_recv = lax.optimization_barrier((proj_once, rest_once, in_recv))
    in_shard = sum_low(in_keep, in_recv)
    in_pair = jnp.stack([in_shard, send_flip(in_shard, 4)])
    proj_parts = spread_twice(*proj_once)
    back = sum_low(d_pieces[:4], back_x, back_y, after(back_xy, in_shard))
    proj_parts, in_pair, rest_once, back = lax.optimization_barrier((proj_parts, in_pair, rest_once, back))
    in_all = jnp.concatenate([in_pair, send_flip(in_pair, 8)], axis=0)
    rest_parts = spread_twice(*rest_once)
    d_first, unused = norm_back(
        back.reshape(seqs * span_rows, width).astype(f32), tokens.astype(f32), vector(0)
    )
    d_input = (d_resid + d_first).astype(bf16).reshape(seqs, span_rows, width)
    d_input = z_first(by_chip(d_input))
    hidden_own, hidden_oth, unused = lax.optimization_barrier((hidden_own, hidden_oth, in_pair))
    mlp = dot(hidden_own, w_proj, ((1,), (0,))) + dot(hidden_oth, proj_oth, ((1,), (0,))) + vector(7)
    block_out = (resid + branch_scale * mlp).astype(bf16).reshape(seqs, span_rows, width)
    block_out = by_chip(block_out)
    rest_parts, in_all, block_out, proj_parts, d_input = lax.optimization_barrier(
        (rest_parts, in_all, block_out, proj_parts, d_input)
    )
    in_once = spread_once(in_all[:, :56], in_all[:, 56:])
    d_input = z_second(*d_input)
    block_out = z_first(block_out)
    in_once, d_input, block_out, proj_parts, rest_parts = lax.optimization_barrier(
        (in_once, d_input, block_out, proj_parts, rest_parts)
    )
    in_parts = spread_twice(*in_once)
    block_out = z_second(*block_out)
    (grad_proj,) = place(
        place_proj_kernel, "place_proj", 5, here, proj_parts, [(fc_cols // 2, width)]
    )
    grad_fc, grad_out = place(
        place_rest_kernel, "place_rest", 5, here, rest_parts, [(half, fc_cols), (half, width)]
    )
    grad_w_qkv, small_all = place(
        place_in_kernel, "place_in", 4, here, in_parts,
        [(half, 3 * width), (4, 8, PACK)],
        [VMEM((4, 4, half // 4, PACK), f32)],
    )

    def piece(index):
        return small_all[index // 3, index % 3, :half]

    return (
        give_spans(by_source(block_out)),
        give_spans(by_source(d_input)).astype(f32),
        piece(0),
        piece(1),
        grad_w_qkv,
        jnp.stack([piece(2), piece(3)]),
        grad_out,
        piece(4),
        piece(5),
        piece(6),
        grad_fc,
        jnp.concatenate([piece(8), piece(9), piece(10), piece(11)]),
        grad_proj,
        piece(7),
    )


def layer_norm(values, gain, shift):
    center = jnp.mean(values, axis=-1, keepdims=True)
    moved = values - center
    spread = jnp.mean(moved * moved, axis=-1, keepdims=True)
    return moved * lax.rsqrt(spread + 1e-05) * gain + shift


def gelu_tanh(values):
    return (
        0.5
        * values
        * (1.0 + jnp.tanh(0.7978845608028654 * (values + 0.044715 * values * values * values)))
    )


def split_count(row_total, limit):
    pieces = 1
    while row_total % pieces != 0 or row_total // pieces > limit:
        pieces += 1
    return pieces


def row_positions(order_table, first_index, row_total, seq_dev, span_rows):
    rows_here = first_index + jnp.arange(row_total, dtype=jnp.int32)
    device_of = rows_here // seq_dev
    half_of = rows_here % seq_dev // span_rows
    slot_index = device_of * 2 + half_of
    flat_order = order_table.reshape(-1)
    table_slots = jnp.arange(flat_order.shape[0], dtype=jnp.int32)
    picked = jnp.sum(
        jnp.where(slot_index[:, None] == table_slots[None, :], flat_order[None, :], 0), axis=1
    )
    return picked * span_rows + rows_here % span_rows


def doc_of(positions, lengths_row):
    ends_at = jnp.cumsum(lengths_row)
    inner_ends = ends_at[:-1]
    return jnp.sum((positions[:, None] >= inner_ends[None, :]).astype(jnp.int32), axis=1)


def visible(query_pos, query_doc, key_pos, key_doc):
    causal = key_pos[None, None, :] <= query_pos[None, :, None]
    same_doc = key_doc[:, None, :] == query_doc[:, :, None]
    return (causal & same_doc)[:, :, None, :]


def per_device(
    block_input,
    span_order,
    doc_lengths,
    ln1_gain,
    ln1_bias,
    w_qkv,
    qv_bias,
    w_out,
    out_bias,
    ln2_gain,
    ln2_bias,
    w_fc,
    fc_bias,
    w_proj,
    proj_bias,
    d_out,
):
    seq_group, seq_dev, width = block_input.shape
    heads = HEADS
    head_dim = width // heads
    span_rows = seq_dev // 2
    score_scale = head_dim ** (-0.5)

    def docs_for(positions):
        return jax.vmap(doc_of, in_axes=(None, 0))(positions, doc_lengths)

    weights_all = (
        lax.all_gather(ln1_gain, "wt", axis=0, tiled=True),
        lax.all_gather(ln1_bias, "wt", axis=0, tiled=True),
        lax.all_gather(w_qkv, "wt", axis=0, tiled=True),
        lax.all_gather(qv_bias, "wt", axis=1, tiled=True),
        lax.all_gather(w_out, "wt", axis=0, tiled=True),
        lax.all_gather(out_bias, "wt", axis=0, tiled=True),
        lax.all_gather(ln2_gain, "wt", axis=0, tiled=True),
        lax.all_gather(ln2_bias, "wt", axis=0, tiled=True),
        lax.all_gather(w_fc, "wt", axis=0, tiled=True),
        lax.all_gather(fc_bias, "wt", axis=0, tiled=True),
        lax.all_gather(w_proj, "wt", axis=0, tiled=True),
        lax.all_gather(proj_bias, "wt", axis=0, tiled=True),
    )
    gain_one = weights_all[0].astype(jnp.float32)
    shift_one = weights_all[1].astype(jnp.float32)
    bias_pair = weights_all[3].astype(jnp.float32)
    bias_out = weights_all[5].astype(jnp.float32)
    gain_two = weights_all[6].astype(jnp.float32)
    shift_two = weights_all[7].astype(jnp.float32)
    bias_fc = weights_all[9].astype(jnp.float32)
    bias_proj = weights_all[11].astype(jnp.float32)
    me_ctx = lax.axis_index("ctx")
    local_pos = row_positions(span_order, me_ctx * seq_dev, seq_dev, seq_dev, span_rows)
    local_doc = docs_for(local_pos)
    tokens_in = block_input.astype(jnp.float32)
    normed_one = layer_norm(tokens_in, gain_one, shift_one).astype(jnp.bfloat16)
    qkv_bias = jnp.concatenate([bias_pair[0], jnp.zeros((width,), jnp.float32), bias_pair[1]])
    projected = (
        jnp.einsum("btd,de->bte", normed_one, weights_all[2], preferred_element_type=jnp.float32)
        + qkv_bias
    )
    projected_low = projected.astype(jnp.bfloat16)
    query_low = projected_low[..., :width]
    key_low = projected_low[..., width : 2 * width]
    value_low = projected_low[..., 2 * width :]
    query_heads = query_low.reshape(seq_group, seq_dev, heads, head_dim)
    key_heads = key_low.reshape(seq_group, seq_dev, heads, head_dim)
    value_heads = value_low.reshape(seq_group, seq_dev, heads, head_dim)
    start_state = (
        jnp.zeros((seq_group, seq_dev, heads, head_dim), jnp.float32),
        jnp.full((seq_group, seq_dev, heads), neg_large, jnp.float32),
        jnp.zeros((seq_group, seq_dev, heads), jnp.float32),
    )
    key_piece = lax.all_gather(key_low, "ctx", axis=1, tiled=True)
    value_piece = lax.all_gather(value_low, "ctx", axis=1, tiled=True)
    piece_rows = key_piece.shape[1]
    key_pos = row_positions(span_order, jnp.int32(0), piece_rows, seq_dev, span_rows)
    key_doc = docs_for(key_pos)
    block_rows = piece_rows // split_count(piece_rows, 1024)

    def one_block(block_index, running):
        acc_sum, run_max, run_total = running
        first_row = block_index * block_rows
        key_block = lax.dynamic_slice_in_dim(key_piece, first_row, block_rows, 1).reshape(
            seq_group, block_rows, heads, head_dim
        )
        value_block = lax.dynamic_slice_in_dim(value_piece, first_row, block_rows, 1).reshape(
            seq_group, block_rows, heads, head_dim
        )
        allowed = visible(
            local_pos,
            local_doc,
            lax.dynamic_slice_in_dim(key_pos, first_row, block_rows, 0),
            lax.dynamic_slice_in_dim(key_doc, first_row, block_rows, 1),
        )
        scores = (
            jnp.einsum(
                "bqhd,bkhd->bqhk", query_heads, key_block, preferred_element_type=jnp.float32
            )
            * score_scale
        )
        scores = jnp.where(allowed, scores, neg_large)
        new_max = jnp.maximum(run_max, jnp.max(scores, axis=-1))
        weights = jnp.where(allowed, jnp.exp(scores - new_max[..., None]), 0.0)
        rescale = jnp.exp(run_max - new_max)
        run_total = run_total * rescale + jnp.sum(weights, axis=-1)
        acc_sum = acc_sum * rescale[..., None] + jnp.einsum(
            "bqhk,bkhd->bqhd",
            weights.astype(jnp.bfloat16),
            value_block,
            preferred_element_type=jnp.float32,
        )
        return (acc_sum, new_max, run_total)

    acc_sum, run_max, run_total = lax.fori_loop(0, piece_rows // block_rows, one_block, start_state)
    attn_heads = acc_sum / run_total[..., None]
    log_total = run_max + jnp.log(run_total)
    attn_out = attn_heads.reshape(seq_group, seq_dev, width)
    attn_low = attn_out.astype(jnp.bfloat16)
    branch_pre = (
        jnp.einsum("btd,de->bte", attn_low, weights_all[4], preferred_element_type=jnp.float32)
        + bias_out
    )
    resid_one = tokens_in + branch_scale * branch_pre
    normed_two = layer_norm(resid_one, gain_two, shift_two).astype(jnp.bfloat16)
    hidden_pre = (
        jnp.einsum("btd,df->btf", normed_two, weights_all[8], preferred_element_type=jnp.float32)
        + bias_fc
    )
    hidden_low = gelu_tanh(hidden_pre).astype(jnp.bfloat16)
    mlp_pre = (
        jnp.einsum("btf,fd->btd", hidden_low, weights_all[10], preferred_element_type=jnp.float32)
        + bias_proj
    )
    block_out = (resid_one + branch_scale * mlp_pre).astype(jnp.bfloat16)
    weights_back = (
        lax.all_gather(ln1_gain, "wt", axis=0, tiled=True),
        lax.all_gather(ln1_bias, "wt", axis=0, tiled=True),
        lax.all_gather(w_qkv, "wt", axis=0, tiled=True),
        lax.all_gather(qv_bias, "wt", axis=1, tiled=True),
        lax.all_gather(w_out, "wt", axis=0, tiled=True),
        lax.all_gather(out_bias, "wt", axis=0, tiled=True),
        lax.all_gather(ln2_gain, "wt", axis=0, tiled=True),
        lax.all_gather(ln2_bias, "wt", axis=0, tiled=True),
        lax.all_gather(w_fc, "wt", axis=0, tiled=True),
        lax.all_gather(fc_bias, "wt", axis=0, tiled=True),
        lax.all_gather(w_proj, "wt", axis=0, tiled=True),
        lax.all_gather(proj_bias, "wt", axis=0, tiled=True),
    )
    back_gain_one = weights_back[0].astype(jnp.float32)
    back_shift_one = weights_back[1].astype(jnp.float32)
    back_gain_two = weights_back[6].astype(jnp.float32)
    back_shift_two = weights_back[7].astype(jnp.float32)
    cotangent = d_out.astype(jnp.float32)
    d_mlp = (branch_scale * cotangent).astype(jnp.bfloat16)
    grad_w_proj = jnp.einsum("btf,btd->fd", hidden_low, d_mlp, preferred_element_type=jnp.float32)
    grad_proj_bias = jnp.sum(d_mlp.astype(jnp.float32), axis=(0, 1))
    d_hidden = jnp.einsum(
        "btd,fd->btf", d_mlp, weights_back[10], preferred_element_type=jnp.float32
    )
    gelu_unused, gelu_pull = jax.vjp(gelu_tanh, hidden_pre)
    d_pre = gelu_pull(d_hidden)[0].astype(jnp.bfloat16)
    grad_w_fc = jnp.einsum("btd,btf->df", normed_two, d_pre, preferred_element_type=jnp.float32)
    grad_fc_bias = jnp.sum(d_pre.astype(jnp.float32), axis=(0, 1))
    d_normed_two = jnp.einsum(
        "btf,df->btd", d_pre, weights_back[8], preferred_element_type=jnp.float32
    )
    norm_unused, norm_pull = jax.vjp(layer_norm, resid_one, back_gain_two, back_shift_two)
    d_resid_part, grad_ln2_gain, grad_ln2_bias = norm_pull(d_normed_two)
    d_resid = cotangent + d_resid_part
    d_branch = (branch_scale * d_resid).astype(jnp.bfloat16)
    grad_w_out = jnp.einsum("btd,bte->de", attn_low, d_branch, preferred_element_type=jnp.float32)
    grad_out_bias = jnp.sum(d_branch.astype(jnp.float32), axis=(0, 1))
    d_attn_low = jnp.einsum(
        "bte,de->btd", d_branch, weights_back[4], preferred_element_type=jnp.float32
    ).astype(jnp.bfloat16)
    d_attn_heads = d_attn_low.reshape(seq_group, seq_dev, heads, head_dim)
    delta = jnp.sum(d_attn_heads.astype(jnp.float32) * attn_heads, axis=-1)
    fold_key_piece = lax.all_gather(key_low, "ctx", axis=1, tiled=True)
    fold_value_piece = lax.all_gather(value_low, "ctx", axis=1, tiled=True)
    piece_rows = fold_key_piece.shape[1]
    fold_key_pos = row_positions(span_order, jnp.int32(0), piece_rows, seq_dev, span_rows)
    fold_key_doc = docs_for(fold_key_pos)
    fold_block_rows = piece_rows // split_count(piece_rows, 1024)

    def one_block(block_index, grad_query):
        first_row = block_index * fold_block_rows
        key_block = lax.dynamic_slice_in_dim(fold_key_piece, first_row, fold_block_rows, 1).reshape(
            seq_group, fold_block_rows, heads, head_dim
        )
        value_block = lax.dynamic_slice_in_dim(
            fold_value_piece, first_row, fold_block_rows, 1
        ).reshape(seq_group, fold_block_rows, heads, head_dim)
        allowed = visible(
            local_pos,
            local_doc,
            lax.dynamic_slice_in_dim(fold_key_pos, first_row, fold_block_rows, 0),
            lax.dynamic_slice_in_dim(fold_key_doc, first_row, fold_block_rows, 1),
        )
        scores = (
            jnp.einsum(
                "bqhd,bkhd->bqhk", query_heads, key_block, preferred_element_type=jnp.float32
            )
            * score_scale
        )
        probs = jnp.where(allowed, jnp.exp(scores - log_total[..., None]), 0.0)
        d_probs = jnp.einsum(
            "bqhd,bkhd->bqhk", d_attn_heads, value_block, preferred_element_type=jnp.float32
        )
        d_scores = (probs * (d_probs - delta[..., None])).astype(jnp.bfloat16)
        return (
            grad_query
            + jnp.einsum("bqhk,bkhd->bqhd", d_scores, key_block, preferred_element_type=jnp.float32)
            * score_scale
        )

    grad_query = lax.fori_loop(
        0,
        piece_rows // fold_block_rows,
        one_block,
        jnp.zeros((seq_group, seq_dev, heads, head_dim), jnp.float32),
    )
    stats_all = (
        lax.all_gather(log_total, "ctx", axis=1, tiled=True),
        lax.all_gather(delta, "ctx", axis=1, tiled=True),
    )
    totals_every = stats_all[0]
    deltas_every = stats_all[1]

    def fold_keys(carried, received, first_index):
        query_piece, grad_piece = received
        piece_rows = query_piece.shape[1]
        query_pos = row_positions(span_order, first_index, piece_rows, seq_dev, span_rows)
        query_doc = docs_for(query_pos)
        block_rows = piece_rows // split_count(piece_rows, 1024)

        def one_block(block_index, running):
            grad_key, grad_value = running
            first_row = block_index * block_rows
            query_block = lax.dynamic_slice_in_dim(query_piece, first_row, block_rows, 1).reshape(
                seq_group, block_rows, heads, head_dim
            )
            grad_block = lax.dynamic_slice_in_dim(grad_piece, first_row, block_rows, 1).reshape(
                seq_group, block_rows, heads, head_dim
            )
            total_block = lax.dynamic_slice_in_dim(totals_every, first_row, block_rows, 1)
            delta_block = lax.dynamic_slice_in_dim(deltas_every, first_row, block_rows, 1)
            allowed = visible(
                lax.dynamic_slice_in_dim(query_pos, first_row, block_rows, 0),
                lax.dynamic_slice_in_dim(query_doc, first_row, block_rows, 1),
                local_pos,
                local_doc,
            )
            scores = (
                jnp.einsum(
                    "bqhd,bkhd->bqhk", query_block, key_heads, preferred_element_type=jnp.float32
                )
                * score_scale
            )
            probs = jnp.where(allowed, jnp.exp(scores - total_block[..., None]), 0.0)
            grad_value = grad_value + jnp.einsum(
                "bqhk,bqhd->bkhd",
                probs.astype(jnp.bfloat16),
                grad_block,
                preferred_element_type=jnp.float32,
            )
            d_probs = jnp.einsum(
                "bqhd,bkhd->bqhk", grad_block, value_heads, preferred_element_type=jnp.float32
            )
            d_scores = (probs * (d_probs - delta_block[..., None])).astype(jnp.bfloat16)
            grad_key = (
                grad_key
                + jnp.einsum(
                    "bqhk,bqhd->bkhd", d_scores, query_block, preferred_element_type=jnp.float32
                )
                * score_scale
            )
            return (grad_key, grad_value)

        return lax.fori_loop(0, piece_rows // block_rows, one_block, carried)

    zero_heads = jnp.zeros((seq_group, seq_dev, heads, head_dim), jnp.float32)
    grad_key, grad_value = fold_keys(
        (zero_heads, zero_heads),
        (
            lax.all_gather(query_low, "ctx", axis=1, tiled=True),
            lax.all_gather(d_attn_low, "ctx", axis=1, tiled=True),
        ),
        jnp.int32(0),
    )
    d_projected = jnp.concatenate(
        [
            grad_query.reshape(seq_group, seq_dev, width),
            grad_key.reshape(seq_group, seq_dev, width),
            grad_value.reshape(seq_group, seq_dev, width),
        ],
        axis=-1,
    ).astype(jnp.bfloat16)
    grad_w_qkv = jnp.einsum(
        "btd,bte->de", normed_one, d_projected, preferred_element_type=jnp.float32
    )
    column_sums = jnp.sum(d_projected.astype(jnp.float32), axis=(0, 1))
    grad_qv_bias = jnp.stack([column_sums[:width], column_sums[2 * width :]])
    d_normed_one = jnp.einsum(
        "bte,de->btd", d_projected, weights_back[2], preferred_element_type=jnp.float32
    )
    first_unused, first_pull = jax.vjp(layer_norm, tokens_in, back_gain_one, back_shift_one)
    d_input_part, grad_ln1_gain, grad_ln1_bias = first_pull(d_normed_one)
    d_input = d_resid + d_input_part
    shares = (
        lax.psum_scatter(
            grad_ln1_gain.astype(jnp.bfloat16), "wt", scatter_dimension=0, tiled=True
        ).astype(jnp.float32),
        lax.psum_scatter(
            grad_ln1_bias.astype(jnp.bfloat16), "wt", scatter_dimension=0, tiled=True
        ).astype(jnp.float32),
        lax.psum_scatter(
            grad_w_qkv.astype(jnp.bfloat16), "wt", scatter_dimension=0, tiled=True
        ).astype(jnp.float32),
        lax.psum_scatter(
            grad_qv_bias.astype(jnp.bfloat16), "wt", scatter_dimension=1, tiled=True
        ).astype(jnp.float32),
        lax.psum_scatter(
            grad_w_out.astype(jnp.bfloat16), "wt", scatter_dimension=0, tiled=True
        ).astype(jnp.float32),
        lax.psum_scatter(
            grad_out_bias.astype(jnp.bfloat16), "wt", scatter_dimension=0, tiled=True
        ).astype(jnp.float32),
        lax.psum_scatter(
            grad_ln2_gain.astype(jnp.bfloat16), "wt", scatter_dimension=0, tiled=True
        ).astype(jnp.float32),
        lax.psum_scatter(
            grad_ln2_bias.astype(jnp.bfloat16), "wt", scatter_dimension=0, tiled=True
        ).astype(jnp.float32),
        lax.psum_scatter(
            grad_w_fc.astype(jnp.bfloat16), "wt", scatter_dimension=0, tiled=True
        ).astype(jnp.float32),
        lax.psum_scatter(
            grad_fc_bias.astype(jnp.bfloat16), "wt", scatter_dimension=0, tiled=True
        ).astype(jnp.float32),
        lax.psum_scatter(
            grad_w_proj.astype(jnp.bfloat16), "wt", scatter_dimension=0, tiled=True
        ).astype(jnp.float32),
        lax.psum_scatter(
            grad_proj_bias.astype(jnp.bfloat16), "wt", scatter_dimension=0, tiled=True
        ).astype(jnp.float32),
    )
    totals = lax.psum(
        (
            shares[0],
            shares[1],
            shares[2],
            shares[3],
            shares[4],
            shares[5],
            shares[6],
            shares[7],
            shares[8],
            shares[9],
            shares[10],
            shares[11],
        ),
        "ctx",
    )
    return (
        block_out,
        d_input,
        totals[0],
        totals[1],
        totals[2],
        totals[3],
        totals[4],
        totals[5],
        totals[6],
        totals[7],
        totals[8],
        totals[9],
        totals[10],
        totals[11],
    )


def solution(mesh):
    placed = (
        P("wt", "ctx", None),
        P(),
        P("wt", None),
        P("wt"),
        P("wt"),
        P("wt", None),
        P(None, "wt"),
        P("wt", None),
        P("wt"),
        P("wt"),
        P("wt"),
        P("wt", None),
        P("wt"),
        P("wt", None),
        P("wt"),
        P("wt", "ctx", None),
    )
    fast = dict(mesh.shape) == {"ctx": 16, "wt": 2}
    return jax.shard_map(
        by_owner if fast else per_device,
        mesh=mesh,
        in_specs=placed,
        out_specs=(
            P("wt", "ctx", None),
            P("wt", "ctx", None),
            P("wt"),
            P("wt"),
            P("wt", None),
            P(None, "wt"),
            P("wt", None),
            P("wt"),
            P("wt"),
            P("wt"),
            P("wt", None),
            P("wt"),
            P("wt", None),
            P("wt"),
        ),
        check_vma=False,
    )
```

profile of v0, /device:TPU:0, one launch (start us, length us, event | category | flops | bytes accessed | tf_op | source)
XLA Modules:
  0.0 349.1 jit_solution(3852620344605308338)
XLA Ops:
  6.7 4.0 %collective-permute-start.2 = (bf16[72,768]{1,0:T(8,128)(2,1)S(1)}, bf16[72,768]{1,0:T(8,128)(2,1)S(1)}, u32[]{:S(2)}, u32[]{:S(2)}) collective-permute-start(bf16[72,768]{1,0:T(8,128)(2,1)S(1)} %get-tuple-element.395), channel_id=1, source_target_pairs={{0,16},{2,18},{4,20},{6,22},{8,24},{10,26},{12,28},{14,30},{16,0},... | collective-permute-start | bytes 331784 | tf_op jit(solution)/shard_map/ppermute | solution.py:41
  12.8 4.4 %collective-permute-done.2 = bf16[72,768]{1,0:T(8,128)(2,1)S(1)} collective-permute-done((bf16[72,768]{1,0:T(8,128)(2,1)S(1)}, bf16[72,768]{1,0:T(8,128)(2,1)S(1)}, u32[]{:S(2)}, u32[]{:S(2)}) %collective-permute-start.2) | collective-permute-done | bytes 110624 | tf_op jit(solution)/shard_map/ppermute | solution.py:41
  33.1 3.6 %collective-permute-start.14 = (bf16[72,768]{1,0:T(8,128)(2,1)S(1)}, bf16[72,768]{1,0:T(8,128)(2,1)S(1)}, u32[]{:S(2)}, u32[]{:S(2)}) collective-permute-start(bf16[72,768]{1,0:T(8,128)(2,1)S(1)} %get-tuple-element.390), channel_id=1, source_target_pairs={{0,24},{2,26},{4,28},{6,30},{8,0},{10,2},{12,4},{14,6},{16,8},{18,... | collective-permute-start | bytes 331784 | tf_op jit(solution)/shard_map/ppermute | solution.py:41
  42.4 5.8 %collective-permute-done.13 = bf16[72,768]{1,0:T(8,128)(2,1)S(1)} collective-permute-done((bf16[72,768]{1,0:T(8,128)(2,1)S(1)}, bf16[72,768]{1,0:T(8,128)(2,1)S(1)}, u32[]{:S(2)}, u32[]{:S(2)}) %collective-permute-start.13) | collective-permute-done | bytes 110624 | tf_op jit(solution)/shard_map/ppermute | solution.py:41
  53.4 6.6 %project.1 = (bf16[1152,768]{1,0:T(8,128)(2,1)}, bf16[1152,768]{1,0:T(8,128)(2,1)}, bf16[1152,256]{1,0:T(8,128)(2,1)}, bf16[1152,512]{1,0:T(8,128)(2,1)}, bf16[768,768]{1,0:T(8,128)(2,1)}) custom-call(s32[16]{0:T(128)} %compare_select_fusion.6.order_ref, s32[3]{0:T(128)} %pad_add_fusion.3.where_ref, bf16[4,72,768]{2,1,0:T(8,128)(2,1)} %copy-done.23, ...), custom_call_target="tpu_custom_call" | custom-call | flops 6600000000 | bytes 1048576 | tf_op jit(solution)/shard_map/project/pallas_call | solution.py:147
  65.7 15.5 %attend.1 = (f32[1152,256]{1,0:T(8,128)}, f32[9,1,384]{2,1,0:T(1,128)}, bf16[16,72,192]{2,1,0:T(8,128)(2,1)}) custom-call(s32[3,16]{1,0:T(4,128)} %pad_add_fusion.2.plan_ref, bf16[1152,256]{1,0:T(8,128)(2,1)} %get-tuple-element.187.q_ref, bf16[1152,512]{1,0:T(8,128)(2,1)} %get-tuple-element.188.own_ref, bf16[1152,512]{1,0:T(8,128)(2,1)} %copy-done.9, ...), custom_call_target="tpu_custom_call" | custom-call | flops 15000000 | bytes 4096 | tf_op jit(solution)/shard_map/attend/pallas_call | solution.py:436
  81.2 3.7 %all-to-all-start = ((bf16[4,4,72,192]{3,2,1,0:T(8,128)(2,1)}), bf16[4,4,72,192]{3,2,1,0:T(8,128)(2,1)S(1)}, u32[]{:S(2)}, u32[]{:S(2)}) async-start(bf16[4,4,72,192]{3,2,1,0:T(8,128)(2,1)} %bitcast.257), calls=%async_computation | async-start | bytes 1179648 | tf_op jit(solution)/shard_map/all_to_all | solution.py:48
  87.8 3.8 %fusion.89.grad_own_ref = f32[288,1536]{1,0:T(8,128)} fusion(bf16[288,768]{1,0:T(8,128)(2,1)S(1)} %multiply_convert_fusion.d_mlp_ref, bf16[1536,768]{1,0:T(8,128)(2,1)} %param.29), kind=kOutput, calls=%fused_computation.350 | convolution fusion | flops 679477248 | bytes 4571136 | tf_op jit(solution)/shard_map/dot_general | solution.py:80
  94.0 15.2 %middle.1 = (f32[288,768]{1,0:T(8,128)}, bf16[288,768]{1,0:T(8,128)(2,1)}, bf16[288,768]{1,0:T(8,128)(2,1)}, bf16[288,3072]{1,0:T(8,128)(2,1)}, bf16[288,3072]{1...) custom-call(s32[3]{0:T(128)} %pad_add_fusion.3.where_ref, ...), custom_call_target="tpu_custom_call" | custom-call | flops 12000000 | bytes 4096 | tf_op jit(solution)/shard_map/middle/pallas_call | solution.py:257
  114.6 4.4 %all-to-all-start.1 = ((bf16[4,4,72,192]{3,2,1,0:T(8,128)(2,1)}), bf16[4,4,72,192]{3,2,1,0:T(8,128)(2,1)}, u32[]{:S(2)}, u32[]{:S(2)}) async-start(bf16[4,4,72,192]{3,2,1,0:T(8,128)(2,1)} %bitcast.256), calls=%async_computation.1 | async-start | bytes 1179648 | tf_op jit(solution)/shard_map/all_to_all | solution.py:48
  133.0 3.5 %convolution_convert_fusion = bf16[384,3072]{1,0:T(8,128)(2,1)S(1)} fusion(bf16[576,384]{1,0:T(8,128)(2,1)S(1)} %copy-done.25, bf16[288,3072]{1,0:T(8,128)(2,1)} %collective-permute-done.25, bf16[288,3072]{1,0:T(8,128)(2,1)S(1)} %copy-done.43), kind=kOutput, calls=%fused_computation | convolution fusion | flops 1367212032 | bytes 6340608 | tf_op jit(solution)/shard_map/dot_general | solution.py:80
  150.6 22.0 %attend_back.1 = (bf16[1152,256]{1,0:T(8,128)(2,1)}, f32[1152,512]{1,0:T(8,128)}, bf16[1152,512]{1,0:T(8,128)(2,1)}) custom-call(s32[3,16]{1,0:T(4,128)} %pad_add_fusion.2.plan_ref, bf16[1152,256]{1,0:T(8,128)(2,1)} %get-tuple-element.187.q_ref, bf16[1152,512]{1,0:T(8,128)(2,1)} %get-tuple-element.188.own_ref, bf16[1152,512]{1,0:T(8,128)(2,1)} %copy-done.9, ...), custom_call_target="tpu_custom_call" | custom-call | flops 26400000000 | bytes 1048576 | tf_op jit(solution)/shard_map/attend_back/pallas_call | solution.py:526
  172.6 7.5 %collective-permute-done.27 = bf16[384,384]{1,0:T(8,128)(2,1)S(1)} collective-permute-done((bf16[384,384]{1,0:T(8,128)(2,1)S(1)}, bf16[384,384]{1,0:T(8,128)(2,1)S(1)}, u32[]{:S(2)}, u32[]{:S(2)}) %collective-permute-start.27) | collective-permute-done | bytes 294944 | tf_op jit(solution)/shard_map/ppermute | solution.py:37
  185.6 5.1 %collective-permute-done.32 = bf16[192,768]{1,0:T(8,128)(2,1)S(1)} collective-permute-done((bf16[192,768]{1,0:T(8,128)(2,1)S(1)}, bf16[192,768]{1,0:T(8,128)(2,1)S(1)}, u32[]{:S(2)}, u32[]{:S(2)}) %collective-permute-start.32) | collective-permute-done | bytes 294944 | tf_op jit(solution)/shard_map/ppermute | solution.py:37
  196.7 7.7 %unproject.1 = (bf16[16,72,768]{2,1,0:T(8,128)(2,1)}, bf16[1152,640]{1,0:T(8,128)(2,1)}, f32[1,768]{1,0:T(1,128)}, f32[1,768]{1,0:T(1,128)}, f32[1,768]{1,0:T(1,128)}) custom-call(s32[16]{0:T(128)} %get-tuple-element.330.place_ref, bf16[1152,768]{1,0:T(8,128)(2,1)} %get-tuple-element.223.x_ref, bf16[1152,256]{1,0:T(8,128)(2,1)} %get-tuple-element.224.dq_ref, ...), custom_call_target="tpu_custom_call" | custom-call | flops 8800000000 | bytes 1048576 | tf_op jit(solution)/shard_map/unproject/pallas_call | solution.py:603
  206.8 3.9 %collective-permute-done.36 = bf16[24,3840]{1,0:T(8,128)(2,1)S(1)} collective-permute-done((bf16[24,3840]{1,0:T(8,128)(2,1)S(1)}, bf16[24,3840]{1,0:T(8,128)(2,1)S(1)}, u32[]{:S(2)}, u32[]{:S(2)}) %collective-permute-start.36) | collective-permute-done | bytes 184352 | tf_op jit(solution)/shard_map/ppermute | solution.py:41
  215.8 3.7 %convolution_convert_fusion.3 = bf16[384,640]{1,0:T(8,128)(2,1)} fusion(bf16[1152,640]{1,0:T(8,128)(2,1)} %get-tuple-element.246, pred[]{:T(512)S(6)} %eq.161, bf16[1152,768]{1,0:T(8,128)(2,1)} %get-tuple-element.244), kind=kOutput, calls=%fused_computation.17 | convolution fusion | flops 566919168 | bytes 3735553 | tf_op jit(solution)/shard_map/dot_general | solution.py:80
  225.6 3.4 collective-permute-done.39
  233.8 3.9 %collective-permute-start.44 = (bf16[2,96,768]{2,1,0:T(8,128)(2,1)S(1)}, bf16[2,96,768]{2,1,0:T(8,128)(2,1)}, u32[]{:S(2)}, u32[]{:S(2)}) collective-permute-start(bf16[2,96,768]{2,1,0:T(8,128)(2,1)S(1)} %pad_maximum_fusion.25), channel_id=1, source_target_pairs={{0,8},{2,10},{4,12},{6,14},{8,0},{10,2},{12,4},{14,6},{16,24},{18,... | collective-permute-start | bytes 884744 | tf_op jit(solution)/shard_map/ppermute | solution.py:37
  243.3 8.1 %collective-permute-done.44 = bf16[2,96,768]{2,1,0:T(8,128)(2,1)} collective-permute-done((bf16[2,96,768]{2,1,0:T(8,128)(2,1)S(1)}, bf16[2,96,768]{2,1,0:T(8,128)(2,1)}, u32[]{:S(2)}, u32[]{:S(2)}) %collective-permute-start.44) | collective-permute-done | bytes 294944 | tf_op jit(solution)/shard_map/ppermute | solution.py:37
  252.4 5.0 %collective-permute-done.45 = bf16[2,24,3840]{2,1,0:T(8,128)(2,1)} collective-permute-done((bf16[2,24,3840]{2,1,0:T(8,128)(2,1)S(1)}, bf16[2,24,3840]{2,1,0:T(8,128)(2,1)}, u32[]{:S(2)}, u32[]{:S(2)}) %collective-permute-start.45) | collective-permute-done | bytes 368672 | tf_op jit(solution)/shard_map/ppermute | solution.py:37
  263.1 5.5 %collective-permute-done.49 = bf16[4,96,384]{2,1,0:T(8,128)(2,1)S(1)} collective-permute-done((bf16[4,96,384]{2,1,0:T(8,128)(2,1)S(1)}, bf16[4,96,384]{2,1,0:T(8,128)(2,1)S(1)}, u32[]{:S(2)}, u32[]{:S(2)}) %collective-permute-start.49) | collective-permute-done | bytes 294944 | tf_op jit(solution)/shard_map/ppermute | solution.py:37
  270.1 3.6 %collective-permute-done.51 = bf16[4,24,1920]{2,1,0:T(8,128)(2,1)S(1)} collective-permute-done((bf16[4,24,1920]{2,1,0:T(8,128)(2,1)S(1)}, bf16[4,24,1920]{2,1,0:T(8,128)(2,1)S(1)}, u32[]{:S(2)}, u32[]{:S(2)}) %collective-permute-start.51) | collective-permute-done | bytes 368672 | tf_op jit(solution)/shard_map/ppermute | solution.py:37
  280.1 3.5 %collective-permute-done.55 = bf16[104,640]{1,0:T(8,128)(2,1)S(1)} collective-permute-done((bf16[104,640]{1,0:T(8,128)(2,1)S(1)}, bf16[104,640]{1,0:T(8,128)(2,1)S(1)}, u32[]{:S(2)}, u32[]{:S(2)}) %collective-permute-start.55) | collective-permute-done | bytes 133152 | tf_op jit(solution)/shard_map/ppermute | solution.py:37
  283.6 4.6 %collective-permute-done.53.refs_1_ = bf16[8,96,384]{2,1,0:T(8,128)(2,1)S(1)} collective-permute-done((bf16[8,96,384]{2,1,0:T(8,128)(2,1)S(1)}, bf16[8,96,384]{2,1,0:T(8,128)(2,1)S(1)}, u32[]{:S(2)}, u32[]{:S(2)}) %collective-permute-start.53) | collective-permute-done | bytes 589856 | tf_op jit(solution)/shard_map/ppermute | solution.py:37
  290.6 3.5 %fusion.90 = f32[288,768]{1,0:T(8,128)} fusion(bf16[288,1536]{1,0:T(8,128)(2,1)S(1)} %copy-done.14, bf16[1536,768]{1,0:T(8,128)(2,1)} %collective-permute-done.17.proj_oth_ref), kind=kOutput, calls=%fused_computation.351 | convolution fusion | flops 679477248 | bytes 4128768 | tf_op jit(solution)/shard_map/dot_general | solution.py:80
  303.3 3.5 %collective-permute-done.59 = bf16[2,72,768]{2,1,0:T(8,128)(2,1)S(1)} collective-permute-done((bf16[2,72,768]{2,1,0:T(8,128)(2,1)S(1)}, bf16[2,72,768]{2,1,0:T(8,128)(2,1)S(1)}, u32[]{:S(2)}, u32[]{:S(2)}) %collective-permute-start.59) | collective-permute-done | bytes 221216 | tf_op jit(solution)/shard_map/ppermute | solution.py:37
  309.1 3.5 %collective-permute-start.62 = (bf16[2,72,768]{2,1,0:T(8,128)(2,1)S(1)}, bf16[2,72,768]{2,1,0:T(8,128)(2,1)S(1)}, u32[]{:S(2)}, u32[]{:S(2)}) collective-permute-start(bf16[2,72,768]{2,1,0:T(8,128)(2,1)S(1)} %get-tuple-element.372), channel_id=1, source_target_pairs={{0,16},{2,18},{4,20},{6,22},{8,24},{10,26},{12,28},{14,30},{16,0},... | collective-permute-start | bytes 663560 | tf_op jit(solution)/shard_map/ppermute | solution.py:37
  316.0 6.9 %collective-permute-done.62 = bf16[2,72,768]{2,1,0:T(8,128)(2,1)S(1)} collective-permute-done((bf16[2,72,768]{2,1,0:T(8,128)(2,1)S(1)}, bf16[2,72,768]{2,1,0:T(8,128)(2,1)S(1)}, u32[]{:S(2)}, u32[]{:S(2)}) %collective-permute-start.62) | collective-permute-done | bytes 221216 | tf_op jit(solution)/shard_map/ppermute | solution.py:37
  326.8 4.1 %place_proj.1 = f32[1536,768]{1,0:T(8,128)} custom-call(s32[3]{0:T(128)} %pad_add_fusion.3.where_ref, bf16[8,96,384]{2,1,0:T(8,128)(2,1)} %copy-done.18, bf16[8,96,384]{2,1,0:T(8,128)(2,1)} %copy-done.48, bf16[8,96,384]{2,1,0:T(8,128)(2,1)} %copy-done.17, bf16[8,96,384]{2,1,0:T(8,128)(2,1)} %copy-done.49), custom_call_target="tpu_custom_call" | custom-call | flops 5500000256 | bytes 1048576 | tf_op jit(solution)/shard_map/place_proj/pallas_call | solution.py:726
  330.9 4.7 %place_rest.1 = (f32[384,3072]{1,0:T(8,128)}, f32[384,768]{1,0:T(8,128)}) custom-call(s32[3]{0:T(128)} %pad_add_fusion.3.where_ref, bf16[8,24,1920]{2,1,0:T(8,128)(2,1)} %pad_maximum_fusion.4.refs_0_, bf16[8,24,1920]{2,1,0:T(8,128)(2,1)} %copy-done.46, bf16[8,24,1920]{2,1,0:T(8,128)(2,1)} %pad_maximum_fusion.5.refs_2_, bf16[8,24,1920]{2,1,0:T(8,128)(2,1)} %copy-done.47), custom_call_target="tpu_custom_call" | custom-call | flops 5500000256 | bytes 1048576 | tf_op jit(solution)/shard_map/place_rest/pallas_call | solution.py:726
  342.1 4.3 %place_in.1 = (f32[384,2304]{1,0:T(8,128)}, f32[4,8,640]{2,1,0:T(8,128)}) custom-call(s32[3]{0:T(128)} %pad_add_fusion.3.where_ref, bf16[8,56,640]{2,1,0:T(8,128)(2,1)} %copy-done.19, bf16[8,56,640]{2,1,0:T(8,128)(2,1)} %copy-done.50, bf16[8,48,640]{2,1,0:T(8,128)(2,1)} %copy-done.20, bf16[8,48,640]{2,1,0:T(8,128)(2,1)} %copy-done.51), custom_call_target="tpu_custom_call" | custom-call | flops 4400000000 | bytes 1048576 | tf_op jit(solution)/shard_map/place_in/pallas_call | solution.py:726
  (389 shorter events, 156.6 us)
Async XLA Ops:
  28.2 21.3 %collective-permute-start.8 = (bf16[4,72,768]{2,1,0:T(8,128)(2,1)S(1)}, bf16[4,72,768]{2,1,0:T(8,128)(2,1)S(1)}, u32[]{:S(2)}, u32[]{:S(2)}) collective-permute-start(bf16[4,72,768]{2,1,0:T(8,128)(2,1)S(1)} %pad_maximum_fusion.15.c_ref), channel_id=1, source_target_pairs={{0,2},{2,0},{4,6},{6,4},{8,10},{10,8},{12,14},{14,12},{16,18},{18,... | collective-permute-start | bytes 1327112 | tf_op jit(solution)/shard_map/ppermute | solution.py:37
  29.7 19.8 %collective-permute-start.7 = (bf16[4,72,768]{2,1,0:T(8,128)(2,1)S(1)}, bf16[4,72,768]{2,1,0:T(8,128)(2,1)S(1)}, u32[]{:S(2)}, u32[]{:S(2)}) collective-permute-start(bf16[4,72,768]{2,1,0:T(8,128)(2,1)S(1)} %pad_maximum_fusion.13.a_ref), channel_id=1, source_target_pairs={{0,4},{2,6},{4,0},{6,2},{8,12},{10,14},{12,8},{14,10},{16,20},{18,... | collective-permute-start | bytes 1327112 | tf_op jit(solution)/shard_map/ppermute | solution.py:37
  31.8 19.3 %collective-permute-start.9 = (bf16[384,1152]{1,0:T(8,128)(2,1)S(1)}, bf16[384,1152]{1,0:T(8,128)(2,1)}, u32[]{:S(2)}, u32[]{:S(2)}) collective-permute-start(bf16[384,1152]{1,0:T(8,128)(2,1)S(1)} %pad_maximum_fusion.2.own_ref), channel_id=1, source_target_pairs={{0,1},{1,0},{2,3},{3,2},{4,5},{5,4},{6,7},{7,6},{8,9},{9,8},{10,11... | collective-permute-start | bytes 2654216 | tf_op jit(solution)/shard_map/ppermute | solution.py:33
  114.6 16.2 %all-to-all-start.1 = ((bf16[4,4,72,192]{3,2,1,0:T(8,128)(2,1)}), bf16[4,4,72,192]{3,2,1,0:T(8,128)(2,1)}, u32[]{:S(2)}, u32[]{:S(2)}) async-start(bf16[4,4,72,192]{3,2,1,0:T(8,128)(2,1)} %bitcast.256), calls=%async_computation.1 | async-start | bytes 1179648 | tf_op jit(solution)/shard_map/all_to_all | solution.py:48
  119.1 13.9 %collective-permute-start.25 = (bf16[288,3072]{1,0:T(8,128)(2,1)}, bf16[288,3072]{1,0:T(8,128)(2,1)}, u32[]{:S(2)}, u32[]{:S(2)}) collective-permute-start(bf16[288,3072]{1,0:T(8,128)(2,1)} %get-tuple-element.202), channel_id=1, source_target_pairs={{0,1},{1,0},{2,3},{3,2},{4,5},{5,4},{6,7},{7,6},{8,9},{9,8},{10,11... | collective-permute-start | bytes 5308424 | tf_op jit(solution)/shard_map/ppermute | solution.py:33
  126.8 16.4 %collective-permute-start.22 = (bf16[768,384]{1,0:T(8,128)(2,1)S(1)}, bf16[768,384]{1,0:T(8,128)(2,1)}, u32[]{:S(2)}, u32[]{:S(2)}) collective-permute-start(bf16[768,384]{1,0:T(8,128)(2,1)S(1)} %dynamic-slice_bitcast_fusion.3), channel_id=1, source_target_pairs={{0,4},{2,6},{4,0},{6,2},{8,12},{10,14},{12,8},{14,10},{16,20},{18,... | collective-permute-start | bytes 1769480 | tf_op jit(solution)/shard_map/ppermute | solution.py:37
  129.4 16.5 %collective-permute-start.21 = (bf16[768,384]{1,0:T(8,128)(2,1)}, bf16[768,384]{1,0:T(8,128)(2,1)}, u32[]{:S(2)}, u32[]{:S(2)}) collective-permute-start(bf16[768,384]{1,0:T(8,128)(2,1)} %dynamic-slice_bitcast_fusion.4), channel_id=1, source_target_pairs={{0,2},{2,0},{4,6},{6,4},{8,10},{10,8},{12,14},{14,12},{16,18},{18,... | collective-permute-start | bytes 1769480 | tf_op jit(solution)/shard_map/ppermute | solution.py:37
  138.0 44.6 %collective-permute-start.31 = (bf16[96,3840]{1,0:T(8,128)(2,1)}, bf16[96,3840]{1,0:T(8,128)(2,1)S(1)}, u32[]{:S(2)}, u32[]{:S(2)}) collective-permute-start(bf16[96,3840]{1,0:T(8,128)(2,1)} %get-tuple-element.333), channel_id=1, source_target_pairs={{0,6},{2,4},{4,2},{6,0},{8,14},{10,12},{12,10},{14,8},{16,22},{18,... | collective-permute-start | bytes 2211848 | tf_op jit(solution)/shard_map/ppermute | solution.py:37
  138.3 44.2 %collective-permute-start.30 = (bf16[96,3840]{1,0:T(8,128)(2,1)}, bf16[96,3840]{1,0:T(8,128)(2,1)}, u32[]{:S(2)}, u32[]{:S(2)}) collective-permute-start(bf16[96,3840]{1,0:T(8,128)(2,1)} %get-tuple-element.334), channel_id=1, source_target_pairs={{0,4},{2,6},{4,0},{6,2},{8,12},{10,14},{12,8},{14,10},{16,20},{18,... | collective-permute-start | bytes 2211848 | tf_op jit(solution)/shard_map/ppermute | solution.py:37
  140.0 42.5 %collective-permute-start.29 = (bf16[96,3840]{1,0:T(8,128)(2,1)S(1)}, bf16[96,3840]{1,0:T(8,128)(2,1)}, u32[]{:S(2)}, u32[]{:S(2)}) collective-permute-start(bf16[96,3840]{1,0:T(8,128)(2,1)S(1)} %get-tuple-element.335), channel_id=1, source_target_pairs={{0,2},{2,0},{4,6},{6,4},{8,10},{10,8},{12,14},{14,12},{16,18},{18,... | collective-permute-start | bytes 2211848 | tf_op jit(solution)/shard_map/ppermute | solution.py:37
  148.5 31.6 %collective-permute-start.27 = (bf16[384,384]{1,0:T(8,128)(2,1)S(1)}, bf16[384,384]{1,0:T(8,128)(2,1)S(1)}, u32[]{:S(2)}, u32[]{:S(2)}) collective-permute-start(bf16[384,384]{1,0:T(8,128)(2,1)S(1)} %dynamic-slice_bitcast_fusion.7), channel_id=1, source_target_pairs={{0,4},{2,6},{4,0},{6,2},{8,12},{10,14},{12,8},{14,10},{16,20},{18,... | collective-permute-start | bytes 884744 | tf_op jit(solution)/shard_map/ppermute | solution.py:37
  148.9 33.7 %collective-permute-start.28 = (bf16[384,384]{1,0:T(8,128)(2,1)S(1)}, bf16[384,384]{1,0:T(8,128)(2,1)S(1)}, u32[]{:S(2)}, u32[]{:S(2)}) collective-permute-start(bf16[384,384]{1,0:T(8,128)(2,1)S(1)} %dynamic-slice_bitcast_fusion.6), channel_id=1, source_target_pairs={{0,2},{2,0},{4,6},{6,4},{8,10},{10,8},{12,14},{14,12},{16,18},{18,... | collective-permute-start | bytes 884744 | tf_op jit(solution)/shard_map/ppermute | solution.py:37
  190.8 16.0 %collective-permute-start.34 = (bf16[96,768]{1,0:T(8,128)(2,1)S(1)}, bf16[96,768]{1,0:T(8,128)(2,1)S(1)}, u32[]{:S(2)}, u32[]{:S(2)}) collective-permute-start(bf16[96,768]{1,0:T(8,128)(2,1)S(1)} %dynamic-slice_bitcast_fusion.12), channel_id=1, source_target_pairs={{0,16},{2,18},{4,20},{6,22},{8,24},{10,26},{12,28},{14,30},{16,0},... | collective-permute-start | bytes 442376 | tf_op jit(solution)/shard_map/ppermute | solution.py:37
  192.1 14.7 %collective-permute-start.35 = (bf16[24,3840]{1,0:T(8,128)(2,1)S(1)}, bf16[24,3840]{1,0:T(8,128)(2,1)S(1)}, u32[]{:S(2)}, u32[]{:S(2)}) collective-permute-start(bf16[24,3840]{1,0:T(8,128)(2,1)S(1)} %get-tuple-element.220), channel_id=1, source_target_pairs={{0,8},{2,10},{4,12},{6,14},{8,16},{10,18},{12,20},{14,22},{16,24},... | collective-permute-start | bytes 552968 | tf_op jit(solution)/shard_map/ppermute | solution.py:41
  192.4 18.4 %collective-permute-start.36 = (bf16[24,3840]{1,0:T(8,128)(2,1)S(1)}, bf16[24,3840]{1,0:T(8,128)(2,1)S(1)}, u32[]{:S(2)}, u32[]{:S(2)}) collective-permute-start(bf16[24,3840]{1,0:T(8,128)(2,1)S(1)} %get-tuple-element.221), channel_id=1, source_target_pairs={{0,16},{2,18},{4,20},{6,22},{8,24},{10,26},{12,28},{14,30},{16,0},... | collective-permute-start | bytes 552968 | tf_op jit(solution)/shard_map/ppermute | solution.py:41
  194.0 16.7 %collective-permute-start.37 = (bf16[24,3840]{1,0:T(8,128)(2,1)S(1)}, bf16[24,3840]{1,0:T(8,128)(2,1)S(1)}, u32[]{:S(2)}, u32[]{:S(2)}) collective-permute-start(bf16[24,3840]{1,0:T(8,128)(2,1)S(1)} %get-tuple-element.222), channel_id=1, source_target_pairs={{0,24},{2,26},{4,28},{6,30},{8,0},{10,2},{12,4},{14,6},{16,8},{18,... | collective-permute-start | bytes 552968 | tf_op jit(solution)/shard_map/ppermute | solution.py:41
  210.8 14.8 %collective-permute-start.38 = (bf16[96,768]{1,0:T(8,128)(2,1)S(1)}, bf16[96,768]{1,0:T(8,128)(2,1)S(1)}, u32[]{:S(2)}, u32[]{:S(2)}) collective-permute-start(bf16[96,768]{1,0:T(8,128)(2,1)S(1)} %fusion.41), channel_id=1, source_target_pairs={{0,16},{2,18},{4,20},{6,22},{8,24},{10,26},{12,28},{14,30},{16,0},... | collective-permute-start | bytes 442376 | tf_op jit(solution)/shard_map/ppermute | solution.py:37
  214.2 14.8 %collective-permute-start.39 = (bf16[24,3840]{1,0:T(8,128)(2,1)S(1)}, bf16[24,3840]{1,0:T(8,128)(2,1)S(1)}, u32[]{:S(2)}, u32[]{:S(2)}) collective-permute-start(bf16[24,3840]{1,0:T(8,128)(2,1)S(1)} %fusion.40), channel_id=1, source_target_pairs={{0,16},{2,18},{4,20},{6,22},{8,24},{10,26},{12,28},{14,30},{16,0},... | collective-permute-start | bytes 552968 | tf_op jit(solution)/shard_map/ppermute | solution.py:37
  221.1 12.4 %collective-permute-start.41 = (bf16[4,72,768]{2,1,0:T(8,128)(2,1)}, bf16[4,72,768]{2,1,0:T(8,128)(2,1)}, u32[]{:S(2)}, u32[]{:S(2)}) collective-permute-start(bf16[4,72,768]{2,1,0:T(8,128)(2,1)} %get-tuple-element.339), channel_id=1, source_target_pairs={{0,4},{2,6},{4,0},{6,2},{8,12},{10,14},{12,8},{14,10},{16,20},{18,... | collective-permute-start | bytes 1327112 | tf_op jit(solution)/shard_map/ppermute | solution.py:37
  233.8 17.6 %collective-permute-start.44 = (bf16[2,96,768]{2,1,0:T(8,128)(2,1)S(1)}, bf16[2,96,768]{2,1,0:T(8,128)(2,1)}, u32[]{:S(2)}, u32[]{:S(2)}) collective-permute-start(bf16[2,96,768]{2,1,0:T(8,128)(2,1)S(1)} %pad_maximum_fusion.25), channel_id=1, source_target_pairs={{0,8},{2,10},{4,12},{6,14},{8,0},{10,2},{12,4},{14,6},{16,24},{18,... | collective-permute-start | bytes 884744 | tf_op jit(solution)/shard_map/ppermute | solution.py:37
  237.7 19.8 %collective-permute-start.45 = (bf16[2,24,3840]{2,1,0:T(8,128)(2,1)S(1)}, bf16[2,24,3840]{2,1,0:T(8,128)(2,1)}, u32[]{:S(2)}, u32[]{:S(2)}) collective-permute-start(bf16[2,24,3840]{2,1,0:T(8,128)(2,1)S(1)} %pad_maximum_fusion.24), channel_id=1, source_target_pairs={{0,8},{2,10},{4,12},{6,14},{8,0},{10,2},{12,4},{14,6},{16,24},{18,... | collective-permute-start | bytes 1105928 | tf_op jit(solution)/shard_map/ppermute | solution.py:37
  239.9 18.6 %collective-permute-start.46 = (bf16[208,640]{1,0:T(8,128)(2,1)}, bf16[208,640]{1,0:T(8,128)(2,1)S(1)}, u32[]{:S(2)}, u32[]{:S(2)}) collective-permute-start(bf16[208,640]{1,0:T(8,128)(2,1)} %dynamic-slice_bitcast_fusion.8), channel_id=1, source_target_pairs={{0,16},{2,18},{4,20},{6,22},{8,24},{10,26},{12,28},{14,30},{16,0},... | collective-permute-start | bytes 798728 | tf_op jit(solution)/shard_map/ppermute | solution.py:37
  241.0 17.6 %collective-permute-start.47 = (bf16[4,72,768]{2,1,0:T(8,128)(2,1)}, bf16[4,72,768]{2,1,0:T(8,128)(2,1)S(1)}, u32[]{:S(2)}, u32[]{:S(2)}) collective-permute-start(bf16[4,72,768]{2,1,0:T(8,128)(2,1)} %get-tuple-element.260), channel_id=1, source_target_pairs={{0,6},{2,4},{4,2},{6,0},{8,14},{10,12},{12,10},{14,8},{16,22},{18,... | collective-permute-start | bytes 1327112 | tf_op jit(solution)/shard_map/ppermute | solution.py:37
  262.4 13.4 %collective-permute-start.52 = (bf16[104,640]{1,0:T(8,128)(2,1)S(1)}, bf16[104,640]{1,0:T(8,128)(2,1)S(1)}, u32[]{:S(2)}, u32[]{:S(2)}) collective-permute-start(bf16[104,640]{1,0:T(8,128)(2,1)S(1)} %dynamic-slice_bitcast_fusion.13), channel_id=1, source_target_pairs={{0,8},{2,10},{4,12},{6,14},{8,0},{10,2},{12,4},{14,6},{16,24},{18,... | collective-permute-start | bytes 399368 | tf_op jit(solution)/shard_map/ppermute | solution.py:37
  262.5 12.4 %collective-permute-start.50 = (bf16[4,24,1920]{2,1,0:T(8,128)(2,1)S(1)}, bf16[4,24,1920]{2,1,0:T(8,128)(2,1)S(1)}, u32[]{:S(2)}, u32[]{:S(2)}) collective-permute-start(bf16[4,24,1920]{2,1,0:T(8,128)(2,1)S(1)} %get-tuple-element.347), channel_id=1, source_target_pairs={{0,2},{2,0},{4,6},{6,4},{8,10},{10,8},{12,14},{14,12},{16,18},{18,... | collective-permute-start | bytes 1105928 | tf_op jit(solution)/shard_map/ppermute | solution.py:37
  275.8 12.4 %collective-permute-start.53 = (bf16[8,96,384]{2,1,0:T(8,128)(2,1)S(1)}, bf16[8,96,384]{2,1,0:T(8,128)(2,1)S(1)}, u32[]{:S(2)}, u32[]{:S(2)}) collective-permute-start(bf16[8,96,384]{2,1,0:T(8,128)(2,1)S(1)} %pad_maximum_fusion.8.refs_0_), channel_id=1, source_target_pairs={{0,4},{2,6},{4,0},{6,2},{8,12},{10,14},{12,8},{14,10},{16,20},{18,... | collective-permute-start | bytes 1769480 | tf_op jit(solution)/shard_map/ppermute | solution.py:37
  289.2 13.1 %collective-permute-start.58 = (bf16[2,104,640]{2,1,0:T(8,128)(2,1)S(1)}, bf16[2,104,640]{2,1,0:T(8,128)(2,1)}, u32[]{:S(2)}, u32[]{:S(2)}) collective-permute-start(bf16[2,104,640]{2,1,0:T(8,128)(2,1)S(1)} %pad_maximum_fusion.26), channel_id=1, source_target_pairs={{0,16},{2,18},{4,20},{6,22},{8,24},{10,26},{12,28},{14,30},{16,0},... | collective-permute-start | bytes 798728 | tf_op jit(solution)/shard_map/ppermute | solution.py:37
  294.2 14.5 %collective-permute-start.56 = (bf16[8,24,1920]{2,1,0:T(8,128)(2,1)}, bf16[8,24,1920]{2,1,0:T(8,128)(2,1)S(1)}, u32[]{:S(2)}, u32[]{:S(2)}) collective-permute-start(bf16[8,24,1920]{2,1,0:T(8,128)(2,1)} %pad_maximum_fusion.4.refs_0_), channel_id=1, source_target_pairs={{0,4},{2,6},{4,0},{6,2},{8,12},{10,14},{12,8},{14,10},{16,20},{18,... | collective-permute-start | bytes 2211848 | tf_op jit(solution)/shard_map/ppermute | solution.py:37
  294.9 14.0 %collective-permute-start.57 = (bf16[8,24,1920]{2,1,0:T(8,128)(2,1)}, bf16[8,24,1920]{2,1,0:T(8,128)(2,1)S(1)}, u32[]{:S(2)}, u32[]{:S(2)}) collective-permute-start(bf16[8,24,1920]{2,1,0:T(8,128)(2,1)} %pad_maximum_fusion.5.refs_2_), channel_id=1, source_target_pairs={{0,2},{2,0},{4,6},{6,4},{8,10},{10,8},{12,14},{14,12},{16,18},{18,... | collective-permute-start | bytes 2211848 | tf_op jit(solution)/shard_map/ppermute | solution.py:37
  309.1 13.8 %collective-permute-start.62 = (bf16[2,72,768]{2,1,0:T(8,128)(2,1)S(1)}, bf16[2,72,768]{2,1,0:T(8,128)(2,1)S(1)}, u32[]{:S(2)}, u32[]{:S(2)}) collective-permute-start(bf16[2,72,768]{2,1,0:T(8,128)(2,1)S(1)} %get-tuple-element.372), channel_id=1, source_target_pairs={{0,16},{2,18},{4,20},{6,22},{8,24},{10,26},{12,28},{14,30},{16,0},... | collective-permute-start | bytes 663560 | tf_op jit(solution)/shard_map/ppermute | solution.py:37
  326.0 13.6 %collective-permute-start.68 = (bf16[8,48,640]{2,1,0:T(8,128)(2,1)S(1)}, bf16[8,48,640]{2,1,0:T(8,128)(2,1)S(1)}, u32[]{:S(2)}, u32[]{:S(2)}) collective-permute-start(bf16[8,48,640]{2,1,0:T(8,128)(2,1)S(1)} %pad_maximum_fusion.12.refs_2_), channel_id=1, source_target_pairs={{0,2},{2,0},{4,6},{6,4},{8,10},{10,8},{12,14},{14,12},{16,18},{18,... | collective-permute-start | bytes 1474568 | tf_op jit(solution)/shard_map/ppermute | solution.py:37
  326.2 15.2 %collective-permute-start.67 = (bf16[8,56,640]{2,1,0:T(8,128)(2,1)S(1)}, bf16[8,56,640]{2,1,0:T(8,128)(2,1)S(1)}, u32[]{:S(2)}, u32[]{:S(2)}) collective-permute-start(bf16[8,56,640]{2,1,0:T(8,128)(2,1)S(1)} %pad_maximum_fusion.10.refs_0_), channel_id=1, source_target_pairs={{0,4},{2,6},{4,0},{6,2},{8,12},{10,14},{12,8},{14,10},{16,20},{18,... | collective-permute-start | bytes 1720328 | tf_op jit(solution)/shard_map/ppermute | solution.py:37
  (93 other events, 703.9 us)
where the time goes:
time: 351 us; the launch traced here: 349 us
  waiting for transfers between devices  104 us (30%)
  starting transfers between devices  83.1 us (24%)
  Pallas kernels  81.6 us (23%)
  other arithmetic  30.5 us (9%)
  matrix products  25.5 us (7%)
  local copies, waits for them, and re-layouts  20.3 us (6%)
  between operations  3.92 us (1%)
    ppermute x40, waiting for transfers between devices, send_flip(): return lax.ppermute(value, 'ctx', flips[flip])  81.5 us
    ppermute x40, starting transfers between devices, send_flip(): return lax.ppermute(value, 'ctx', flips[flip])  49 us
    dot_general x8, matrix products, dot(): lax.dot_general(left, right, (dims, ((), ())), preferred_element_type=f32)  25.5 us
    pallas_call x1, Pallas kernels, attend_back(): pl.pallas_call(attend_back_kernel, in_specs=[pl.BlockSpec(memory_space=pl...  22 us
    ppermute x9, starting transfers between devices, send_z(): return lax.ppermute(value, 'ctx', z_shift(step))  17.7 us
    ppermute x9, waiting for transfers between devices, send_z(): return lax.ppermute(value, 'ctx', z_shift(step))  16.9 us
    pallas_call x1, Pallas kernels, attend(): pl.pallas_call(attend_kernel, in_specs=[pl.BlockSpec(memory_space=pltpu.S...  15.5 us
    pallas_call x1, Pallas kernels, middle(): pl.pallas_call(middle_kernel, in_specs=[pl.BlockSpec(memory_space=pltpu.S...  15.2 us
  transfers between devices with their start and end apart: 71, of which 38 were waited for; matrix products, arithmetic and copies ran while one was open for 17% of the time, Pallas kernels for 13%

commit v1 on v0

--- a/solution.py
+++ b/solution.py
@@ -166,7 +166,7 @@
 def middle_kernel(
     where_ref, attn_ref, x_ref, cot_ref, d_mlp_ref, grad_own_ref, proj_oth_ref, out_own_ref, out_oth_ref, fc_own_ref, fc_oth_ref,
     small_own_ref, small_oth_ref,
-    resid_ref, attn_low_ref, normed_ref, hidden_ref, pre_ref, d_resid_ref, d_branch_ref, send_ref,
+    resid_ref, attn_own_ref, attn_oth_ref, normed_own_ref, normed_oth_ref, hidden_own_ref, hidden_oth_ref, pre_ref, d_resid_ref, d_branch_ref, send_ref,
     branch_sum_ref, gain_sum_ref, shift_sum_ref, mlp_sum_ref, pre_sum_ref,
     back, bias_fc, w_out_ref, w_fc_ref,
 ):
@@ -186,18 +186,21 @@
             core == 0, small_oth_ref[8 + i : 9 + i], small_own_ref[8 + i : 9 + i]
         )
     attn = jnp.concatenate([attn_ref[g].astype(f32) for g in range(GROUPS)], axis=1).astype(bf16)
-    attn_low_ref[...] = attn
+    half = small_own_ref.shape[1]
+    attn_own_ref[...] = jnp.where(core == 0, attn[:, :half], attn[:, half:])
+    attn_oth_ref[...] = jnp.where(core == 0, attn[:, half:], attn[:, :half])
     cot = cot_ref[...].astype(f32)
     branch = dot(attn, w_out_ref[...], ((1,), (0,))) + small[4:5]
     resid = x_ref[...].astype(f32) + branch_scale * branch
     resid_ref[...] = resid
     unit, inverse = norm_parts(resid)
     low = (unit * gain + small[6:7]).astype(bf16)
-    normed_ref[...] = low
+    normed_own_ref[...] = jnp.where(core == 0, low[:, :half], low[:, half:])
+    normed_oth_ref[...] = jnp.where(core == 0, low[:, half:], low[:, :half])
     back[...] = jnp.zeros_like(back)
     wide = 512
 
-    def columns(hidden_grad, first, t, carry):
+    def columns(hidden_grad, hidden_ref, first, t, carry):
         here = pl.ds(pl.multiple_of(t * wide, wide), wide)
         at = pl.ds(pl.multiple_of(first + t * wide, wide), wide)
         weight = w_fc_ref[:, at]
@@ -205,7 +208,7 @@
         square = u * u
         th = jnp.tanh(0.7978845608028654 * (u + 0.044715 * (square * u)))
         one = 0.5 * (1.0 + th)
-        hidden_ref[:, at] = (u * one).astype(bf16)
+        hidden_ref[:, here] = (u * one).astype(bf16)
         slope = one + 0.5 * u * (1.0 - th * th) * (0.7978845608028654 * (1.0 + 0.134145 * square))
         pre = (hidden_grad(here) * slope).astype(bf16)
         pre_ref[:, at] = pre
@@ -215,13 +218,14 @@
 
     span = grad_own_ref.shape[1]
     lax.fori_loop(
-        0, span // wide, functools.partial(columns, lambda here: grad_own_ref[:, here], core * span), 0
+        0, span // wide, functools.partial(columns, lambda here: grad_own_ref[:, here], hidden_own_ref, core * span), 0
     )
     lax.fori_loop(
         0, span // wide,
         functools.partial(
             columns,
             lambda here: dot(d_mlp_ref[...], proj_oth_ref[here, :], ((1,), (1,))),
+            hidden_oth_ref,
             (1 - core) * span,
         ),
         0,
@@ -250,7 +254,9 @@
     groups, rows, feats = attn.shape
     width, wide = out_own.shape[1], fc_own.shape[1]
     shapes = [
-        ((rows, width), f32), ((rows, width), bf16), ((rows, width), bf16), ((rows, wide), bf16),
+        ((rows, width), f32), ((rows, width // 2), bf16), ((rows, width // 2), bf16),
+        ((rows, width // 2), bf16), ((rows, width // 2), bf16), ((rows, wide // 2), bf16),
+        ((rows, wide // 2), bf16),
         ((rows, wide), bf16), ((rows, width), f32), ((rows, width), bf16), (attn.shape, bf16),
         ((1, width), f32), ((1, width), f32), ((1, width), f32), ((1, width), f32), ((1, wide), f32),
     ]
@@ -812,7 +818,9 @@
     kept = to_sequence(take_spans(block_input))
     left, right = jnp.stack(kept[:2]), jnp.stack(kept[2:])
     tokens_low = jnp.concatenate([left, right], axis=0)
-    span_order, doc_lengths, unused = lax.optimization_barrier((span_order, doc_lengths, (left, right)))
+    span_order, doc_lengths, d_out, unused = lax.optimization_barrier(
+        (span_order, doc_lengths, d_out, (left, right))
+    )
     left_x, right_y = send_flip(left, 1), send_flip(right, 2)
     ranks = jnp.arange(rows, dtype=jnp.int32)
     even_pos = 2 * span_rows * (ranks // span_rows) + ranks % span_rows
@@ -824,10 +832,10 @@
     right = jnp.concatenate([right, right_y], axis=0)
     pieces = (left, send_flip(left, 2), right, send_flip(right, 1))
     (
-        ln1_gain, ln1_bias, w_qkv, qv_bias, d_out, out_bias, ln2_gain, ln2_bias, proj_bias, fc_bias, unused,
+        ln1_gain, ln1_bias, w_qkv, qv_bias, out_bias, ln2_gain, ln2_bias, proj_bias, fc_bias, unused,
     ) = lax.optimization_barrier(
         (
-            ln1_gain, ln1_bias, w_qkv, qv_bias, d_out, out_bias, ln2_gain, ln2_bias, proj_bias, fc_bias,
+            ln1_gain, ln1_bias, w_qkv, qv_bias, out_bias, ln2_gain, ln2_bias, proj_bias, fc_bias,
             (left, right),
         )
     )
@@ -920,18 +928,15 @@
 
     tokens = tokens_low.reshape(seqs * span_rows, width)
     (
-        resid, attn_low, normed_two, hidden_low, d_pre, d_resid, d_branch, d_send, *sums
+        resid, attn_own, attn_oth, normed_own, normed_oth, hidden_own, hidden_oth, d_pre, d_resid, d_branch, d_send, *sums
     ) = middle(
         attn_got, tokens, cot_low, d_mlp, grad_own, proj_oth,
         w_out, out_oth, w_fc, fc_oth, here, small, small_oth,
     )
     d_got = swap_plane(d_send.reshape(GROUPS, seqs, span_rows, feats)).reshape(chips, span_rows, feats)
-    hidden_own, hidden_oth = split_halves(hidden_low, w, 1)
     hidden_both = jnp.concatenate([hidden_own, other_core(hidden_oth)], axis=0)
     pre_both = jnp.concatenate([d_pre, other_core(d_pre)], axis=0)
-    normed_own, normed_oth = split_halves(normed_two, w, 1)
     normed_both = jnp.concatenate([normed_own, other_core(normed_oth)], axis=0)
-    attn_own, attn_oth = split_halves(attn_low, w, 1)
     attn_both = jnp.concatenate([attn_own, other_core(attn_oth)], axis=0)
     low_bit, high_bit = z % 2, z // 2
     branch_both = jnp.concatenate([d_branch, other_core(d_branch)], axis=0)
@@ -957,8 +962,12 @@
 
     d_got = after(d_got, left_send, right_send, *rest_sends)
     d_query, d_own, d_oth = attend_back(plan, query, kv_own, kv_oth, kpos, meta, d_got, attn, lse)
-    left_recv, right_recv, rest_plane, d_query, d_oth = lax.optimization_barrier(
-        (left_recv, right_recv, rest_plane, d_query, d_oth)
+    hidden_own, hidden_oth, unused = lax.optimization_barrier((hidden_own, hidden_oth, d_query))
+    mlp = dot(hidden_own, w_proj, ((1,), (0,))) + dot(hidden_oth, proj_oth, ((1,), (0,))) + vector(7)
+    block_out = (resid + branch_scale * mlp).astype(bf16).reshape(seqs, span_rows, width)
+    block_out = by_chip(block_out)
+    left_recv, right_recv, rest_plane, d_query, d_oth, block_out = lax.optimization_barrier(
+        (left_recv, right_recv, rest_plane, d_query, d_oth, block_out)
     )
     d_recv = other_core(d_oth)
     grad_proj = jnp.concatenate(
@@ -967,7 +976,10 @@
     proj_keep, proj_send = halve(grad_proj, low_bit)
     proj_recv = send_flip(proj_send, 4)
     rest_keep, rest_sends = reduce_z(sum_low(rest_keep, *rest_plane), z)
-    proj_recv, d_recv, rest_sends = lax.optimization_barrier((proj_recv, d_recv, rest_sends))
+    proj_recv, d_recv, rest_sends, block_out = lax.optimization_barrier(
+        (proj_recv, d_recv, rest_sends, block_out)
+    )
+    block_out = z_first(block_out)
     rest_z = over_z(rest_sends)
     proj_keep, proj_send = halve(sum_low(proj_keep, proj_recv), high_bit)
     proj_recv = send_flip(proj_send, 8)
@@ -975,8 +987,10 @@
     d_pieces, d_qkv, part_gain, part_shift, part_bias = unproject(
         order_back, x_sorted, d_query, d_own, d_recv, weight_in, chips
     )
-    proj_recv, rest_z, d_pieces, d_qkv, part_gain, part_shift, part_bias, sums = lax.optimization_barrier(
-        (proj_recv, rest_z, d_pieces, d_qkv, part_gain, part_shift, part_bias, sums)
+    proj_recv, rest_z, d_pieces, d_qkv, part_gain, part_shift, part_bias, sums, block_out = (
+        lax.optimization_barrier(
+            (proj_recv, rest_z, d_pieces, d_qkv, part_gain, part_shift, part_bias, sums, block_out)
+        )
     )
 
     proj_shard = sum_low(proj_keep, proj_recv)
@@ -1012,7 +1026,11 @@
     in_pair = jnp.stack([in_shard, send_flip(in_shard, 4)])
     proj_parts = spread_twice(*proj_once)
     back = sum_low(d_pieces[:4], back_x, back_y, after(back_xy, in_shard))
-    proj_parts, in_pair, rest_once, back = lax.optimization_barrier((proj_parts, in_pair, rest_once, back))
+    block_out, unused = lax.optimization_barrier((block_out, in_shard))
+    block_out = z_second(*block_out)
+    proj_parts, in_pair, rest_once, back, block_out = lax.optimization_barrier(
+        (proj_parts, in_pair, rest_once, back, block_out)
+    )
     in_all = jnp.concatenate([in_pair, send_flip(in_pair, 8)], axis=0)
     rest_parts = spread_twice(*rest_once)
     d_first, unused = norm_back(
@@ -1020,21 +1038,15 @@
     )
     d_input = (d_resid + d_first).astype(bf16).reshape(seqs, span_rows, width)
     d_input = z_first(by_chip(d_input))
-    hidden_own, hidden_oth, unused = lax.optimization_barrier((hidden_own, hidden_oth, in_pair))
-    mlp = dot(hidden_own, w_proj, ((1,), (0,))) + dot(hidden_oth, proj_oth, ((1,), (0,))) + vector(7)
-    block_out = (resid + branch_scale * mlp).astype(bf16).reshape(seqs, span_rows, width)
-    block_out = by_chip(block_out)
-    rest_parts, in_all, block_out, proj_parts, d_input = lax.optimization_barrier(
-        (rest_parts, in_all, block_out, proj_parts, d_input)
+    rest_parts, in_all, proj_parts, d_input = lax.optimization_barrier(
+        (rest_parts, in_all, proj_parts, d_input)
     )
     in_once = spread_once(in_all[:, :56], in_all[:, 56:])
-    d_input = z_second(*d_input)
-    block_out = z_first(block_out)
     in_once, d_input, block_out, proj_parts, rest_parts = lax.optimization_barrier(
         (in_once, d_input, block_out, proj_parts, rest_parts)
     )
     in_parts = spread_twice(*in_once)
-    block_out = z_second(*block_out)
+    d_input = z_second(*d_input)
     (grad_proj,) = place(
         place_proj_kernel, "place_proj", 5, here, proj_parts, [(fc_cols // 2, width)]
     )

time: 351 us -> 333 us (0.949)
  waiting for transfers between devices: 104 us -> 98.7 us
  starting transfers between devices: 83.1 us -> 78.3 us
    all_to_all x2, waiting for transfers between devices: 0.01 us -> 4.08 us  [swap_plane(): lax.all_to_all(value, 'ctx', 0, 0, axis_index_groups=planes, tiled=True)]
    unnamed x109 -> x111, local copies, waits for them, and re-layouts: 8.64 us -> 5.12 us
  transfers between devices with their start and end apart: 71 -> 71, of which waited for: 38 -> 40; matrix products, arithmetic and copies ran while one was open for 17% -> 17% of each run, Pallas kernels for 13% -> 14%
where the time goes in v1:
time: 333 us; the launch traced here: 332 us
  waiting for transfers between devices  98.7 us (30%)
  Pallas kernels  82.4 us (25%)
  starting transfers between devices  78.3 us (24%)
  other arithmetic  28.3 us (8%)
  matrix products  22.7 us (7%)
  local copies, waits for them, and re-layouts  17.8 us (5%)
  between operations  3.89 us (1%)
    ppermute x40, waiting for transfers between devices, send_flip(): return lax.ppermute(value, 'ctx', flips[flip])  78.2 us
    ppermute x40, starting transfers between devices, send_flip(): return lax.ppermute(value, 'ctx', flips[flip])  47.8 us
    pallas_call x1, Pallas kernels, attend_back(): pl.pallas_call(attend_back_kernel, in_specs=[pl.BlockSpec(memory_space=pl...  23 us
    dot_general x8, matrix products, dot(): lax.dot_general(left, right, (dims, ((), ())), preferred_element_type=f32)  22.7 us
    ppermute x9, starting transfers between devices, send_z(): return lax.ppermute(value, 'ctx', z_shift(step))  16.8 us
    pallas_call x1, Pallas kernels, attend(): pl.pallas_call(attend_kernel, in_specs=[pl.BlockSpec(memory_space=pltpu.S...  16.1 us
    pallas_call x1, Pallas kernels, middle(): pl.pallas_call(middle_kernel, in_specs=[pl.BlockSpec(memory_space=pltpu.S...  14.6 us
    ppermute x9, waiting for transfers between devices, send_z(): return lax.ppermute(value, 'ctx', z_shift(step))  13.7 us
  transfers between devices with their start and end apart: 71, of which 40 were waited for; matrix products, arithmetic and copies ran while one was open for 17% of the time, Pallas kernels for 14%

profile of v1, /device:TPU:0, one launch (start us, length us, event | category | flops | bytes accessed | tf_op | source)
XLA Modules:
  0.0 332.2 jit_solution(9598578882372924013)
XLA Ops:
  6.8 4.0 %collective-permute-start.2 = (bf16[72,768]{1,0:T(8,128)(2,1)S(1)}, bf16[72,768]{1,0:T(8,128)(2,1)S(1)}, u32[]{:S(2)}, u32[]{:S(2)}) collective-permute-start(bf16[72,768]{1,0:T(8,128)(2,1)S(1)} %get-tuple-element.407), channel_id=1, source_target_pairs={{0,16},{2,18},{4,20},{6,22},{8,24},{10,26},{12,28},{14,30},{16,0},... | collective-permute-start | bytes 331784 | tf_op jit(solution)/shard_map/ppermute | solution.py:41
  12.9 4.4 %collective-permute-done.2 = bf16[72,768]{1,0:T(8,128)(2,1)S(1)} collective-permute-done((bf16[72,768]{1,0:T(8,128)(2,1)S(1)}, bf16[72,768]{1,0:T(8,128)(2,1)S(1)}, u32[]{:S(2)}, u32[]{:S(2)}) %collective-permute-start.2) | collective-permute-done | bytes 110624 | tf_op jit(solution)/shard_map/ppermute | solution.py:41
  25.2 4.1 %collective-permute-start.14 = (bf16[72,768]{1,0:T(8,128)(2,1)S(1)}, bf16[72,768]{1,0:T(8,128)(2,1)S(1)}, u32[]{:S(2)}, u32[]{:S(2)}) collective-permute-start(bf16[72,768]{1,0:T(8,128)(2,1)S(1)} %get-tuple-element.402), channel_id=1, source_target_pairs={{0,24},{2,26},{4,28},{6,30},{8,0},{10,2},{12,4},{14,6},{16,8},{18,... | collective-permute-start | bytes 331784 | tf_op jit(solution)/shard_map/ppermute | solution.py:41
  38.0 2.6 collective-permute-done.12
  46.6 6.6 %project.1 = (bf16[1152,768]{1,0:T(8,128)(2,1)}, bf16[1152,768]{1,0:T(8,128)(2,1)}, bf16[1152,256]{1,0:T(8,128)(2,1)}, bf16[1152,512]{1,0:T(8,128)(2,1)}, bf16[768,768]{1,0:T(8,128)(2,1)}) custom-call(s32[16]{0:T(128)} %compare_select_fusion.6.order_ref, s32[3]{0:T(128)} %pad_add_fusion.3.where_ref, bf16[4,72,768]{2,1,0:T(8,128)(2,1)} %copy-done.23, ...), custom_call_target="tpu_custom_call" | custom-call | flops 6600000000 | bytes 1048576 | tf_op jit(solution)/shard_map/project/pallas_call | solution.py:147
  57.7 16.1 %attend.1 = (f32[1152,256]{1,0:T(8,128)}, f32[9,1,384]{2,1,0:T(1,128)}, bf16[16,72,192]{2,1,0:T(8,128)(2,1)}) custom-call(s32[3,16]{1,0:T(4,128)} %pad_add_fusion.2.plan_ref, bf16[1152,256]{1,0:T(8,128)(2,1)} %get-tuple-element.196.q_ref, bf16[1152,512]{1,0:T(8,128)(2,1)} %get-tuple-element.197.own_ref, bf16[1152,512]{1,0:T(8,128)(2,1)} %copy-done.9, ...), custom_call_target="tpu_custom_call" | custom-call | flops 15000000 | bytes 4096 | tf_op jit(solution)/shard_map/attend/pallas_call | solution.py:442
  73.8 3.7 %all-to-all-start = ((bf16[4,4,72,192]{3,2,1,0:T(8,128)(2,1)}), bf16[4,4,72,192]{3,2,1,0:T(8,128)(2,1)S(1)}, u32[]{:S(2)}, u32[]{:S(2)}) async-start(bf16[4,4,72,192]{3,2,1,0:T(8,128)(2,1)} %bitcast.257), calls=%async_computation | async-start | bytes 1179648 | tf_op jit(solution)/shard_map/all_to_all | solution.py:48
  79.0 3.8 %fusion.89.grad_own_ref = f32[288,1536]{1,0:T(8,128)} fusion(bf16[288,768]{1,0:T(8,128)(2,1)S(1)} %multiply_convert_fusion.d_mlp_ref, bf16[1536,768]{1,0:T(8,128)(2,1)} %param.29), kind=kOutput, calls=%fused_computation.344 | convolution fusion | flops 679477248 | bytes 4571136 | tf_op jit(solution)/shard_map/dot_general | solution.py:80
  82.9 4.1 %all-to-all-done = bf16[4,4,72,192]{3,2,1,0:T(8,128)(2,1)S(1)} async-done(((bf16[4,4,72,192]{3,2,1,0:T(8,128)(2,1)}), bf16[4,4,72,192]{3,2,1,0:T(8,128)(2,1)S(1)}, u32[]{:S(2)}, u32[]{:S(2)}) %all-to-all-start) | async-done | bytes 442400 | tf_op jit(solution)/shard_map/all_to_all | solution.py:48
  87.8 14.6 %middle.1 = (f32[288,768]{1,0:T(8,128)}, bf16[288,384]{1,0:T(8,128)(2,1)}, bf16[288,384]{1,0:T(8,128)(2,1)}, bf16[288,384]{1,0:T(8,128)(2,1)}, bf16[288,384]{1,0...) custom-call(s32[3]{0:T(128)} %pad_add_fusion.3.where_ref, ...), custom_call_target="tpu_custom_call" | custom-call | flops 12000000 | bytes 4096 | tf_op jit(solution)/shard_map/middle/pallas_call | solution.py:263
  104.7 4.4 %all-to-all-start.1 = ((bf16[4,4,72,192]{3,2,1,0:T(8,128)(2,1)}), bf16[4,4,72,192]{3,2,1,0:T(8,128)(2,1)}, u32[]{:S(2)}, u32[]{:S(2)}) async-start(bf16[4,4,72,192]{3,2,1,0:T(8,128)(2,1)} %bitcast.256), calls=%async_computation.1 | async-start | bytes 1179648 | tf_op jit(solution)/shard_map/all_to_all | solution.py:48
  121.7 3.5 %convolution_convert_fusion = bf16[384,3072]{1,0:T(8,128)(2,1)S(1)} fusion(bf16[576,384]{1,0:T(8,128)(2,1)S(1)} %copy-done.25, bf16[288,3072]{1,0:T(8,128)(2,1)} %collective-permute-done.25, bf16[288,3072]{1,0:T(8,128)(2,1)S(1)} %copy-done.44), kind=kOutput, calls=%fused_computation | convolution fusion | flops 1367212032 | bytes 6340608 | tf_op jit(solution)/shard_map/dot_general | solution.py:80
  132.0 2.7 collective-permute-done.21
  140.0 23.0 %attend_back.1 = (bf16[1152,256]{1,0:T(8,128)(2,1)}, f32[1152,512]{1,0:T(8,128)}, bf16[1152,512]{1,0:T(8,128)(2,1)}) custom-call(s32[3,16]{1,0:T(4,128)} %pad_add_fusion.2.plan_ref, bf16[1152,256]{1,0:T(8,128)(2,1)} %get-tuple-element.196.q_ref, bf16[1152,512]{1,0:T(8,128)(2,1)} %get-tuple-element.197.own_ref, bf16[1152,512]{1,0:T(8,128)(2,1)} %copy-done.9, ...), custom_call_target="tpu_custom_call" | custom-call | flops 26400000000 | bytes 1048576 | tf_op jit(solution)/shard_map/attend_back/pallas_call | solution.py:532
  165.0 2.6 fusion.7
  174.6 4.9 %collective-permute-done.32 = bf16[192,768]{1,0:T(8,128)(2,1)S(1)} collective-permute-done((bf16[192,768]{1,0:T(8,128)(2,1)S(1)}, bf16[192,768]{1,0:T(8,128)(2,1)S(1)}, u32[]{:S(2)}, u32[]{:S(2)}) %collective-permute-start.32) | collective-permute-done | bytes 294944 | tf_op jit(solution)/shard_map/ppermute | solution.py:37
  186.3 7.4 %unproject.1 = (bf16[16,72,768]{2,1,0:T(8,128)(2,1)}, bf16[1152,640]{1,0:T(8,128)(2,1)}, f32[1,768]{1,0:T(1,128)}, f32[1,768]{1,0:T(1,128)}, f32[1,768]{1,0:T(1,128)}) custom-call(s32[16]{0:T(128)} %get-tuple-element.348.place_ref, bf16[1152,768]{1,0:T(8,128)(2,1)} %get-tuple-element.239.x_ref, bf16[1152,256]{1,0:T(8,128)(2,1)} %get-tuple-element.240.dq_ref, ...), custom_call_target="tpu_custom_call" | custom-call | flops 8800000000 | bytes 1048576 | tf_op jit(solution)/shard_map/unproject/pallas_call | solution.py:609
  196.7 3.9 %collective-permute-done.36 = bf16[24,3840]{1,0:T(8,128)(2,1)S(1)} collective-permute-done((bf16[24,3840]{1,0:T(8,128)(2,1)S(1)}, bf16[24,3840]{1,0:T(8,128)(2,1)S(1)}, u32[]{:S(2)}, u32[]{:S(2)}) %collective-permute-start.36) | collective-permute-done | bytes 184352 | tf_op jit(solution)/shard_map/ppermute | solution.py:41
  207.2 3.8 %convolution_convert_fusion.3 = bf16[384,640]{1,0:T(8,128)(2,1)} fusion(bf16[1152,640]{1,0:T(8,128)(2,1)} %get-tuple-element.263, pred[]{:T(512)S(6)} %eq.155, bf16[1152,768]{1,0:T(8,128)(2,1)} %get-tuple-element.261), kind=kOutput, calls=%fused_computation.17 | convolution fusion | flops 566919168 | bytes 3735553 | tf_op jit(solution)/shard_map/dot_general | solution.py:80
  218.7 2.9 fusion.8
  232.1 9.4 %collective-permute-done.45 = bf16[2,96,768]{2,1,0:T(8,128)(2,1)} collective-permute-done((bf16[2,96,768]{2,1,0:T(8,128)(2,1)S(1)}, bf16[2,96,768]{2,1,0:T(8,128)(2,1)}, u32[]{:S(2)}, u32[]{:S(2)}) %collective-permute-start.45) | collective-permute-done | bytes 294944 | tf_op jit(solution)/shard_map/ppermute | solution.py:37
  242.5 4.7 %collective-permute-done.46 = bf16[2,24,3840]{2,1,0:T(8,128)(2,1)} collective-permute-done((bf16[2,24,3840]{2,1,0:T(8,128)(2,1)S(1)}, bf16[2,24,3840]{2,1,0:T(8,128)(2,1)}, u32[]{:S(2)}, u32[]{:S(2)}) %collective-permute-start.46) | collective-permute-done | bytes 368672 | tf_op jit(solution)/shard_map/ppermute | solution.py:37
  253.3 5.0 %collective-permute-done.50 = bf16[4,96,384]{2,1,0:T(8,128)(2,1)S(1)} collective-permute-done((bf16[4,96,384]{2,1,0:T(8,128)(2,1)S(1)}, bf16[4,96,384]{2,1,0:T(8,128)(2,1)S(1)}, u32[]{:S(2)}, u32[]{:S(2)}) %collective-permute-start.50) | collective-permute-done | bytes 294944 | tf_op jit(solution)/shard_map/ppermute | solution.py:37
  259.4 3.7 %collective-permute-done.52 = bf16[4,24,1920]{2,1,0:T(8,128)(2,1)S(1)} collective-permute-done((bf16[4,24,1920]{2,1,0:T(8,128)(2,1)S(1)}, bf16[4,24,1920]{2,1,0:T(8,128)(2,1)S(1)}, u32[]{:S(2)}, u32[]{:S(2)}) %collective-permute-start.52) | collective-permute-done | bytes 368672 | tf_op jit(solution)/shard_map/ppermute | solution.py:37
  268.3 2.7 collective-permute-start.57
  272.5 5.3 %collective-permute-done.57 = bf16[2,72,768]{2,1,0:T(8,128)(2,1)S(1)} collective-permute-done((bf16[2,72,768]{2,1,0:T(8,128)(2,1)S(1)}, bf16[2,72,768]{2,1,0:T(8,128)(2,1)S(1)}, u32[]{:S(2)}, u32[]{:S(2)}) %collective-permute-start.57) | collective-permute-done | bytes 221216 | tf_op jit(solution)/shard_map/ppermute | solution.py:37
  285.9 4.9 %collective-permute-done.60 = bf16[2,104,640]{2,1,0:T(8,128)(2,1)S(1)} collective-permute-done((bf16[2,104,640]{2,1,0:T(8,128)(2,1)S(1)}, bf16[2,104,640]{2,1,0:T(8,128)(2,1)S(1)}, u32[]{:S(2)}, u32[]{:S(2)}) %collective-permute-start.60) | collective-permute-done | bytes 266272 | tf_op jit(solution)/shard_map/ppermute | solution.py:37
  293.1 5.6 %collective-permute-done.58.refs_1_ = bf16[8,24,1920]{2,1,0:T(8,128)(2,1)S(1)} collective-permute-done((bf16[8,24,1920]{2,1,0:T(8,128)(2,1)}, bf16[8,24,1920]{2,1,0:T(8,128)(2,1)S(1)}, u32[]{:S(2)}, u32[]{:S(2)}) %collective-permute-start.58) | collective-permute-done | bytes 737312 | tf_op jit(solution)/shard_map/ppermute | solution.py:37
  301.8 3.7 %collective-permute-done.63 = bf16[4,48,640]{2,1,0:T(8,128)(2,1)S(1)} collective-permute-done((bf16[4,48,640]{2,1,0:T(8,128)(2,1)S(1)}, bf16[4,48,640]{2,1,0:T(8,128)(2,1)S(1)}, u32[]{:S(2)}, u32[]{:S(2)}) %collective-permute-start.63) | collective-permute-done | bytes 245792 | tf_op jit(solution)/shard_map/ppermute | solution.py:37
  310.0 4.1 %place_proj.1 = f32[1536,768]{1,0:T(8,128)} custom-call(s32[3]{0:T(128)} %pad_add_fusion.3.where_ref, bf16[8,96,384]{2,1,0:T(8,128)(2,1)} %copy-done.18, bf16[8,96,384]{2,1,0:T(8,128)(2,1)} %copy-done.49, bf16[8,96,384]{2,1,0:T(8,128)(2,1)} %copy-done.17, bf16[8,96,384]{2,1,0:T(8,128)(2,1)} %copy-done.50), custom_call_target="tpu_custom_call" | custom-call | flops 5500000256 | bytes 1048576 | tf_op jit(solution)/shard_map/place_proj/pallas_call | solution.py:732
  314.1 4.7 %place_rest.1 = (f32[384,3072]{1,0:T(8,128)}, f32[384,768]{1,0:T(8,128)}) custom-call(s32[3]{0:T(128)} %pad_add_fusion.3.where_ref, bf16[8,24,1920]{2,1,0:T(8,128)(2,1)} %pad_maximum_fusion.4.refs_0_, bf16[8,24,1920]{2,1,0:T(8,128)(2,1)} %copy-done.47, bf16[8,24,1920]{2,1,0:T(8,128)(2,1)} %pad_maximum_fusion.5.refs_2_, bf16[8,24,1920]{2,1,0:T(8,128)(2,1)} %copy-done.48), custom_call_target="tpu_custom_call" | custom-call | flops 5500000256 | bytes 1048576 | tf_op jit(solution)/shard_map/place_rest/pallas_call | solution.py:732
  325.2 4.3 %place_in.1 = (f32[384,2304]{1,0:T(8,128)}, f32[4,8,640]{2,1,0:T(8,128)}) custom-call(s32[3]{0:T(128)} %pad_add_fusion.3.where_ref, bf16[8,56,640]{2,1,0:T(8,128)(2,1)} %copy-done.19, bf16[8,56,640]{2,1,0:T(8,128)(2,1)} %copy-done.51, bf16[8,48,640]{2,1,0:T(8,128)(2,1)} %copy-done.20, bf16[8,48,640]{2,1,0:T(8,128)(2,1)} %copy-done.52), custom_call_target="tpu_custom_call" | custom-call | flops 4400000000 | bytes 1048576 | tf_op jit(solution)/shard_map/place_in/pallas_call | solution.py:732
  (388 shorter events, 147.0 us)
Async XLA Ops:
  17.2 12.9 %collective-permute-start.6 = (bf16[2,72,768]{2,1,0:T(8,128)(2,1)S(1)}, bf16[2,72,768]{2,1,0:T(8,128)(2,1)S(1)}, u32[]{:S(2)}, u32[]{:S(2)}) collective-permute-start(bf16[2,72,768]{2,1,0:T(8,128)(2,1)S(1)} %pad_maximum_fusion.28), channel_id=1, source_target_pairs={{0,4},{2,6},{4,0},{6,2},{8,12},{10,14},{12,8},{14,10},{16,20},{18,... | collective-permute-start | bytes 663560 | tf_op jit(solution)/shard_map/ppermute | solution.py:37
  73.8 13.2 %all-to-all-start = ((bf16[4,4,72,192]{3,2,1,0:T(8,128)(2,1)}), bf16[4,4,72,192]{3,2,1,0:T(8,128)(2,1)S(1)}, u32[]{:S(2)}, u32[]{:S(2)}) async-start(bf16[4,4,72,192]{3,2,1,0:T(8,128)(2,1)} %bitcast.257), calls=%async_computation | async-start | bytes 1179648 | tf_op jit(solution)/shard_map/all_to_all | solution.py:48
  104.7 14.9 %all-to-all-start.1 = ((bf16[4,4,72,192]{3,2,1,0:T(8,128)(2,1)}), bf16[4,4,72,192]{3,2,1,0:T(8,128)(2,1)}, u32[]{:S(2)}, u32[]{:S(2)}) async-start(bf16[4,4,72,192]{3,2,1,0:T(8,128)(2,1)} %bitcast.256), calls=%async_computation.1 | async-start | bytes 1179648 | tf_op jit(solution)/shard_map/all_to_all | solution.py:48
  109.4 12.3 %collective-permute-start.25 = (bf16[288,3072]{1,0:T(8,128)(2,1)}, bf16[288,3072]{1,0:T(8,128)(2,1)}, u32[]{:S(2)}, u32[]{:S(2)}) collective-permute-start(bf16[288,3072]{1,0:T(8,128)(2,1)} %get-tuple-element.214), channel_id=1, source_target_pairs={{0,1},{1,0},{2,3},{3,2},{4,5},{5,4},{6,7},{7,6},{8,9},{9,8},{10,11... | collective-permute-start | bytes 5308424 | tf_op jit(solution)/shard_map/ppermute | solution.py:33
  115.6 16.5 %collective-permute-start.22 = (bf16[768,384]{1,0:T(8,128)(2,1)}, bf16[768,384]{1,0:T(8,128)(2,1)}, u32[]{:S(2)}, u32[]{:S(2)}) collective-permute-start(bf16[768,384]{1,0:T(8,128)(2,1)} %dynamic-slice_bitcast_fusion.3), channel_id=1, source_target_pairs={{0,4},{2,6},{4,0},{6,2},{8,12},{10,14},{12,8},{14,10},{16,20},{18,... | collective-permute-start | bytes 1769480 | tf_op jit(solution)/shard_map/ppermute | solution.py:37
  118.1 16.5 %collective-permute-start.21 = (bf16[768,384]{1,0:T(8,128)(2,1)}, bf16[768,384]{1,0:T(8,128)(2,1)}, u32[]{:S(2)}, u32[]{:S(2)}) collective-permute-start(bf16[768,384]{1,0:T(8,128)(2,1)} %dynamic-slice_bitcast_fusion.4), channel_id=1, source_target_pairs={{0,2},{2,0},{4,6},{6,4},{8,10},{10,8},{12,14},{14,12},{16,18},{18,... | collective-permute-start | bytes 1769480 | tf_op jit(solution)/shard_map/ppermute | solution.py:37
  126.9 44.5 %collective-permute-start.31 = (bf16[96,3840]{1,0:T(8,128)(2,1)}, bf16[96,3840]{1,0:T(8,128)(2,1)}, u32[]{:S(2)}, u32[]{:S(2)}) collective-permute-start(bf16[96,3840]{1,0:T(8,128)(2,1)} %get-tuple-element.351), channel_id=1, source_target_pairs={{0,6},{2,4},{4,2},{6,0},{8,14},{10,12},{12,10},{14,8},{16,22},{18,... | collective-permute-start | bytes 2211848 | tf_op jit(solution)/shard_map/ppermute | solution.py:37
  127.2 44.1 %collective-permute-start.30 = (bf16[96,3840]{1,0:T(8,128)(2,1)}, bf16[96,3840]{1,0:T(8,128)(2,1)}, u32[]{:S(2)}, u32[]{:S(2)}) collective-permute-start(bf16[96,3840]{1,0:T(8,128)(2,1)} %get-tuple-element.352), channel_id=1, source_target_pairs={{0,4},{2,6},{4,0},{6,2},{8,12},{10,14},{12,8},{14,10},{16,20},{18,... | collective-permute-start | bytes 2211848 | tf_op jit(solution)/shard_map/ppermute | solution.py:37
  128.9 42.5 %collective-permute-start.29 = (bf16[96,3840]{1,0:T(8,128)(2,1)}, bf16[96,3840]{1,0:T(8,128)(2,1)}, u32[]{:S(2)}, u32[]{:S(2)}) collective-permute-start(bf16[96,3840]{1,0:T(8,128)(2,1)} %get-tuple-element.353), channel_id=1, source_target_pairs={{0,2},{2,0},{4,6},{6,4},{8,10},{10,8},{12,14},{14,12},{16,18},{18,... | collective-permute-start | bytes 2211848 | tf_op jit(solution)/shard_map/ppermute | solution.py:37
  137.9 31.3 %collective-permute-start.27 = (bf16[384,384]{1,0:T(8,128)(2,1)}, bf16[384,384]{1,0:T(8,128)(2,1)S(1)}, u32[]{:S(2)}, u32[]{:S(2)}) collective-permute-start(bf16[384,384]{1,0:T(8,128)(2,1)} %dynamic-slice_bitcast_fusion.7), channel_id=1, source_target_pairs={{0,4},{2,6},{4,0},{6,2},{8,12},{10,14},{12,8},{14,10},{16,20},{18,... | collective-permute-start | bytes 884744 | tf_op jit(solution)/shard_map/ppermute | solution.py:37
  138.2 33.1 %collective-permute-start.28 = (bf16[384,384]{1,0:T(8,128)(2,1)S(1)}, bf16[384,384]{1,0:T(8,128)(2,1)S(1)}, u32[]{:S(2)}, u32[]{:S(2)}) collective-permute-start(bf16[384,384]{1,0:T(8,128)(2,1)S(1)} %dynamic-slice_bitcast_fusion.6), channel_id=1, source_target_pairs={{0,2},{2,0},{4,6},{6,4},{8,10},{10,8},{12,14},{14,12},{16,18},{18,... | collective-permute-start | bytes 884744 | tf_op jit(solution)/shard_map/ppermute | solution.py:37
  179.6 17.1 %collective-permute-start.34 = (bf16[96,768]{1,0:T(8,128)(2,1)S(1)}, bf16[96,768]{1,0:T(8,128)(2,1)S(1)}, u32[]{:S(2)}, u32[]{:S(2)}) collective-permute-start(bf16[96,768]{1,0:T(8,128)(2,1)S(1)} %dynamic-slice_bitcast_fusion.12), channel_id=1, source_target_pairs={{0,16},{2,18},{4,20},{6,22},{8,24},{10,26},{12,28},{14,30},{16,0},... | collective-permute-start | bytes 442376 | tf_op jit(solution)/shard_map/ppermute | solution.py:37
  181.8 15.0 %collective-permute-start.35 = (bf16[24,3840]{1,0:T(8,128)(2,1)S(1)}, bf16[24,3840]{1,0:T(8,128)(2,1)S(1)}, u32[]{:S(2)}, u32[]{:S(2)}) collective-permute-start(bf16[24,3840]{1,0:T(8,128)(2,1)S(1)} %get-tuple-element.236), channel_id=1, source_target_pairs={{0,8},{2,10},{4,12},{6,14},{8,16},{10,18},{12,20},{14,22},{16,24},... | collective-permute-start | bytes 552968 | tf_op jit(solution)/shard_map/ppermute | solution.py:41
  182.1 18.6 %collective-permute-start.36 = (bf16[24,3840]{1,0:T(8,128)(2,1)S(1)}, bf16[24,3840]{1,0:T(8,128)(2,1)S(1)}, u32[]{:S(2)}, u32[]{:S(2)}) collective-permute-start(bf16[24,3840]{1,0:T(8,128)(2,1)S(1)} %get-tuple-element.237), channel_id=1, source_target_pairs={{0,16},{2,18},{4,20},{6,22},{8,24},{10,26},{12,28},{14,30},{16,0},... | collective-permute-start | bytes 552968 | tf_op jit(solution)/shard_map/ppermute | solution.py:41
  183.3 17.3 %collective-permute-start.37 = (bf16[24,3840]{1,0:T(8,128)(2,1)S(1)}, bf16[24,3840]{1,0:T(8,128)(2,1)S(1)}, u32[]{:S(2)}, u32[]{:S(2)}) collective-permute-start(bf16[24,3840]{1,0:T(8,128)(2,1)S(1)} %get-tuple-element.238), channel_id=1, source_target_pairs={{0,24},{2,26},{4,28},{6,30},{8,0},{10,2},{12,4},{14,6},{16,8},{18,... | collective-permute-start | bytes 552968 | tf_op jit(solution)/shard_map/ppermute | solution.py:41
  185.7 16.8 %collective-permute-start.38 = (bf16[2,72,768]{2,1,0:T(8,128)(2,1)S(1)}, bf16[2,72,768]{2,1,0:T(8,128)(2,1)S(1)}, u32[]{:S(2)}, u32[]{:S(2)}) collective-permute-start(bf16[2,72,768]{2,1,0:T(8,128)(2,1)S(1)} %pad_maximum_fusion.30), channel_id=1, source_target_pairs={{0,8},{2,10},{4,12},{6,14},{8,0},{10,2},{12,4},{14,6},{16,24},{18,... | collective-permute-start | bytes 663560 | tf_op jit(solution)/shard_map/ppermute | solution.py:37
  202.5 13.6 %collective-permute-start.39 = (bf16[96,768]{1,0:T(8,128)(2,1)S(1)}, bf16[96,768]{1,0:T(8,128)(2,1)S(1)}, u32[]{:S(2)}, u32[]{:S(2)}) collective-permute-start(bf16[96,768]{1,0:T(8,128)(2,1)S(1)} %fusion.41), channel_id=1, source_target_pairs={{0,16},{2,18},{4,20},{6,22},{8,24},{10,26},{12,28},{14,30},{16,0},... | collective-permute-start | bytes 442376 | tf_op jit(solution)/shard_map/ppermute | solution.py:37
  203.2 15.5 %collective-permute-start.40 = (bf16[24,3840]{1,0:T(8,128)(2,1)S(1)}, bf16[24,3840]{1,0:T(8,128)(2,1)S(1)}, u32[]{:S(2)}, u32[]{:S(2)}) collective-permute-start(bf16[24,3840]{1,0:T(8,128)(2,1)S(1)} %fusion.40), channel_id=1, source_target_pairs={{0,16},{2,18},{4,20},{6,22},{8,24},{10,26},{12,28},{14,30},{16,0},... | collective-permute-start | bytes 552968 | tf_op jit(solution)/shard_map/ppermute | solution.py:37
  212.5 12.4 %collective-permute-start.42 = (bf16[4,72,768]{2,1,0:T(8,128)(2,1)}, bf16[4,72,768]{2,1,0:T(8,128)(2,1)}, u32[]{:S(2)}, u32[]{:S(2)}) collective-permute-start(bf16[4,72,768]{2,1,0:T(8,128)(2,1)} %get-tuple-element.357), channel_id=1, source_target_pairs={{0,4},{2,6},{4,0},{6,2},{8,12},{10,14},{12,8},{14,10},{16,20},{18,... | collective-permute-start | bytes 1327112 | tf_op jit(solution)/shard_map/ppermute | solution.py:37
  225.7 15.8 %collective-permute-start.45 = (bf16[2,96,768]{2,1,0:T(8,128)(2,1)S(1)}, bf16[2,96,768]{2,1,0:T(8,128)(2,1)}, u32[]{:S(2)}, u32[]{:S(2)}) collective-permute-start(bf16[2,96,768]{2,1,0:T(8,128)(2,1)S(1)} %pad_maximum_fusion.25), channel_id=1, source_target_pairs={{0,8},{2,10},{4,12},{6,14},{8,0},{10,2},{12,4},{14,6},{16,24},{18,... | collective-permute-start | bytes 884744 | tf_op jit(solution)/shard_map/ppermute | solution.py:37
  227.1 20.1 %collective-permute-start.46 = (bf16[2,24,3840]{2,1,0:T(8,128)(2,1)S(1)}, bf16[2,24,3840]{2,1,0:T(8,128)(2,1)}, u32[]{:S(2)}, u32[]{:S(2)}) collective-permute-start(bf16[2,24,3840]{2,1,0:T(8,128)(2,1)S(1)} %pad_maximum_fusion.24), channel_id=1, source_target_pairs={{0,8},{2,10},{4,12},{6,14},{8,0},{10,2},{12,4},{14,6},{16,24},{18,... | collective-permute-start | bytes 1105928 | tf_op jit(solution)/shard_map/ppermute | solution.py:37
  228.8 19.4 %collective-permute-start.47 = (bf16[208,640]{1,0:T(8,128)(2,1)}, bf16[208,640]{1,0:T(8,128)(2,1)S(1)}, u32[]{:S(2)}, u32[]{:S(2)}) collective-permute-start(bf16[208,640]{1,0:T(8,128)(2,1)} %dynamic-slice_bitcast_fusion.8), channel_id=1, source_target_pairs={{0,16},{2,18},{4,20},{6,22},{8,24},{10,26},{12,28},{14,30},{16,0},... | collective-permute-start | bytes 798728 | tf_op jit(solution)/shard_map/ppermute | solution.py:37
  230.4 17.9 %collective-permute-start.48 = (bf16[4,72,768]{2,1,0:T(8,128)(2,1)}, bf16[4,72,768]{2,1,0:T(8,128)(2,1)S(1)}, u32[]{:S(2)}, u32[]{:S(2)}) collective-permute-start(bf16[4,72,768]{2,1,0:T(8,128)(2,1)} %get-tuple-element.277), channel_id=1, source_target_pairs={{0,6},{2,4},{4,2},{6,0},{8,14},{10,12},{12,10},{14,8},{16,22},{18,... | collective-permute-start | bytes 1327112 | tf_op jit(solution)/shard_map/ppermute | solution.py:37
  250.8 12.3 %collective-permute-start.52 = (bf16[4,24,1920]{2,1,0:T(8,128)(2,1)S(1)}, bf16[4,24,1920]{2,1,0:T(8,128)(2,1)S(1)}, u32[]{:S(2)}, u32[]{:S(2)}) collective-permute-start(bf16[4,24,1920]{2,1,0:T(8,128)(2,1)S(1)} %get-tuple-element.362), channel_id=1, source_target_pairs={{0,4},{2,6},{4,0},{6,2},{8,12},{10,14},{12,8},{14,10},{16,20},{18,... | collective-permute-start | bytes 1105928 | tf_op jit(solution)/shard_map/ppermute | solution.py:37
  251.5 13.5 %collective-permute-start.53 = (bf16[104,640]{1,0:T(8,128)(2,1)S(1)}, bf16[104,640]{1,0:T(8,128)(2,1)S(1)}, u32[]{:S(2)}, u32[]{:S(2)}) collective-permute-start(bf16[104,640]{1,0:T(8,128)(2,1)S(1)} %dynamic-slice_bitcast_fusion.13), channel_id=1, source_target_pairs={{0,8},{2,10},{4,12},{6,14},{8,0},{10,2},{12,4},{14,6},{16,24},{18,... | collective-permute-start | bytes 399368 | tf_op jit(solution)/shard_map/ppermute | solution.py:37
  266.0 12.2 %collective-permute-start.54 = (bf16[8,96,384]{2,1,0:T(8,128)(2,1)S(1)}, bf16[8,96,384]{2,1,0:T(8,128)(2,1)S(1)}, u32[]{:S(2)}, u32[]{:S(2)}) collective-permute-start(bf16[8,96,384]{2,1,0:T(8,128)(2,1)S(1)} %pad_maximum_fusion.8.refs_0_), channel_id=1, source_target_pairs={{0,4},{2,6},{4,0},{6,2},{8,12},{10,14},{12,8},{14,10},{16,20},{18,... | collective-permute-start | bytes 1769480 | tf_op jit(solution)/shard_map/ppermute | solution.py:37
  282.3 16.3 %collective-permute-start.58 = (bf16[8,24,1920]{2,1,0:T(8,128)(2,1)}, bf16[8,24,1920]{2,1,0:T(8,128)(2,1)S(1)}, u32[]{:S(2)}, u32[]{:S(2)}) collective-permute-start(bf16[8,24,1920]{2,1,0:T(8,128)(2,1)} %pad_maximum_fusion.4.refs_0_), channel_id=1, source_target_pairs={{0,4},{2,6},{4,0},{6,2},{8,12},{10,14},{12,8},{14,10},{16,20},{18,... | collective-permute-start | bytes 2211848 | tf_op jit(solution)/shard_map/ppermute | solution.py:37
  283.3 15.9 %collective-permute-start.59 = (bf16[8,24,1920]{2,1,0:T(8,128)(2,1)}, bf16[8,24,1920]{2,1,0:T(8,128)(2,1)S(1)}, u32[]{:S(2)}, u32[]{:S(2)}) collective-permute-start(bf16[8,24,1920]{2,1,0:T(8,128)(2,1)} %pad_maximum_fusion.5.refs_2_), channel_id=1, source_target_pairs={{0,2},{2,0},{4,6},{6,4},{8,10},{10,8},{12,14},{14,12},{16,18},{18,... | collective-permute-start | bytes 2211848 | tf_op jit(solution)/shard_map/ppermute | solution.py:37
  307.3 13.8 %collective-permute-start.64 = (bf16[2,72,768]{2,1,0:T(8,128)(2,1)S(1)}, bf16[2,72,768]{2,1,0:T(8,128)(2,1)S(1)}, u32[]{:S(2)}, u32[]{:S(2)}) collective-permute-start(bf16[2,72,768]{2,1,0:T(8,128)(2,1)S(1)} %broadcast_select_fusion.3), channel_id=1, source_target_pairs={{0,1},{1,0},{2,3},{3,2},{4,5},{5,4},{6,7},{7,6},{8,9},{9,8},{10,11... | collective-permute-start | bytes 663560 | tf_op jit(solution)/shard_map/ppermute | solution.py:33
  307.4 13.3 %collective-permute-start.65 = (bf16[2,72,768]{2,1,0:T(8,128)(2,1)S(1)}, bf16[2,72,768]{2,1,0:T(8,128)(2,1)S(1)}, u32[]{:S(2)}, u32[]{:S(2)}) collective-permute-start(bf16[2,72,768]{2,1,0:T(8,128)(2,1)S(1)} %get-tuple-element.377), channel_id=1, source_target_pairs={{0,16},{2,18},{4,20},{6,22},{8,24},{10,26},{12,28},{14,30},{16,0},... | collective-permute-start | bytes 663560 | tf_op jit(solution)/shard_map/ppermute | solution.py:37
  308.1 15.5 %collective-permute-start.68 = (bf16[8,48,640]{2,1,0:T(8,128)(2,1)S(1)}, bf16[8,48,640]{2,1,0:T(8,128)(2,1)S(1)}, u32[]{:S(2)}, u32[]{:S(2)}) collective-permute-start(bf16[8,48,640]{2,1,0:T(8,128)(2,1)S(1)} %pad_maximum_fusion.12.refs_2_), channel_id=1, source_target_pairs={{0,2},{2,0},{4,6},{6,4},{8,10},{10,8},{12,14},{14,12},{16,18},{18,... | collective-permute-start | bytes 1474568 | tf_op jit(solution)/shard_map/ppermute | solution.py:37
  309.3 14.8 %collective-permute-start.67 = (bf16[8,56,640]{2,1,0:T(8,128)(2,1)S(1)}, bf16[8,56,640]{2,1,0:T(8,128)(2,1)S(1)}, u32[]{:S(2)}, u32[]{:S(2)}) collective-permute-start(bf16[8,56,640]{2,1,0:T(8,128)(2,1)S(1)} %pad_maximum_fusion.10.refs_0_), channel_id=1, source_target_pairs={{0,4},{2,6},{4,0},{6,2},{8,12},{10,14},{12,8},{14,10},{16,20},{18,... | collective-permute-start | bytes 1720328 | tf_op jit(solution)/shard_map/ppermute | solution.py:37
  (94 other events, 732.4 us)

commit v2 on v1

--- a/solution.py
+++ b/solution.py
@@ -218,7 +218,8 @@
 
     span = grad_own_ref.shape[1]
     lax.fori_loop(
-        0, span // wide, functools.partial(columns, lambda here: grad_own_ref[:, here], hidden_own_ref, core * span), 0
+        0, span // wide, functools.partial(columns, lambda here: grad_own_ref[:, here], hidden_own_ref, core * span), 0,
+        unroll=True,
     )
     lax.fori_loop(
         0, span // wide,
@@ -229,6 +230,7 @@
             (1 - core) * span,
         ),
         0,
+        unroll=True,
     )
     d_normed = back[...]
     gain_sum_ref[...] = jnp.sum(d_normed * unit, axis=0, keepdims=True)
@@ -273,7 +275,7 @@
             VMEM((width, wide), bf16),
         ],
         compiler_params=pltpu.CompilerParams(vmem_limit_bytes=vmem_cap),
-        cost_estimate=work(12),
+        cost_estimate=busy(12),
         name="middle",
     )(
         where, attn, x, cot, d_mlp, grad_own, proj_oth, out_own, out_oth, fc_own, fc_oth, small_own, small_oth
@@ -314,7 +316,7 @@
         + [pl.BlockSpec(memory_space=pltpu.VMEM)] * 8,
         out_specs=[pl.BlockSpec(memory_space=pltpu.VMEM)] * 2,
         out_shape=[jax.ShapeDtypeStruct((12, half), f32)] * 2,
-        cost_estimate=work(1),
+        cost_estimate=busy(1),
         name="pack",
     )(where, gain, shift, bias, *sums)
 
@@ -458,7 +460,7 @@
             VMEM((2 * rows + 2 * TILE, wide), f32),
         ],
         compiler_params=pltpu.CompilerParams(vmem_limit_bytes=vmem_cap),
-        cost_estimate=work(15),
+        cost_estimate=busy(15),
         name="attend",
     )(plan, q, own, oth, kpos, meta)
 
@@ -935,22 +937,25 @@
     )
     d_got = swap_plane(d_send.reshape(GROUPS, seqs, span_rows, feats)).reshape(chips, span_rows, feats)
     hidden_both = jnp.concatenate([hidden_own, other_core(hidden_oth)], axis=0)
-    pre_both = jnp.concatenate([d_pre, other_core(d_pre)], axis=0)
-    normed_both = jnp.concatenate([normed_own, other_core(normed_oth)], axis=0)
-    attn_both = jnp.concatenate([attn_own, other_core(attn_oth)], axis=0)
+    pre_got = other_core(d_pre)
+    normed_got_rows = other_core(normed_oth)
+    attn_got_rows = other_core(attn_oth)
     low_bit, high_bit = z % 2, z // 2
-    branch_both = jnp.concatenate([d_branch, other_core(d_branch)], axis=0)
+    branch_got = other_core(d_branch)
     hidden_both = after(hidden_both, d_send)
     grad_proj = grad_dot(hidden_both, mlp_both).astype(bf16)
     proj_left, left_send = halve(grad_proj[:, :half], x)
     proj_right, right_send = halve(grad_proj[:, half:], y)
     left_recv, right_recv = send_flip(left_send, 1), send_flip(right_send, 2)
-    normed_both, attn_both, d_got, unused = lax.optimization_barrier(
-        (normed_both, attn_both, d_got, (left_send, right_send))
+    normed_own, normed_got_rows, attn_own, attn_got_rows, d_got, unused = lax.optimization_barrier(
+        (normed_own, normed_got_rows, attn_own, attn_got_rows, d_got, (left_send, right_send))
     )
     fc_cols = d_pre.shape[1]
     grad_rest = jnp.concatenate(
-        [grad_dot(normed_both, pre_both).astype(bf16), grad_dot(attn_both, branch_both).astype(bf16)],
+        [
+            (grad_dot(normed_own, d_pre) + grad_dot(normed_got_rows, pre_got)).astype(bf16),
+            (grad_dot(attn_own, d_branch) + grad_dot(attn_got_rows, branch_got)).astype(bf16),
+        ],
         axis=1,
     )
     rest_keep, rest_sends = reduce_plane(grad_rest, group)

time: 333 us -> 336 us (level); the launches traced: 332 us -> 331 us
  other arithmetic: 28.3 us -> 24.3 us
    ppermute x20, starting transfers between devices: 5.74 us -> 10.1 us  [other_core(): return lax.ppermute(value, 'wt', pair)]
    dot_general x8 -> x10, matrix products: 22.7 us -> 24.4 us  [dot(): lax.dot_general(left, right, (dims, ((), ())), preferred_element_type=f32)]
  transfers between devices with their start and end apart: 71 -> 71, of which waited for: 40 -> 41; matrix products, arithmetic and copies ran while one was open for 17% -> 16% of each run, Pallas kernels for 14% -> 14%
where the time goes in v2:
time: 336 us; the launch traced here: 331 us
  waiting for transfers between devices  98.9 us (29%)
  starting transfers between devices  81.6 us (24%)
  Pallas kernels  79.9 us (24%)
  matrix products  24.4 us (7%)
  other arithmetic  24.3 us (7%)
  local copies, waits for them, and re-layouts  17 us (5%)
  between operations  4.39 us (1%)
    ppermute x40, waiting for transfers between devices, send_flip(): return lax.ppermute(value, 'ctx', flips[flip])  80 us
    ppermute x40, starting transfers between devices, send_flip(): return lax.ppermute(value, 'ctx', flips[flip])  46.5 us
    dot_general x10, matrix products, dot(): lax.dot_general(left, right, (dims, ((), ())), preferred_element_type=f32)  24.4 us
    pallas_call x1, Pallas kernels, attend_back(): pl.pallas_call(attend_back_kernel, in_specs=[pl.BlockSpec(memory_space=pl...  22.1 us
    ppermute x9, starting transfers between devices, send_z(): return lax.ppermute(value, 'ctx', z_shift(step))  17 us
    pallas_call x1, Pallas kernels, attend(): pl.pallas_call(attend_kernel, in_specs=[pl.BlockSpec(memory_space=pltpu.S...  15.5 us
    ppermute x9, waiting for transfers between devices, send_z(): return lax.ppermute(value, 'ctx', z_shift(step))  14.1 us
    pallas_call x1, Pallas kernels, middle(): pl.pallas_call(middle_kernel, in_specs=[pl.BlockSpec(memory_space=pltpu.S...  13.7 us
  transfers between devices with their start and end apart: 71, of which 41 were waited for; matrix products, arithmetic and copies ran while one was open for 16% of the time, Pallas kernels for 14%

profile of v2, /device:TPU:0, one launch (start us, length us, event | category | flops | bytes accessed | tf_op | source)
XLA Modules:
  0.0 330.6 jit_solution(9221235911753612641)
XLA Ops:
  6.8 4.0 %collective-permute-start.2 = (bf16[72,768]{1,0:T(8,128)(2,1)S(1)}, bf16[72,768]{1,0:T(8,128)(2,1)S(1)}, u32[]{:S(2)}, u32[]{:S(2)}) collective-permute-start(bf16[72,768]{1,0:T(8,128)(2,1)S(1)} %get-tuple-element.411), channel_id=1, source_target_pairs={{0,16},{2,18},{4,20},{6,22},{8,24},{10,26},{12,28},{14,30},{16,0},... | collective-permute-start | bytes 331784 | tf_op jit(solution)/shard_map/ppermute | solution.py:41
  12.9 4.4 %collective-permute-done.2 = bf16[72,768]{1,0:T(8,128)(2,1)S(1)} collective-permute-done((bf16[72,768]{1,0:T(8,128)(2,1)S(1)}, bf16[72,768]{1,0:T(8,128)(2,1)S(1)}, u32[]{:S(2)}, u32[]{:S(2)}) %collective-permute-start.2) | collective-permute-done | bytes 110624 | tf_op jit(solution)/shard_map/ppermute | solution.py:41
  25.2 4.1 %collective-permute-start.14 = (bf16[72,768]{1,0:T(8,128)(2,1)S(1)}, bf16[72,768]{1,0:T(8,128)(2,1)S(1)}, u32[]{:S(2)}, u32[]{:S(2)}) collective-permute-start(bf16[72,768]{1,0:T(8,128)(2,1)S(1)} %get-tuple-element.406), channel_id=1, source_target_pairs={{0,24},{2,26},{4,28},{6,30},{8,0},{10,2},{12,4},{14,6},{16,8},{18,... | collective-permute-start | bytes 331784 | tf_op jit(solution)/shard_map/ppermute | solution.py:41
  46.0 6.6 %project.1 = (bf16[1152,768]{1,0:T(8,128)(2,1)}, bf16[1152,768]{1,0:T(8,128)(2,1)}, bf16[1152,256]{1,0:T(8,128)(2,1)}, bf16[1152,512]{1,0:T(8,128)(2,1)}, bf16[768,768]{1,0:T(8,128)(2,1)}) custom-call(s32[16]{0:T(128)} %compare_select_fusion.6.order_ref, s32[3]{0:T(128)} %pad_add_fusion.3.where_ref, bf16[4,72,768]{2,1,0:T(8,128)(2,1)} %copy-done.18, ...), custom_call_target="tpu_custom_call" | custom-call | flops 6600000000 | bytes 1048576 | tf_op jit(solution)/shard_map/project/pallas_call | solution.py:147
  56.9 15.5 %attend.1 = (f32[1152,256]{1,0:T(8,128)}, f32[9,1,384]{2,1,0:T(1,128)}, bf16[16,72,192]{2,1,0:T(8,128)(2,1)}) custom-call(s32[3,16]{1,0:T(4,128)} %pad_add_fusion.2.plan_ref, bf16[1152,256]{1,0:T(8,128)(2,1)} %get-tuple-element.198.q_ref, bf16[1152,512]{1,0:T(8,128)(2,1)} %get-tuple-element.199.own_ref, bf16[1152,512]{1,0:T(8,128)(2,1)} %copy-done.38, ...), custom_call_target="tpu_custom_call" | custom-call | flops 16499999744 | bytes 1048576 | tf_op jit(solution)/shard_map/attend/pallas_call | solution.py:444
  72.4 3.7 %all-to-all-start = ((bf16[4,4,72,192]{3,2,1,0:T(8,128)(2,1)}), bf16[4,4,72,192]{3,2,1,0:T(8,128)(2,1)S(1)}, u32[]{:S(2)}, u32[]{:S(2)}) async-start(bf16[4,4,72,192]{3,2,1,0:T(8,128)(2,1)} %bitcast.263), calls=%async_computation | async-start | bytes 1179648 | tf_op jit(solution)/shard_map/all_to_all | solution.py:48
  76.0 3.5 %collective-permute-start.19 = (bf16[288,768]{1,0:T(8,128)(2,1)S(1)}, bf16[288,768]{1,0:T(8,128)(2,1)S(1)}, u32[]{:S(2)}, u32[]{:S(2)}) collective-permute-start(bf16[288,768]{1,0:T(8,128)(2,1)S(1)} %multiply_convert_fusion.d_mlp_ref), channel_id=1, source_target_pairs={{0,1},{1,0},{2,3},{3,2},{4,5},{5,4},{6,7},{7,6},{8,9},{9,8},{10,11... | collective-permute-start | bytes 1327112 | tf_op jit(solution)/shard_map/ppermute | solution.py:33
  79.6 3.8 %fusion.82.grad_own_ref = f32[288,1536]{1,0:T(8,128)} fusion(bf16[288,768]{1,0:T(8,128)(2,1)S(1)} %multiply_convert_fusion.d_mlp_ref, bf16[1536,768]{1,0:T(8,128)(2,1)} %param.29), kind=kOutput, calls=%fused_computation.335 | convolution fusion | flops 679477248 | bytes 4571136 | tf_op jit(solution)/shard_map/dot_general | solution.py:80
  84.5 13.7 %middle.1 = (f32[288,768]{1,0:T(8,128)}, bf16[288,384]{1,0:T(8,128)(2,1)}, bf16[288,384]{1,0:T(8,128)(2,1)}, bf16[288,384]{1,0:T(8,128)(2,1)}, bf16[288,384]{1,0...) custom-call(s32[3]{0:T(128)} %pad_add_fusion.3.where_ref, ...), custom_call_target="tpu_custom_call" | custom-call | flops 13200000000 | bytes 1048576 | tf_op jit(solution)/shard_map/middle/pallas_call | solution.py:265
  101.4 4.4 %all-to-all-start.1 = ((bf16[4,4,72,192]{3,2,1,0:T(8,128)(2,1)}), bf16[4,4,72,192]{3,2,1,0:T(8,128)(2,1)}, u32[]{:S(2)}, u32[]{:S(2)}) async-start(bf16[4,4,72,192]{3,2,1,0:T(8,128)(2,1)} %bitcast.261), calls=%async_computation.1 | async-start | bytes 1179648 | tf_op jit(solution)/shard_map/all_to_all | solution.py:48
  118.1 3.1 fusion.83
  134.2 22.1 %attend_back.1 = (bf16[1152,256]{1,0:T(8,128)(2,1)}, f32[1152,512]{1,0:T(8,128)}, bf16[1152,512]{1,0:T(8,128)(2,1)}) custom-call(s32[3,16]{1,0:T(4,128)} %pad_add_fusion.2.plan_ref, bf16[1152,256]{1,0:T(8,128)(2,1)} %get-tuple-element.198.q_ref, bf16[1152,512]{1,0:T(8,128)(2,1)} %get-tuple-element.199.own_ref, bf16[1152,512]{1,0:T(8,128)(2,1)} %copy-done.38, ...), custom_call_target="tpu_custom_call" | custom-call | flops 26400000000 | bytes 1048576 | tf_op jit(solution)/shard_map/attend_back/pallas_call | solution.py:534
  161.6 4.0 %collective-permute-done.27 = bf16[384,384]{1,0:T(8,128)(2,1)S(1)} collective-permute-done((bf16[384,384]{1,0:T(8,128)(2,1)S(1)}, bf16[384,384]{1,0:T(8,128)(2,1)S(1)}, u32[]{:S(2)}, u32[]{:S(2)}) %collective-permute-start.27) | collective-permute-done | bytes 294944 | tf_op jit(solution)/shard_map/ppermute | solution.py:37
  169.5 4.9 %collective-permute-done.32 = bf16[192,768]{1,0:T(8,128)(2,1)S(1)} collective-permute-done((bf16[192,768]{1,0:T(8,128)(2,1)S(1)}, bf16[192,768]{1,0:T(8,128)(2,1)S(1)}, u32[]{:S(2)}, u32[]{:S(2)}) %collective-permute-start.32) | collective-permute-done | bytes 294944 | tf_op jit(solution)/shard_map/ppermute | solution.py:37
  174.5 4.2 %collective-permute-start.34 = (bf16[96,768]{1,0:T(8,128)(2,1)S(1)}, bf16[96,768]{1,0:T(8,128)(2,1)S(1)}, u32[]{:S(2)}, u32[]{:S(2)}) collective-permute-start(bf16[96,768]{1,0:T(8,128)(2,1)S(1)} %dynamic-slice_bitcast_fusion.12), channel_id=1, source_target_pairs={{0,16},{2,18},{4,20},{6,22},{8,24},{10,26},{12,28},{14,30},{16,0},... | collective-permute-start | bytes 442376 | tf_op jit(solution)/shard_map/ppermute | solution.py:37
  178.9 3.9 %collective-permute-start.37 = (bf16[24,3840]{1,0:T(8,128)(2,1)S(1)}, bf16[24,3840]{1,0:T(8,128)(2,1)S(1)}, u32[]{:S(2)}, u32[]{:S(2)}) collective-permute-start(bf16[24,3840]{1,0:T(8,128)(2,1)S(1)} %get-tuple-element.242), channel_id=1, source_target_pairs={{0,24},{2,26},{4,28},{6,30},{8,0},{10,2},{12,4},{14,6},{16,8},{18,... | collective-permute-start | bytes 552968 | tf_op jit(solution)/shard_map/ppermute | solution.py:41
  183.5 7.4 %unproject.1 = (bf16[16,72,768]{2,1,0:T(8,128)(2,1)}, bf16[1152,640]{1,0:T(8,128)(2,1)}, f32[1,768]{1,0:T(1,128)}, f32[1,768]{1,0:T(1,128)}, f32[1,768]{1,0:T(1,128)}) custom-call(s32[16]{0:T(128)} %get-tuple-element.352.place_ref, bf16[1152,768]{1,0:T(8,128)(2,1)} %get-tuple-element.243.x_ref, bf16[1152,256]{1,0:T(8,128)(2,1)} %get-tuple-element.244.dq_ref, ...), custom_call_target="tpu_custom_call" | custom-call | flops 8800000000 | bytes 1048576 | tf_op jit(solution)/shard_map/unproject/pallas_call | solution.py:611
  192.5 3.9 %collective-permute-done.36 = bf16[24,3840]{1,0:T(8,128)(2,1)S(1)} collective-permute-done((bf16[24,3840]{1,0:T(8,128)(2,1)S(1)}, bf16[24,3840]{1,0:T(8,128)(2,1)S(1)}, u32[]{:S(2)}, u32[]{:S(2)}) %collective-permute-start.36) | collective-permute-done | bytes 184352 | tf_op jit(solution)/shard_map/ppermute | solution.py:41
  204.4 3.7 %convolution_convert_fusion.1 = bf16[384,640]{1,0:T(8,128)(2,1)} fusion(bf16[1152,640]{1,0:T(8,128)(2,1)} %get-tuple-element.267, pred[]{:T(512)S(6)} %eq.155, bf16[1152,768]{1,0:T(8,128)(2,1)} %get-tuple-element.265), kind=kOutput, calls=%fused_computation.15 | convolution fusion | flops 566919168 | bytes 3735553 | tf_op jit(solution)/shard_map/dot_general | solution.py:80
  215.8 2.9 fusion.6
  219.6 3.4 %collective-permute-done.42 = bf16[4,72,768]{2,1,0:T(8,128)(2,1)} collective-permute-done((bf16[4,72,768]{2,1,0:T(8,128)(2,1)}, bf16[4,72,768]{2,1,0:T(8,128)(2,1)}, u32[]{:S(2)}, u32[]{:S(2)}) %collective-permute-start.42) | collective-permute-done | bytes 442400 | tf_op jit(solution)/shard_map/ppermute | solution.py:37
  229.0 11.2 %collective-permute-done.45 = bf16[2,96,768]{2,1,0:T(8,128)(2,1)} collective-permute-done((bf16[2,96,768]{2,1,0:T(8,128)(2,1)S(1)}, bf16[2,96,768]{2,1,0:T(8,128)(2,1)}, u32[]{:S(2)}, u32[]{:S(2)}) %collective-permute-start.45) | collective-permute-done | bytes 294944 | tf_op jit(solution)/shard_map/ppermute | solution.py:37
  241.2 4.7 %collective-permute-done.46 = bf16[2,24,3840]{2,1,0:T(8,128)(2,1)} collective-permute-done((bf16[2,24,3840]{2,1,0:T(8,128)(2,1)S(1)}, bf16[2,24,3840]{2,1,0:T(8,128)(2,1)}, u32[]{:S(2)}, u32[]{:S(2)}) %collective-permute-start.46) | collective-permute-done | bytes 368672 | tf_op jit(solution)/shard_map/ppermute | solution.py:37
  251.5 5.5 %collective-permute-done.50 = bf16[4,96,384]{2,1,0:T(8,128)(2,1)S(1)} collective-permute-done((bf16[4,96,384]{2,1,0:T(8,128)(2,1)S(1)}, bf16[4,96,384]{2,1,0:T(8,128)(2,1)S(1)}, u32[]{:S(2)}, u32[]{:S(2)}) %collective-permute-start.50) | collective-permute-done | bytes 294944 | tf_op jit(solution)/shard_map/ppermute | solution.py:37
  257.8 4.1 %collective-permute-done.52 = bf16[4,24,1920]{2,1,0:T(8,128)(2,1)S(1)} collective-permute-done((bf16[4,24,1920]{2,1,0:T(8,128)(2,1)S(1)}, bf16[4,24,1920]{2,1,0:T(8,128)(2,1)S(1)}, u32[]{:S(2)}, u32[]{:S(2)}) %collective-permute-start.52) | collective-permute-done | bytes 368672 | tf_op jit(solution)/shard_map/ppermute | solution.py:37
  270.0 5.4 %collective-permute-done.57 = bf16[2,72,768]{2,1,0:T(8,128)(2,1)S(1)} collective-permute-done((bf16[2,72,768]{2,1,0:T(8,128)(2,1)S(1)}, bf16[2,72,768]{2,1,0:T(8,128)(2,1)S(1)}, u32[]{:S(2)}, u32[]{:S(2)}) %collective-permute-start.57) | collective-permute-done | bytes 221216 | tf_op jit(solution)/shard_map/ppermute | solution.py:37
  284.0 5.3 %collective-permute-done.60 = bf16[2,104,640]{2,1,0:T(8,128)(2,1)S(1)} collective-permute-done((bf16[2,104,640]{2,1,0:T(8,128)(2,1)S(1)}, bf16[2,104,640]{2,1,0:T(8,128)(2,1)S(1)}, u32[]{:S(2)}, u32[]{:S(2)}) %collective-permute-start.60) | collective-permute-done | bytes 266272 | tf_op jit(solution)/shard_map/ppermute | solution.py:37
  291.5 5.3 %collective-permute-done.58.refs_1_ = bf16[8,24,1920]{2,1,0:T(8,128)(2,1)S(1)} collective-permute-done((bf16[8,24,1920]{2,1,0:T(8,128)(2,1)}, bf16[8,24,1920]{2,1,0:T(8,128)(2,1)S(1)}, u32[]{:S(2)}, u32[]{:S(2)}) %collective-permute-start.58) | collective-permute-done | bytes 737312 | tf_op jit(solution)/shard_map/ppermute | solution.py:37
  299.1 4.1 %collective-permute-done.63 = bf16[4,48,640]{2,1,0:T(8,128)(2,1)S(1)} collective-permute-done((bf16[4,48,640]{2,1,0:T(8,128)(2,1)S(1)}, bf16[4,48,640]{2,1,0:T(8,128)(2,1)S(1)}, u32[]{:S(2)}, u32[]{:S(2)}) %collective-permute-start.63) | collective-permute-done | bytes 245792 | tf_op jit(solution)/shard_map/ppermute | solution.py:37
  308.3 4.1 %place_proj.1 = f32[1536,768]{1,0:T(8,128)} custom-call(s32[3]{0:T(128)} %pad_add_fusion.3.where_ref, bf16[8,96,384]{2,1,0:T(8,128)(2,1)} %copy-done.11, bf16[8,96,384]{2,1,0:T(8,128)(2,1)} %copy-done.46, bf16[8,96,384]{2,1,0:T(8,128)(2,1)} %copy-done.10, bf16[8,96,384]{2,1,0:T(8,128)(2,1)} %copy-done.47), custom_call_target="tpu_custom_call" | custom-call | flops 5500000256 | bytes 1048576 | tf_op jit(solution)/shard_map/place_proj/pallas_call | solution.py:734
  312.4 4.7 %place_rest.1 = (f32[384,3072]{1,0:T(8,128)}, f32[384,768]{1,0:T(8,128)}) custom-call(s32[3]{0:T(128)} %pad_add_fusion.3.where_ref, bf16[8,24,1920]{2,1,0:T(8,128)(2,1)} %pad_maximum_fusion.4.refs_0_, bf16[8,24,1920]{2,1,0:T(8,128)(2,1)} %copy-done.43, bf16[8,24,1920]{2,1,0:T(8,128)(2,1)} %pad_maximum_fusion.5.refs_2_, bf16[8,24,1920]{2,1,0:T(8,128)(2,1)} %copy-done.44), custom_call_target="tpu_custom_call" | custom-call | flops 5500000256 | bytes 1048576 | tf_op jit(solution)/shard_map/place_rest/pallas_call | solution.py:734
  323.1 4.3 %place_in.1 = (f32[384,2304]{1,0:T(8,128)}, f32[4,8,640]{2,1,0:T(8,128)}) custom-call(s32[3]{0:T(128)} %pad_add_fusion.3.where_ref, bf16[8,56,640]{2,1,0:T(8,128)(2,1)} %copy-done.13, bf16[8,56,640]{2,1,0:T(8,128)(2,1)} %copy-done.49, bf16[8,48,640]{2,1,0:T(8,128)(2,1)} %copy-done.14, bf16[8,48,640]{2,1,0:T(8,128)(2,1)} %copy-done.50), custom_call_target="tpu_custom_call" | custom-call | flops 4400000000 | bytes 1048576 | tf_op jit(solution)/shard_map/place_in/pallas_call | solution.py:734
  (384 shorter events, 140.2 us)
Async XLA Ops:
  17.2 12.9 %collective-permute-start.6 = (bf16[2,72,768]{2,1,0:T(8,128)(2,1)S(1)}, bf16[2,72,768]{2,1,0:T(8,128)(2,1)S(1)}, u32[]{:S(2)}, u32[]{:S(2)}) collective-permute-start(bf16[2,72,768]{2,1,0:T(8,128)(2,1)S(1)} %pad_maximum_fusion.26), channel_id=1, source_target_pairs={{0,4},{2,6},{4,0},{6,2},{8,12},{10,14},{12,8},{14,10},{16,20},{18,... | collective-permute-start | bytes 663560 | tf_op jit(solution)/shard_map/ppermute | solution.py:37
  101.4 14.5 %all-to-all-start.1 = ((bf16[4,4,72,192]{3,2,1,0:T(8,128)(2,1)}), bf16[4,4,72,192]{3,2,1,0:T(8,128)(2,1)}, u32[]{:S(2)}, u32[]{:S(2)}) async-start(bf16[4,4,72,192]{3,2,1,0:T(8,128)(2,1)} %bitcast.261), calls=%async_computation.1 | async-start | bytes 1179648 | tf_op jit(solution)/shard_map/all_to_all | solution.py:48
  110.1 18.2 %collective-permute-start.22 = (bf16[768,384]{1,0:T(8,128)(2,1)}, bf16[768,384]{1,0:T(8,128)(2,1)}, u32[]{:S(2)}, u32[]{:S(2)}) collective-permute-start(bf16[768,384]{1,0:T(8,128)(2,1)} %dynamic-slice_bitcast_fusion.3), channel_id=1, source_target_pairs={{0,4},{2,6},{4,0},{6,2},{8,12},{10,14},{12,8},{14,10},{16,20},{18,... | collective-permute-start | bytes 1769480 | tf_op jit(solution)/shard_map/ppermute | solution.py:37
  113.0 16.5 %collective-permute-start.21 = (bf16[768,384]{1,0:T(8,128)(2,1)}, bf16[768,384]{1,0:T(8,128)(2,1)}, u32[]{:S(2)}, u32[]{:S(2)}) collective-permute-start(bf16[768,384]{1,0:T(8,128)(2,1)} %dynamic-slice_bitcast_fusion.4), channel_id=1, source_target_pairs={{0,2},{2,0},{4,6},{6,4},{8,10},{10,8},{12,14},{14,12},{16,18},{18,... | collective-permute-start | bytes 1769480 | tf_op jit(solution)/shard_map/ppermute | solution.py:37
  124.4 41.8 %collective-permute-start.31 = (bf16[96,3840]{1,0:T(8,128)(2,1)}, bf16[96,3840]{1,0:T(8,128)(2,1)}, u32[]{:S(2)}, u32[]{:S(2)}) collective-permute-start(bf16[96,3840]{1,0:T(8,128)(2,1)} %get-tuple-element.355), channel_id=1, source_target_pairs={{0,6},{2,4},{4,2},{6,0},{8,14},{10,12},{12,10},{14,8},{16,22},{18,... | collective-permute-start | bytes 2211848 | tf_op jit(solution)/shard_map/ppermute | solution.py:37
  125.3 40.9 %collective-permute-start.30 = (bf16[96,3840]{1,0:T(8,128)(2,1)}, bf16[96,3840]{1,0:T(8,128)(2,1)}, u32[]{:S(2)}, u32[]{:S(2)}) collective-permute-start(bf16[96,3840]{1,0:T(8,128)(2,1)} %get-tuple-element.356), channel_id=1, source_target_pairs={{0,4},{2,6},{4,0},{6,2},{8,12},{10,14},{12,8},{14,10},{16,20},{18,... | collective-permute-start | bytes 2211848 | tf_op jit(solution)/shard_map/ppermute | solution.py:37
  126.7 39.5 %collective-permute-start.29 = (bf16[96,3840]{1,0:T(8,128)(2,1)}, bf16[96,3840]{1,0:T(8,128)(2,1)}, u32[]{:S(2)}, u32[]{:S(2)}) collective-permute-start(bf16[96,3840]{1,0:T(8,128)(2,1)} %get-tuple-element.357), channel_id=1, source_target_pairs={{0,2},{2,0},{4,6},{6,4},{8,10},{10,8},{12,14},{14,12},{16,18},{18,... | collective-permute-start | bytes 2211848 | tf_op jit(solution)/shard_map/ppermute | solution.py:37
  132.1 33.6 %collective-permute-start.27 = (bf16[384,384]{1,0:T(8,128)(2,1)S(1)}, bf16[384,384]{1,0:T(8,128)(2,1)S(1)}, u32[]{:S(2)}, u32[]{:S(2)}) collective-permute-start(bf16[384,384]{1,0:T(8,128)(2,1)S(1)} %dynamic-slice_bitcast_fusion.7), channel_id=1, source_target_pairs={{0,4},{2,6},{4,0},{6,2},{8,12},{10,14},{12,8},{14,10},{16,20},{18,... | collective-permute-start | bytes 884744 | tf_op jit(solution)/shard_map/ppermute | solution.py:37
  132.5 33.7 %collective-permute-start.28 = (bf16[384,384]{1,0:T(8,128)(2,1)S(1)}, bf16[384,384]{1,0:T(8,128)(2,1)S(1)}, u32[]{:S(2)}, u32[]{:S(2)}) collective-permute-start(bf16[384,384]{1,0:T(8,128)(2,1)S(1)} %dynamic-slice_bitcast_fusion.6), channel_id=1, source_target_pairs={{0,2},{2,0},{4,6},{6,4},{8,10},{10,8},{12,14},{14,12},{16,18},{18,... | collective-permute-start | bytes 884744 | tf_op jit(solution)/shard_map/ppermute | solution.py:37
  174.5 18.0 %collective-permute-start.34 = (bf16[96,768]{1,0:T(8,128)(2,1)S(1)}, bf16[96,768]{1,0:T(8,128)(2,1)S(1)}, u32[]{:S(2)}, u32[]{:S(2)}) collective-permute-start(bf16[96,768]{1,0:T(8,128)(2,1)S(1)} %dynamic-slice_bitcast_fusion.12), channel_id=1, source_target_pairs={{0,16},{2,18},{4,20},{6,22},{8,24},{10,26},{12,28},{14,30},{16,0},... | collective-permute-start | bytes 442376 | tf_op jit(solution)/shard_map/ppermute | solution.py:37
  178.8 13.8 %collective-permute-start.35 = (bf16[24,3840]{1,0:T(8,128)(2,1)S(1)}, bf16[24,3840]{1,0:T(8,128)(2,1)S(1)}, u32[]{:S(2)}, u32[]{:S(2)}) collective-permute-start(bf16[24,3840]{1,0:T(8,128)(2,1)S(1)} %get-tuple-element.240), channel_id=1, source_target_pairs={{0,8},{2,10},{4,12},{6,14},{8,16},{10,18},{12,20},{14,22},{16,24},... | collective-permute-start | bytes 552968 | tf_op jit(solution)/shard_map/ppermute | solution.py:41
  178.8 17.7 %collective-permute-start.36 = (bf16[24,3840]{1,0:T(8,128)(2,1)S(1)}, bf16[24,3840]{1,0:T(8,128)(2,1)S(1)}, u32[]{:S(2)}, u32[]{:S(2)}) collective-permute-start(bf16[24,3840]{1,0:T(8,128)(2,1)S(1)} %get-tuple-element.241), channel_id=1, source_target_pairs={{0,16},{2,18},{4,20},{6,22},{8,24},{10,26},{12,28},{14,30},{16,0},... | collective-permute-start | bytes 552968 | tf_op jit(solution)/shard_map/ppermute | solution.py:41
  178.9 17.9 %collective-permute-start.37 = (bf16[24,3840]{1,0:T(8,128)(2,1)S(1)}, bf16[24,3840]{1,0:T(8,128)(2,1)S(1)}, u32[]{:S(2)}, u32[]{:S(2)}) collective-permute-start(bf16[24,3840]{1,0:T(8,128)(2,1)S(1)} %get-tuple-element.242), channel_id=1, source_target_pairs={{0,24},{2,26},{4,28},{6,30},{8,0},{10,2},{12,4},{14,6},{16,8},{18,... | collective-permute-start | bytes 552968 | tf_op jit(solution)/shard_map/ppermute | solution.py:41
  182.9 16.8 %collective-permute-start.38 = (bf16[2,72,768]{2,1,0:T(8,128)(2,1)S(1)}, bf16[2,72,768]{2,1,0:T(8,128)(2,1)S(1)}, u32[]{:S(2)}, u32[]{:S(2)}) collective-permute-start(bf16[2,72,768]{2,1,0:T(8,128)(2,1)S(1)} %pad_maximum_fusion.28), channel_id=1, source_target_pairs={{0,8},{2,10},{4,12},{6,14},{8,0},{10,2},{12,4},{14,6},{16,24},{18,... | collective-permute-start | bytes 663560 | tf_op jit(solution)/shard_map/ppermute | solution.py:37
  199.7 13.1 %collective-permute-start.39 = (bf16[96,768]{1,0:T(8,128)(2,1)S(1)}, bf16[96,768]{1,0:T(8,128)(2,1)S(1)}, u32[]{:S(2)}, u32[]{:S(2)}) collective-permute-start(bf16[96,768]{1,0:T(8,128)(2,1)S(1)} %fusion.36), channel_id=1, source_target_pairs={{0,16},{2,18},{4,20},{6,22},{8,24},{10,26},{12,28},{14,30},{16,0},... | collective-permute-start | bytes 442376 | tf_op jit(solution)/shard_map/ppermute | solution.py:37
  200.4 15.4 %collective-permute-start.40 = (bf16[24,3840]{1,0:T(8,128)(2,1)S(1)}, bf16[24,3840]{1,0:T(8,128)(2,1)S(1)}, u32[]{:S(2)}, u32[]{:S(2)}) collective-permute-start(bf16[24,3840]{1,0:T(8,128)(2,1)S(1)} %fusion.35), channel_id=1, source_target_pairs={{0,16},{2,18},{4,20},{6,22},{8,24},{10,26},{12,28},{14,30},{16,0},... | collective-permute-start | bytes 552968 | tf_op jit(solution)/shard_map/ppermute | solution.py:37
  209.8 13.2 %collective-permute-start.42 = (bf16[4,72,768]{2,1,0:T(8,128)(2,1)}, bf16[4,72,768]{2,1,0:T(8,128)(2,1)}, u32[]{:S(2)}, u32[]{:S(2)}) collective-permute-start(bf16[4,72,768]{2,1,0:T(8,128)(2,1)} %get-tuple-element.361), channel_id=1, source_target_pairs={{0,4},{2,6},{4,0},{6,2},{8,12},{10,14},{12,8},{14,10},{16,20},{18,... | collective-permute-start | bytes 1327112 | tf_op jit(solution)/shard_map/ppermute | solution.py:37
  224.4 15.8 %collective-permute-start.45 = (bf16[2,96,768]{2,1,0:T(8,128)(2,1)S(1)}, bf16[2,96,768]{2,1,0:T(8,128)(2,1)}, u32[]{:S(2)}, u32[]{:S(2)}) collective-permute-start(bf16[2,96,768]{2,1,0:T(8,128)(2,1)S(1)} %pad_maximum_fusion.23), channel_id=1, source_target_pairs={{0,8},{2,10},{4,12},{6,14},{8,0},{10,2},{12,4},{14,6},{16,24},{18,... | collective-permute-start | bytes 884744 | tf_op jit(solution)/shard_map/ppermute | solution.py:37
  224.4 21.5 %collective-permute-start.46 = (bf16[2,24,3840]{2,1,0:T(8,128)(2,1)S(1)}, bf16[2,24,3840]{2,1,0:T(8,128)(2,1)}, u32[]{:S(2)}, u32[]{:S(2)}) collective-permute-start(bf16[2,24,3840]{2,1,0:T(8,128)(2,1)S(1)} %pad_maximum_fusion.22), channel_id=1, source_target_pairs={{0,8},{2,10},{4,12},{6,14},{8,0},{10,2},{12,4},{14,6},{16,24},{18,... | collective-permute-start | bytes 1105928 | tf_op jit(solution)/shard_map/ppermute | solution.py:37
  227.5 19.4 %collective-permute-start.47 = (bf16[208,640]{1,0:T(8,128)(2,1)}, bf16[208,640]{1,0:T(8,128)(2,1)S(1)}, u32[]{:S(2)}, u32[]{:S(2)}) collective-permute-start(bf16[208,640]{1,0:T(8,128)(2,1)} %dynamic-slice_bitcast_fusion.8), channel_id=1, source_target_pairs={{0,16},{2,18},{4,20},{6,22},{8,24},{10,26},{12,28},{14,30},{16,0},... | collective-permute-start | bytes 798728 | tf_op jit(solution)/shard_map/ppermute | solution.py:37
  228.1 18.9 %collective-permute-start.48 = (bf16[4,72,768]{2,1,0:T(8,128)(2,1)}, bf16[4,72,768]{2,1,0:T(8,128)(2,1)S(1)}, u32[]{:S(2)}, u32[]{:S(2)}) collective-permute-start(bf16[4,72,768]{2,1,0:T(8,128)(2,1)} %get-tuple-element.281), channel_id=1, source_target_pairs={{0,6},{2,4},{4,2},{6,0},{8,14},{10,12},{12,10},{14,8},{16,22},{18,... | collective-permute-start | bytes 1327112 | tf_op jit(solution)/shard_map/ppermute | solution.py:37
  248.2 13.6 %collective-permute-start.52 = (bf16[4,24,1920]{2,1,0:T(8,128)(2,1)S(1)}, bf16[4,24,1920]{2,1,0:T(8,128)(2,1)S(1)}, u32[]{:S(2)}, u32[]{:S(2)}) collective-permute-start(bf16[4,24,1920]{2,1,0:T(8,128)(2,1)S(1)} %get-tuple-element.366), channel_id=1, source_target_pairs={{0,4},{2,6},{4,0},{6,2},{8,12},{10,14},{12,8},{14,10},{16,20},{18,... | collective-permute-start | bytes 1105928 | tf_op jit(solution)/shard_map/ppermute | solution.py:37
  250.0 13.8 %collective-permute-start.53 = (bf16[104,640]{1,0:T(8,128)(2,1)S(1)}, bf16[104,640]{1,0:T(8,128)(2,1)S(1)}, u32[]{:S(2)}, u32[]{:S(2)}) collective-permute-start(bf16[104,640]{1,0:T(8,128)(2,1)S(1)} %dynamic-slice_bitcast_fusion.13), channel_id=1, source_target_pairs={{0,8},{2,10},{4,12},{6,14},{8,0},{10,2},{12,4},{14,6},{16,24},{18,... | collective-permute-start | bytes 399368 | tf_op jit(solution)/shard_map/ppermute | solution.py:37
  250.0 12.7 %collective-permute-start.51 = (bf16[4,24,1920]{2,1,0:T(8,128)(2,1)S(1)}, bf16[4,24,1920]{2,1,0:T(8,128)(2,1)S(1)}, u32[]{:S(2)}, u32[]{:S(2)}) collective-permute-start(bf16[4,24,1920]{2,1,0:T(8,128)(2,1)S(1)} %get-tuple-element.367), channel_id=1, source_target_pairs={{0,2},{2,0},{4,6},{6,4},{8,10},{10,8},{12,14},{14,12},{16,18},{18,... | collective-permute-start | bytes 1105928 | tf_op jit(solution)/shard_map/ppermute | solution.py:37
  263.8 12.3 %collective-permute-start.54 = (bf16[8,96,384]{2,1,0:T(8,128)(2,1)S(1)}, bf16[8,96,384]{2,1,0:T(8,128)(2,1)S(1)}, u32[]{:S(2)}, u32[]{:S(2)}) collective-permute-start(bf16[8,96,384]{2,1,0:T(8,128)(2,1)S(1)} %pad_maximum_fusion.8.refs_0_), channel_id=1, source_target_pairs={{0,4},{2,6},{4,0},{6,2},{8,12},{10,14},{12,8},{14,10},{16,20},{18,... | collective-permute-start | bytes 1769480 | tf_op jit(solution)/shard_map/ppermute | solution.py:37
  264.8 12.3 %collective-permute-start.55 = (bf16[8,96,384]{2,1,0:T(8,128)(2,1)S(1)}, bf16[8,96,384]{2,1,0:T(8,128)(2,1)S(1)}, u32[]{:S(2)}, u32[]{:S(2)}) collective-permute-start(bf16[8,96,384]{2,1,0:T(8,128)(2,1)S(1)} %pad_maximum_fusion.9.refs_2_), channel_id=1, source_target_pairs={{0,2},{2,0},{4,6},{6,4},{8,10},{10,8},{12,14},{14,12},{16,18},{18,... | collective-permute-start | bytes 1769480 | tf_op jit(solution)/shard_map/ppermute | solution.py:37
  280.2 16.6 %collective-permute-start.58 = (bf16[8,24,1920]{2,1,0:T(8,128)(2,1)}, bf16[8,24,1920]{2,1,0:T(8,128)(2,1)S(1)}, u32[]{:S(2)}, u32[]{:S(2)}) collective-permute-start(bf16[8,24,1920]{2,1,0:T(8,128)(2,1)} %pad_maximum_fusion.4.refs_0_), channel_id=1, source_target_pairs={{0,4},{2,6},{4,0},{6,2},{8,12},{10,14},{12,8},{14,10},{16,20},{18,... | collective-permute-start | bytes 2211848 | tf_op jit(solution)/shard_map/ppermute | solution.py:37
  281.0 15.8 %collective-permute-start.59 = (bf16[8,24,1920]{2,1,0:T(8,128)(2,1)}, bf16[8,24,1920]{2,1,0:T(8,128)(2,1)S(1)}, u32[]{:S(2)}, u32[]{:S(2)}) collective-permute-start(bf16[8,24,1920]{2,1,0:T(8,128)(2,1)} %pad_maximum_fusion.5.refs_2_), channel_id=1, source_target_pairs={{0,2},{2,0},{4,6},{6,4},{8,10},{10,8},{12,14},{14,12},{16,18},{18,... | collective-permute-start | bytes 2211848 | tf_op jit(solution)/shard_map/ppermute | solution.py:37
  305.3 13.8 %collective-permute-start.64 = (bf16[2,72,768]{2,1,0:T(8,128)(2,1)S(1)}, bf16[2,72,768]{2,1,0:T(8,128)(2,1)S(1)}, u32[]{:S(2)}, u32[]{:S(2)}) collective-permute-start(bf16[2,72,768]{2,1,0:T(8,128)(2,1)S(1)} %broadcast_select_fusion.3), channel_id=1, source_target_pairs={{0,1},{1,0},{2,3},{3,2},{4,5},{5,4},{6,7},{7,6},{8,9},{9,8},{10,11... | collective-permute-start | bytes 663560 | tf_op jit(solution)/shard_map/ppermute | solution.py:33
  305.4 13.3 %collective-permute-start.65 = (bf16[2,72,768]{2,1,0:T(8,128)(2,1)S(1)}, bf16[2,72,768]{2,1,0:T(8,128)(2,1)S(1)}, u32[]{:S(2)}, u32[]{:S(2)}) collective-permute-start(bf16[2,72,768]{2,1,0:T(8,128)(2,1)S(1)} %get-tuple-element.381), channel_id=1, source_target_pairs={{0,16},{2,18},{4,20},{6,22},{8,24},{10,26},{12,28},{14,30},{16,0},... | collective-permute-start | bytes 663560 | tf_op jit(solution)/shard_map/ppermute | solution.py:37
  306.3 15.3 %collective-permute-start.68 = (bf16[8,48,640]{2,1,0:T(8,128)(2,1)S(1)}, bf16[8,48,640]{2,1,0:T(8,128)(2,1)S(1)}, u32[]{:S(2)}, u32[]{:S(2)}) collective-permute-start(bf16[8,48,640]{2,1,0:T(8,128)(2,1)S(1)} %pad_maximum_fusion.12.refs_2_), channel_id=1, source_target_pairs={{0,2},{2,0},{4,6},{6,4},{8,10},{10,8},{12,14},{14,12},{16,18},{18,... | collective-permute-start | bytes 1474568 | tf_op jit(solution)/shard_map/ppermute | solution.py:37
  306.9 14.8 %collective-permute-start.67 = (bf16[8,56,640]{2,1,0:T(8,128)(2,1)S(1)}, bf16[8,56,640]{2,1,0:T(8,128)(2,1)S(1)}, u32[]{:S(2)}, u32[]{:S(2)}) collective-permute-start(bf16[8,56,640]{2,1,0:T(8,128)(2,1)S(1)} %pad_maximum_fusion.10.refs_0_), channel_id=1, source_target_pairs={{0,4},{2,6},{4,0},{6,2},{8,12},{10,14},{12,8},{14,10},{16,20},{18,... | collective-permute-start | bytes 1720328 | tf_op jit(solution)/shard_map/ppermute | solution.py:37
  (92 other events, 702.3 us)
